TPU v7x, 32 devices: a whole 2x2x4 slice. The times are simulated.
32 devices in a mesh: grp: 2 (over x), scan: 16 (over z, y, core).
Axes of the slice: x: 2, y: 2, z: 4, core: 2. Of those that a mesh axis runs over, the one named last changes fastest.
Arguments:
- patterns: bfloat16 [3072, 64, 256], P(('grp', 'scan')), parts along dimension 0, may hold values from -6 to 6
- templates: bfloat16 [32, 64, 256], P('scan'), may hold values from -6 to 6
- radius_bin: int32 [64], replicated, may hold values from 0 to 7
- radial_gain: float32 [8], replicated, may hold values from 0.25 to 4
- orientation: int32 [32, 1], replicated, may hold values from 0 to 15
Outputs:
- corr_map: float32 [3072, 32], P(('grp', 'scan')), parts along dimension 0
- orient_map: float32 [3072, 16], P(('grp', 'scan')), parts along dimension 0
There are 2 independent parts, one for each index of `grp`. A program takes and returns all parts, laid end to end along the dimension named above; an argument that names none is the same for every part. Nothing has to cross between parts.
Inputs may be any that keep to these rules, and one draw needn't show every extreme that they name: Every orientation group holds at least one template.
All inputs are finite; a program needn't handle non-finite values.
Results may differ from a plain program's by a relative error of at most 0.0024.
Values may be sent and summed in bfloat16 or wider, within the bound.
No kernel may reach another device: no remote copies, remote signals or barrier semaphores. Data moves between devices by JAX's collectives and lax.ppermute only.
A program may use at most 128 MiB of HBM per device.

v0:
```python
import math

import jax
import jax.numpy as jnp
from jax import lax
from jax.sharding import PartitionSpec as P

RADII = 64
ANGLES = 256
GAINS = 8
TMPL_PER_GROUP = 2


def with_halo(shard, sides, width):
    for axis, dim in sides:
        size, length = (lax.axis_size(axis), shard.shape[dim])
        up = [(i, (i + 1) % size) for i in range(size - 1)]
        down = [(j, i) for i, j in up]
        last = lax.slice_in_dim(shard, length - width, length, axis=dim)
        leading = lax.slice_in_dim(shard, 0, width, axis=dim)
        before = lax.ppermute(last, axis, up)
        after = lax.ppermute(leading, axis, down)
        shard = jnp.concatenate([before, shard, after], axis=dim)
    return shard


def make_tables():
    half = ANGLES // 2
    along = jnp.arange(ANGLES, dtype=jnp.int32)
    modes = jnp.arange(half + 1, dtype=jnp.int32)
    phase = 2.0 * math.pi / ANGLES * (along[:, None] * modes[None, :] % ANGLES).astype(jnp.float32)
    basis = jnp.concatenate([jnp.cos(phase), jnp.sin(phase[:, 1:half])], axis=1).astype(
        jnp.bfloat16
    )
    factor_norm = 1.0 / (ANGLES * math.sqrt(RADII * ANGLES))
    mode_weight = jnp.where((modes == 0) | (modes == half), 1.0, 2.0).astype(jnp.float32)
    phase_rows = phase.T
    inverse = jnp.concatenate(
        [mode_weight[:, None] * jnp.cos(phase_rows), -mode_weight[:, None] * jnp.sin(phase_rows)],
        axis=0,
    )
    return (basis, (inverse * factor_norm).astype(jnp.bfloat16))


def spectrum(raw, basis):
    count = raw.shape[0]
    flat = raw.reshape(-1, ANGLES)
    spec = lax.dot_general(
        basis, flat, (((0,), (1,)), ((), ())), preferred_element_type=jnp.float32
    )
    return spec.reshape(ANGLES, count, RADII)


def mode_products(left, right):
    return jnp.einsum("kpr,ktr->ktp", left, right, preferred_element_type=jnp.float32)


def correlate(pat_spec, tmpl_spec, inverse):
    half = ANGLES // 2
    count = tmpl_spec.shape[1]
    pos_count = pat_spec.shape[1]
    pat_cos = pat_spec[: half + 1]
    pat_sin = pat_spec[half + 1 :]
    tmpl_cos = tmpl_spec[: half + 1]
    tmpl_sin = tmpl_spec[half + 1 :]
    both_cos = mode_products(pat_cos, tmpl_cos)
    both_sin = mode_products(pat_sin, tmpl_sin)
    cos_sin = mode_products(pat_cos[1:half], tmpl_sin)
    sin_cos = mode_products(pat_sin, tmpl_cos[1:half])
    edge = jnp.zeros((1, count, pos_count), jnp.float32)
    real_part = both_cos + jnp.concatenate([edge, both_sin, edge], axis=0)
    imag_part = jnp.concatenate([edge, cos_sin - sin_cos, edge], axis=0)
    cross = jnp.concatenate([real_part, imag_part], axis=0).astype(jnp.bfloat16)
    cross = cross.reshape(2 * (half + 1), count * pos_count)
    shifted = lax.dot_general(
        inverse, cross, (((0,), (0,)), ((), ())), preferred_element_type=jnp.float32
    )
    return jnp.max(shifted, axis=0).reshape(count, pos_count)


def block_of(count, limit):
    size = limit
    while size > 1:
        if count % size == 0:
            return size
        size = size // 2
    return 1


def correlate_into(carry, pat_spec, count, prepare, inverse):
    block_size = block_of(count, 64)

    def step(index, total):
        begin = index * block_size
        values = correlate(pat_spec, prepare(begin, block_size), inverse)
        return lax.dynamic_update_slice(total, values, (begin, jnp.int32(0)))

    return lax.fori_loop(0, count // block_size, step, carry)


def on_device(patterns, templates, radius_bin, radial_gain, orientation):
    basis, inverse = make_tables()
    pos_count = patterns.shape[0]
    total_tmpl = templates.shape[0] * lax.axis_size("scan")
    group_count = total_tmpl // TMPL_PER_GROUP
    onehot = (radius_bin[:, None] == jnp.arange(GAINS, dtype=jnp.int32)[None, :]).astype(
        jnp.float32
    )
    radius_weight = jnp.sum(onehot * radial_gain[None, :], axis=1)
    pat_spec = (spectrum(patterns, basis) * radius_weight[None, None, :]).astype(jnp.bfloat16)
    initial = jnp.zeros((total_tmpl, pos_count), jnp.float32)

    def raw_rows(piece):
        return lambda begin, size: spectrum(
            lax.dynamic_slice_in_dim(piece, begin, size, 0), basis
        ).astype(jnp.bfloat16)

    piece = lax.all_gather(templates, "scan", axis=0, tiled=True)
    by_template = correlate_into(initial, pat_spec, piece.shape[0], raw_rows(piece), inverse)
    corr_map = by_template.T
    groups = orientation[:, 0]
    member = groups[None, :] == jnp.arange(group_count, dtype=jnp.int32)[:, None]
    group_block = block_of(group_count, 16)
    member_blocks = member.reshape(group_count // group_block, group_block, total_tmpl)

    def group_max(mask):
        return jnp.max(jnp.where(mask[:, :, None], by_template[None, :, :], -jnp.inf), axis=1)

    best = lax.map(group_max, member_blocks).reshape(group_count, pos_count).T
    padded = with_halo(best, (("scan", 0),), 1)
    orient_map = 0.25 * (padded[:-2] + 2.0 * best + padded[2:])
    return (corr_map, orient_map)


def solution(mesh):
    placed = (P(("grp", "scan"), None, None), P("scan", None, None), P(), P(), P())
    return jax.shard_map(
        on_device,
        mesh=mesh,
        in_specs=placed,
        out_specs=(P(("grp", "scan"), None), P(("grp", "scan"), None)),
        check_vma=False,
    )
```

profile of v0, /device:TPU:5, one launch (start us, length us, event | category | flops | bytes accessed | tf_op | source)
XLA Modules:
  0.0 101.3 jit_solution(18244889343172042133)
XLA Ops:
  7.2 0.0 copy-start
  7.2 0.0 all-gather.2.cloned.1.call-start
  7.2 0.7 all-gather.2.cloned.1.call-update
  7.9 1.0 select_reduce_fusion.1
  8.9 1.0 cosine_convert_fusion
  9.8 0.1 fusion.19
  10.0 0.5 fusion.31
  10.5 0.0 copy-done
  10.5 3.6 %multiply_convert_fusion = bf16[256,96,64]{0,1,2:T(8,128)(2,1)S(1)} fusion(f32[64]{0:T(128)S(1)} %select_reduce_fusion.1, bf16[96,64,256]{2,1,0:T(8,128)(2,1)S(1)} %copy-done, bf16[256,127]{1,0:T(8,128)(2,1)S(1)} %fusion.31, bf16[256,129]{1,0:T(8,128)(2,1)S(1)} %cosine_convert_fusion), kind=kOutput, calls=%fused_computation | convolution fusion | flops 808714240 | bytes 6422784 | tf_op jit(solution)/shard_map/dot_general | solution.py:48
  14.1 0.0 copy-start.2
  14.1 2.7 %fusion.41 = (bf16[127,96,64]{0,1,2:T(8,128)(2,1)}, bf16[127,96,64]{0,1,2:T(8,128)(2,1)}) fusion(bf16[256,96,64]{0,1,2:T(8,128)(2,1)S(1)} %multiply_convert_fusion), kind=kLoop, calls=%fused_computation.59 | loop fusion | bytes 6242304 | tf_op jit(solution)/shard_map/while/body/eval_jaxpr/slice | solution.py:63
  16.9 0.0 copy-done.2
  16.9 4.0 %copy.44 = bf16[127,96,64]{1,2,0:T(8,128)(2,1)} copy(bf16[127,96,64]{0,1,2:T(8,128)(2,1)} %get-tuple-element.28) | data formatting | bytes 3121152 | tf_op jit(solution)/shard_map/while/body/eval_jaxpr/slice | solution.py:68
  20.9 4.0 %copy.42 = bf16[127,96,64]{1,2,0:T(8,128)(2,1)} copy(bf16[127,96,64]{0,1,2:T(8,128)(2,1)} %get-tuple-element.20) | data formatting | bytes 3121152 | tf_op jit(solution)/shard_map/while/body/eval_jaxpr/slice | solution.py:63
  24.9 0.0 copy-start.8
  24.9 5.0 %copy.40 = bf16[129,96,64]{1,2,0:T(8,128)(2,1)} copy(bf16[129,96,64]{0,1,2:T(8,128)(2,1)} %bitcast.19) | data formatting | bytes 3170304 | tf_op jit(solution)/shard_map/while/body/eval_jaxpr/slice | solution.py:62
  29.8 0.0 copy-done.8
  29.9 1.2 %sine_multiply_fusion = (f32[129,256]{1,0:T(8,128)S(1)}, f32[129,256]{1,0:T(8,128)}) fusion(f32[129]{0:T(256)S(1)} %fusion.35, f32[129]{0:T(256)S(1)} %or_select_fusion), kind=kLoop, calls=%fused_computation.35 | loop fusion | flops 528384 | bytes 265224 | tf_op jit(solution)/shard_map/mul | solution.py:39
  31.1 17.7 %all-gather.2.cloned.1.call-done = bf16[32,64,256]{2,1,0:T(8,128)(2,1)} async-done(((bf16[2,64,256]{2,1,0:T(8,128)(2,1)}), bf16[32,64,256]{2,1,0:T(8,128)(2,1)}) %all-gather.2.cloned.1.call-update) | async-done | bytes 1048592 | tf_op jit(solution)/shard_map/all_gather | solution.py:118
  48.8 1.7 %convolution_convert_fusion = bf16[256,32,64]{0,2,1:T(8,128)(2,1)S(1)} fusion(bf16[32,64,256]{2,1,0:T(8,128)(2,1)} %all-gather.2.cloned.1.call-done, bf16[256,127]{1,0:T(8,128)(2,1)S(1)} %fusion.31, bf16[256,129]{1,0:T(8,128)(2,1)S(1)} %cosine_convert_fusion), kind=kOutput, calls=%fused_computation.14 | convolution fusion | flops 269221888 | bytes 2228224 | tf_op jit(solution)/shard_map/while/body/eval_jaxpr/dot_general | solution.py:48
  50.6 0.0 copy-start.3
  50.6 0.9 copy-done.3
  51.5 1.4 %fusion.42 = (bf16[127,32,64]{0,2,1:T(8,128)(2,1)}, bf16[127,32,64]{0,2,1:T(8,128)(2,1)}) fusion(bf16[256,32,64]{0,2,1:T(8,128)(2,1)S(1)} %convolution_convert_fusion), kind=kLoop, calls=%fused_computation.60 | loop fusion | bytes 2080768 | tf_op jit(solution)/shard_map/while/body/eval_jaxpr/slice | solution.py:69
  52.9 3.5 %copy.41 = bf16[127,32,64]{2,1,0:T(8,128)(2,1)} copy(bf16[127,32,64]{0,2,1:T(8,128)(2,1)} %get-tuple-element.30) | data formatting | bytes 1040384 | tf_op jit(solution)/shard_map/while/body/eval_jaxpr/slice | solution.py:65
  56.4 3.5 %copy.45 = bf16[127,32,64]{2,1,0:T(8,128)(2,1)} copy(bf16[127,32,64]{0,2,1:T(8,128)(2,1)} %get-tuple-element.29) | data formatting | bytes 1040384 | tf_op jit(solution)/shard_map/while/body/eval_jaxpr/slice | solution.py:69
  59.9 0.0 copy-start.1
  59.9 2.7 %fusion.45 = f32[127,32,96]{2,1,0:T(8,128)S(1)} fusion(bf16[127,32,64]{2,1,0:T(8,128)(2,1)} %copy.41, bf16[127,96,64]{1,2,0:T(8,128)(2,1)} %copy.44), kind=kOutput, calls=%fused_computation.63 | convolution fusion | flops 49938432 | bytes 3641344 | tf_op jit(solution)/shard_map/while/body/eval_jaxpr/kpr,ktr->ktp/dot_general | solution.py:55
  62.6 0.0 copy-done.1
  62.6 0.1 copy-done.4
  62.7 2.0 %fusion.44 = f32[127,32,96]{2,1,0:T(8,128)} fusion(bf16[127,32,64]{2,1,0:T(8,128)(2,1)S(1)} %copy-done.4, bf16[127,96,64]{1,2,0:T(8,128)(2,1)S(1)} %copy-done.1), kind=kOutput, calls=%fused_computation.62 | convolution fusion | flops 49938432 | bytes 3641344 | tf_op jit(solution)/shard_map/while/body/eval_jaxpr/kpr,ktr->ktp/dot_general | solution.py:55
  64.7 0.0 copy-done.5
  64.7 1.7 %subtract_convert_fusion = bf16[127,32,96]{2,1,0:T(8,128)(2,1)} fusion(f32[127,32,96]{2,1,0:T(8,128)S(1)} %fusion.45, bf16[127,32,64]{2,1,0:T(8,128)(2,1)S(1)} %copy-done.5, bf16[127,96,64]{1,2,0:T(8,128)(2,1)S(1)} %copy-done.1), kind=kOutput, calls=%fused_computation.5 | convolution fusion | flops 50718720 | bytes 4421632 | tf_op jit(solution)/shard_map/while/body/eval_jaxpr/kpr,ktr->ktp/dot_general | solution.py:55
  66.4 2.7 %copy.47 = bf16[127,32,96]{0,2,1:T(8,128)(2,1)} copy(bf16[127,32,96]{2,1,0:T(8,128)(2,1)} %subtract_convert_fusion) | data formatting | bytes 1560576 | tf_op jit(solution)/shard_map/convert.4
  69.1 2.4 %copy.48 = bf16[127,3072]{1,0:T(8,128)(2,1)} copy(bf16[127,3072]{0,1:T(8,128)(2,1)} %bitcast.21) | data formatting | bytes 1560576 | tf_op jit(solution)/shard_map/while/body/eval_jaxpr/concatenate | solution.py:73
  71.5 2.8 %copy.39 = bf16[129,32,64]{2,1,0:T(8,128)(2,1)} copy(bf16[129,32,64]{0,2,1:T(8,128)(2,1)} %bitcast.20) | data formatting | bytes 1056768 | tf_op jit(solution)/shard_map/while/body/eval_jaxpr/slice | solution.py:64
  74.3 4.3 %fusion.4 = bf16[129,32,96]{2,1,0:T(8,128)(2,1)} fusion(f32[1,32,96]{2,1,0:T(8,128)S(1)} %broadcast.63, f32[127,32,96]{2,1,0:T(8,128)} %fusion.44, bf16[129,32,64]{2,1,0:T(8,128)(2,1)} %copy.39, bf16[129,96,64]{1,2,0:T(8,128)(2,1)} %copy.40), kind=kOutput, calls=%fused_computation.4 | convolution fusion | flops 52310016 | bytes 4478976 | tf_op jit(solution)/shard_map/while/body/eval_jaxpr/kpr,ktr->ktp/dot_general | solution.py:55
  78.6 3.4 %concatenate.33 = bf16[129,3072]{1,0:T(8,128)(2,1)} reshape(bf16[129,32,96]{2,1,0:T(8,128)(2,1)} %fusion.4) | data formatting | bytes 1585152 | tf_op jit(solution)/shard_map/while/body/eval_jaxpr/concatenate | solution.py:73
  81.9 0.0 copy-done.6
  82.0 2.5 %fusion.13 = f32[3072]{0:T(1024)S(1)} fusion(bf16[1,3072]{1,0:T(2,128)(2,1)S(1)} %concatenate.34, bf16[127,3072]{1,0:T(8,128)(2,1)} %copy.48, bf16[129,3072]{1,0:T(8,128)(2,1)} %concatenate.33, f32[129,256]{1,0:T(8,128)S(1)} %get-tuple-element.37, f32[129,256]{1,0:T(8,128)S(1)} %copy-done.6), kind=kOutput, calls=%fused_computation.15 | convolution fusion | flops 413121024 | bytes 1855488 | tf_op jit(solution)/shard_map/while/body/eval_jaxpr/dot_general | solution.py:75
  84.4 0.1 reshape.51
  84.5 0.1 select_reduce_fusion
  84.6 0.1 fusion.43
  84.7 3.2 %collective-permute-start = (f32[1,16]{0,1:T(8,128)S(1)}, f32[1,16]{0,1:T(8,128)S(1)}, u32[]{:S(2)}, u32[]{:S(2)}) collective-permute-start(f32[1,16]{0,1:T(8,128)S(1)} %get-tuple-element.31), channel_id=1, source_target_pairs={{0,1},{1,2},{2,3},{3,4},{4,5},{5,6},{6,7},{7,8},{8,9},{9,10},{10,1... | collective-permute-start | bytes 200 | tf_op jit(solution)/shard_map/ppermute | solution.py:21
  87.9 1.9 %collective-permute-start.1 = (f32[1,16]{0,1:T(8,128)S(1)}, f32[1,16]{0,1:T(8,128)S(1)}, u32[]{:S(2)}, u32[]{:S(2)}) collective-permute-start(f32[1,16]{0,1:T(8,128)S(1)} %get-tuple-element.36), channel_id=1, source_target_pairs={{1,0},{2,1},{3,2},{4,3},{5,4},{6,5},{7,6},{8,7},{9,8},{10,9},{11,1... | collective-permute-start | bytes 200 | tf_op jit(solution)/shard_map/ppermute | solution.py:22
  89.9 0.0 collective-permute-done
  89.9 3.9 %collective-permute-done.1 = f32[1,16]{0,1:T(8,128)S(1)} collective-permute-done((f32[1,16]{0,1:T(8,128)S(1)}, f32[1,16]{0,1:T(8,128)S(1)}, u32[]{:S(2)}, u32[]{:S(2)}) %collective-permute-start.1) | collective-permute-done | bytes 96 | tf_op jit(solution)/shard_map/ppermute | solution.py:22
  93.8 0.7 fusion.33
  94.5 0.0 copy-done.7
  (9 shorter events, 0.0 us)
Async XLA Ops:
  7.2 3.3 %copy-start = (bf16[96,64,256]{2,1,0:T(8,128)(2,1)S(1)}, bf16[96,64,256]{2,1,0:T(8,128)(2,1)}, u32[]{:S(2)}) copy-start(bf16[96,64,256]{2,1,0:T(8,128)(2,1)} %param.5) | copy-start | bytes 9437188
  7.2 41.6 %all-gather.2.cloned.1.call-start = ((), (), s32[]{:S(2)}) async-start(), calls=%async_computation | async-start | bytes 1114112 | tf_op jit(solution)/shard_map/all_gather | solution.py:118
  14.1 2.7 %copy-start.2 = (bf16[256,96,64]{0,1,2:T(8,128)(2,1)}, bf16[256,96,64]{0,1,2:T(8,128)(2,1)S(1)}, u32[]{:S(2)}) copy-start(bf16[256,96,64]{0,1,2:T(8,128)(2,1)S(1)} %multiply_convert_fusion) | copy-start | bytes 9437188
  24.9 5.0 %copy-start.8 = (s32[32,1]{0,1:T(1,128)S(1)}, s32[32,1]{0,1:T(1,128)}, u32[]{:S(2)}) copy-start(s32[32,1]{0,1:T(1,128)} %param.9) | copy-start | bytes 388
  50.6 1.0 copy-start.3
  59.9 2.7 %copy-start.1 = (bf16[127,96,64]{1,2,0:T(8,128)(2,1)S(1)}, bf16[127,96,64]{1,2,0:T(8,128)(2,1)}, u32[]{:S(2)}) copy-start(bf16[127,96,64]{1,2,0:T(8,128)(2,1)} %copy.42) | copy-start | bytes 4681732
  59.9 2.8 %copy-start.4 = (bf16[127,32,64]{2,1,0:T(8,128)(2,1)S(1)}, bf16[127,32,64]{2,1,0:T(8,128)(2,1)}, u32[]{:S(2)}) copy-start(bf16[127,32,64]{2,1,0:T(8,128)(2,1)} %copy.41) | copy-start | bytes 1560580
  62.7 2.0 %copy-start.5 = (bf16[127,32,64]{2,1,0:T(8,128)(2,1)S(1)}, bf16[127,32,64]{2,1,0:T(8,128)(2,1)}, u32[]{:S(2)}) copy-start(bf16[127,32,64]{2,1,0:T(8,128)(2,1)} %copy.45) | copy-start | bytes 1560580
  74.3 7.6 %copy-start.6 = (f32[129,256]{1,0:T(8,128)S(1)}, f32[129,256]{1,0:T(8,128)}, u32[]{:S(2)}) copy-start(f32[129,256]{1,0:T(8,128)} %get-tuple-element.38) | copy-start | bytes 396292
  84.5 10.0 %copy-start.7 = (f32[32,96]{1,0:T(8,128)}, f32[32,96]{1,0:T(8,128)S(1)}, u32[]{:S(2)}) copy-start(f32[32,96]{1,0:T(8,128)S(1)} %reshape.51) | copy-start | bytes 36868
  84.7 5.2 %collective-permute-start = (f32[1,16]{0,1:T(8,128)S(1)}, f32[1,16]{0,1:T(8,128)S(1)}, u32[]{:S(2)}, u32[]{:S(2)}) collective-permute-start(f32[1,16]{0,1:T(8,128)S(1)} %get-tuple-element.31), channel_id=1, source_target_pairs={{0,1},{1,2},{2,3},{3,4},{4,5},{5,6},{6,7},{7,8},{8,9},{9,10},{10,1... | collective-permute-start | bytes 200 | tf_op jit(solution)/shard_map/ppermute | solution.py:21
  87.9 5.9 %collective-permute-start.1 = (f32[1,16]{0,1:T(8,128)S(1)}, f32[1,16]{0,1:T(8,128)S(1)}, u32[]{:S(2)}, u32[]{:S(2)}) collective-permute-start(f32[1,16]{0,1:T(8,128)S(1)} %get-tuple-element.36), channel_id=1, source_target_pairs={{1,0},{2,1},{3,2},{4,3},{5,4},{6,5},{7,6},{8,7},{9,8},{10,9},{11,1... | collective-permute-start | bytes 200 | tf_op jit(solution)/shard_map/ppermute | solution.py:22
Sparse Core Ops, SparseCore 0:
  10.2 38.5 all-gather.1
where the time goes:
time: 102 us; the launch traced here: 101 us
  local copies, waits for them, and re-layouts  36.6 us (36%)
  waiting for transfers between devices  22.3 us (22%)
  matrix products  18.5 us (18%)
  between operations  14.2 us (14%)
  starting transfers between devices  5.19 us (5%)
  other arithmetic  4.61 us (5%)
    all_gather x1, waiting for transfers between devices, on_device(): piece = lax.all_gather(templates, 'scan', axis=0, tiled=True)  17.7 us
    dot_general x4, matrix products, mode_products(): jnp.einsum('kpr,ktr->ktp', left, right, preferred_element_type=jnp.float32)  10.6 us
    slice x2, local copies, waits for them, and re-layouts, correlate(): pat_sin = pat_spec[half + 1:]  6.72 us
    concatenate x3, local copies, waits for them, and re-layouts, correlate(): cross = jnp.concatenate([real_part, imag_part], axis=0).astype(jnp.bfloat16)  5.75 us
    dot_general x2, matrix products, spectrum(): lax.dot_general(basis, flat, (((0,), (1,)), ((), ())), preferred_element_...  5.37 us
    slice x1, local copies, waits for them, and re-layouts, correlate(): pat_cos = pat_spec[:half + 1]  4.96 us
    slice x2, local copies, waits for them, and re-layouts, correlate(): sin_cos = mode_products(pat_sin, tmpl_cos[1:half])  4.9 us
    slice x1, local copies, waits for them, and re-layouts, correlate(): cos_sin = mode_products(pat_cos[1:half], tmpl_sin)  4 us
  transfers between devices with their start and end apart: 3, of which 2 were waited for; matrix products, arithmetic and copies ran while one was open for 23% of the time, Pallas kernels for 0%

commit v1 on v0

v1 whole, which is shorter than its diff:
```python
import math

import jax
import jax.numpy as jnp
import numpy as np
from jax import lax
from jax.experimental import pallas as pl
from jax.experimental.pallas import tpu as pltpu
from jax.sharding import PartitionSpec as P

RADII = 64
ANGLES = 256
HALF = ANGLES // 2
GAINS = 8
TMPL_PER_GROUP = 2
LANES = 128
BLOCK = 32
F32 = jnp.float32
BF16 = jnp.bfloat16
CONTRACT_LAST = (((1,), (1,)), ((), ()))


def make_tables():
    along = np.arange(ANGLES, dtype=np.int32)
    modes = np.arange(HALF + 1, dtype=np.int32)
    scale = np.float32(2.0 * math.pi / ANGLES)
    phase = scale * (along[:, None] * modes[None, :] % ANGLES).astype(np.float32)
    cos, sin = np.cos(phase), np.sin(phase)
    basis = np.concatenate([cos, sin[:, 1:HALF]], axis=1)
    norm = np.float32(1.0 / (ANGLES * math.sqrt(RADII * ANGLES)))
    weight = np.where((modes == 0) | (modes == HALF), 1.0, 2.0).astype(np.float32)
    inv_cos = weight[None, :] * cos * norm
    inv_sin = -weight[None, :] * sin * norm
    inverse = np.concatenate([inv_cos, inv_sin[:, 1:HALF]], axis=1)
    return basis.T.astype(jnp.bfloat16), inverse.astype(jnp.bfloat16)


def template_kernel(tmpl_ref, table_ref, out_ref):
    for t in range(tmpl_ref.shape[0]):
        spec = lax.dot_general(table_ref[...], tmpl_ref[t], CONTRACT_LAST, preferred_element_type=F32)
        out_ref[t] = jnp.concatenate([spec[:HALF], spec[HALF:]], axis=1).astype(BF16)


def pattern_kernel(bin_ref, gain_ref, pat_ref, before_ref, after_ref, table_ref, out_ref, raw_ref, spec_ref):
    count = pat_ref.shape[0]
    zero = jnp.zeros((LANES - count, LANES), F32)

    def put(pos, rows):
        wide = rows.astype(F32)
        raw_ref[0, pl.ds(pos, RADII, stride=LANES), :] = wide[:, :LANES]
        raw_ref[1, pl.ds(pos, RADII, stride=LANES), :] = wide[:, LANES:]

    def fill(r, carry):
        raw_ref[0, pl.ds(r * LANES + count, LANES - count), :] = zero
        raw_ref[1, pl.ds(r * LANES + count, LANES - count), :] = zero
        return carry

    lax.fori_loop(0, RADII, fill, 0, unroll=8)

    def place(p, carry):
        put(p, pat_ref[p])
        return carry

    lax.fori_loop(0, count, place, 0, unroll=8)
    put(count, after_ref[0])
    put(LANES - 1, before_ref[0])

    def step(r, carry):
        begin = pl.multiple_of(r * LANES, LANES)
        rows = jnp.concatenate(
            [raw_ref[0, pl.ds(begin, LANES), :], raw_ref[1, pl.ds(begin, LANES), :]], axis=1
        ).astype(BF16)
        spec = lax.dot_general(table_ref[...], rows, CONTRACT_LAST, preferred_element_type=F32)
        spec = spec * gain_ref[bin_ref[r]]
        spec_ref[pl.ds(r, HALF, stride=2 * RADII), :] = spec[:HALF]
        spec_ref[pl.ds(RADII + r, HALF, stride=2 * RADII), :] = spec[HALF:]
        return carry

    lax.fori_loop(0, RADII, step, 0, unroll=4)

    def narrow(k, carry):
        out_ref[k] = spec_ref[pl.ds(pl.multiple_of(k * LANES, LANES), LANES), :].astype(BF16)
        return carry

    lax.fori_loop(0, HALF, narrow, 0, unroll=8)


def match_kernel(order_ref, tmpl_ref, pat_ref, inv_ref, orient_ref, corr_ref, smooth_ref, side_ref, cross_ref, best_ref):
    total = tmpl_ref.shape[0]
    count = corr_ref.shape[0]
    groups = smooth_ref.shape[1]
    low = lax.broadcasted_iota(jnp.int32, (BLOCK, LANES), 1) < RADII
    sign = jnp.where(lax.broadcasted_iota(jnp.int32, (HALF, LANES), 1) < RADII, 1.0, -1.0).astype(F32)
    for begin in range(0, total, BLOCK):

        def spread(t, carry):
            both = tmpl_ref[order_ref[begin + t]].astype(F32)
            turned = pltpu.roll(both, RADII, 1) * sign
            side_ref[pl.ds(t, HALF, stride=2 * BLOCK), :] = both
            side_ref[pl.ds(BLOCK + t, HALF, stride=2 * BLOCK), :] = turned
            return carry

        lax.fori_loop(0, BLOCK, spread, 0, unroll=4)

        def product(k, left):
            value = jnp.dot(left.astype(BF16), pat_ref[k], preferred_element_type=F32)
            at = k * 2 * BLOCK
            if not isinstance(k, int):
                at = pl.multiple_of(at, 2 * BLOCK)
            cross_ref[pl.ds(at, 2 * BLOCK), :] = value

        edge = side_ref[pl.ds(0, BLOCK), :]
        product(0, jnp.concatenate([jnp.where(low, edge, 0.0), jnp.where(low, 0.0, edge)], axis=0))

        def modes(k, carry):
            product(k, side_ref[pl.ds(pl.multiple_of(k * 2 * BLOCK, 2 * BLOCK), 2 * BLOCK), :])
            return carry

        lax.fori_loop(1, HALF, modes, 0, unroll=8)

        def shifts(t, carry):
            real = cross_ref[pl.ds(t, HALF, stride=2 * BLOCK), :]
            imag = cross_ref[pl.ds(BLOCK + t, HALF, stride=2 * BLOCK), :]
            cross = jnp.concatenate([real, imag], axis=0).astype(BF16)
            shifted = jnp.dot(inv_ref[...], cross, preferred_element_type=F32)
            best_ref[pl.ds(begin + t, 1), :] = jnp.max(shifted, axis=0, keepdims=True)
            return carry

        lax.fori_loop(0, BLOCK, shifts, 0, unroll=4)
    corr = best_ref[...]
    corr_ref[...] = corr.T[:count]
    rows = []
    for g in range(groups):
        rows.append(jnp.max(jnp.where(orient_ref[...] == g, corr, -jnp.inf), axis=0, keepdims=True))
    best = jnp.concatenate(rows, axis=0)
    smooth = 0.25 * (pltpu.roll(best, 1, 1) + 2.0 * best + pltpu.roll(best, LANES - 1, 1))
    smooth_ref[...] = smooth.T[:count]


VMEM = pl.BlockSpec(memory_space=pltpu.VMEM)
SMEM = pl.BlockSpec(memory_space=pltpu.SMEM)


def template_spectra(templates, table):
    return pl.pallas_call(
        template_kernel,
        out_shape=jax.ShapeDtypeStruct((templates.shape[0], HALF, LANES), BF16),
        in_specs=[VMEM] * 2,
        out_specs=VMEM,
        name="template_spectra",
    )(templates, table)


def pattern_spectra(bins, gains, patterns, before, after, table):
    return pl.pallas_call(
        pattern_kernel,
        out_shape=jax.ShapeDtypeStruct((HALF, LANES, LANES), BF16),
        in_specs=[SMEM] * 2 + [VMEM] * 4,
        out_specs=VMEM,
        scratch_shapes=[pltpu.VMEM((2, RADII * LANES, LANES), F32), pltpu.VMEM((HALF * LANES, LANES), F32)],
        name="pattern_spectra",
    )(bins, gains, patterns, before, after, table)


def match(order, spectra, pat_spec, inverse, orientation, count, groups):
    total = spectra.shape[0]
    return pl.pallas_call(
        match_kernel,
        out_shape=(jax.ShapeDtypeStruct((count, total), F32), jax.ShapeDtypeStruct((count, groups), F32)),
        in_specs=[SMEM] + [VMEM] * 4,
        out_specs=(VMEM, VMEM),
        scratch_shapes=[
            pltpu.VMEM((HALF * 2 * BLOCK, LANES), F32),
            pltpu.VMEM((HALF * 2 * BLOCK, LANES), F32),
            pltpu.VMEM((total, LANES), F32),
        ],
        name="match",
    )(order, spectra, pat_spec, inverse, orientation)


def on_device(patterns, templates, radius_bin, radial_gain, orientation):
    table, inverse = make_tables()
    table, inverse = jnp.asarray(table), jnp.asarray(inverse)
    count = patterns.shape[0]
    size = lax.axis_size("scan")
    mine = templates.shape[0]
    total = mine * size
    groups = total // TMPL_PER_GROUP
    own = template_spectra(templates, table)
    up = [(i, i + 1) for i in range(size - 1)]
    down = [(j, i) for i, j in up]
    before = lax.ppermute(patterns[count - 1 :], "scan", up)
    after = lax.ppermute(patterns[:1], "scan", down)
    gathered = own
    held = [0]
    bit = size // 2
    while bit:
        other = lax.ppermute(gathered, "scan", [(i, i ^ bit) for i in range(size)])
        gathered = jnp.concatenate([gathered, other], axis=0)
        held = held + [h ^ bit for h in held]
        bit //= 2
    slot = np.zeros(size, np.int32)
    slot[np.array(held)] = np.arange(size, dtype=np.int32)
    which = jnp.arange(size, dtype=jnp.int32) ^ lax.axis_index("scan").astype(jnp.int32)
    order = (jnp.asarray(slot)[which][:, None] * mine + jnp.arange(mine, dtype=jnp.int32)).reshape(total)
    pat_spec = pattern_spectra(radius_bin, radial_gain, patterns, before, after, table)
    return match(order, gathered, pat_spec, inverse, orientation, count, groups)


def solution(mesh):
    placed = (P(("grp", "scan"), None, None), P("scan", None, None), P(), P(), P())
    return jax.shard_map(
        on_device,
        mesh=mesh,
        in_specs=placed,
        out_specs=(P(("grp", "scan"), None), P(("grp", "scan"), None)),
        check_vma=False,
    )
```

time: 102 us -> 72.7 us (0.71)
  the two profiles are of different devices: /device:TPU:5 before, /device:TPU:0 now
where the time goes in v1:
time: 72.7 us; the launch traced here: 72.1 us
  Pallas kernels  37.7 us (52%)
  starting transfers between devices  10.9 us (15%)
  local copies, waits for them, and re-layouts  10.1 us (14%)
  waiting for transfers between devices  10 us (14%)
  other arithmetic  2.7 us (4%)
  between operations  0.73 us (1%)
    pallas_call x1, Pallas kernels, pattern_spectra(): pl.pallas_call(pattern_kernel, out_shape=jax.ShapeDtypeStruct((HALF, LANE...  20.1 us
    pallas_call x1, Pallas kernels, match(): pl.pallas_call(match_kernel, out_shape=(jax.ShapeDtypeStruct((count, tota...  15.7 us
    ppermute x4, waiting for transfers between devices, on_device(): other = lax.ppermute(gathered, 'scan', [(i, i ^ bit) for i in range(size)])  10 us
    ppermute x4, starting transfers between devices, on_device(): other = lax.ppermute(gathered, 'scan', [(i, i ^ bit) for i in range(size)])  6.54 us
    unnamed x11, local copies, waits for them, and re-layouts  4.42 us
    ppermute x1, starting transfers between devices, on_device(): before = lax.ppermute(patterns[count - 1:], 'scan', up)  3.03 us
    pallas_call x2, local copies, waits for them, and re-layouts, match(): pl.pallas_call(match_kernel, out_shape=(jax.ShapeDtypeStruct((count, tota...  2.94 us
    concatenate x3, other arithmetic, on_device(): gathered = jnp.concatenate([gathered, other], axis=0)  2.61 us
  transfers between devices with their start and end apart: 6, of which 2 were waited for; matrix products, arithmetic and copies ran while one was open for 9% of the time, Pallas kernels for 28%

profile of v1, /device:TPU:0, one launch (start us, length us, event | category | flops | bytes accessed | tf_op | source)
XLA Modules:
  0.0 72.1 jit_solution(12036607354215384179)
XLA Ops:
  0.6 1.9 %template_spectra.1 = bf16[2,128,128]{2,1,0:T(8,128)(2,1)} custom-call(bf16[2,64,256]{2,1,0:T(8,128)(2,1)} %tmpl_ref.1, bf16[256,256]{1,0:T(8,128)(2,1)} %constant.16.clone.table_ref), custom_call_target="tpu_custom_call" | custom-call | tf_op jit(solution)/shard_map/template_spectra/pallas_call | solution.py:145
  2.5 4.0 %collective-permute-start = (bf16[2,128,128]{2,1,0:T(8,128)(2,1)}, bf16[2,128,128]{2,1,0:T(8,128)(2,1)S(1)}, u32[]{:S(2)}, u32[]{:S(2)}) collective-permute-start(bf16[2,128,128]{2,1,0:T(8,128)(2,1)} %template_spectra.1), channel_id=1, source_target_pairs={{0,8},{1,9},{2,10},{3,11},{4,12},{5,13},{6,14},{7,15},{8,0},{9,1},... | collective-permute-start | bytes 196616 | tf_op jit(solution)/shard_map/ppermute | solution.py:198
  6.5 3.9 %collective-permute-done = bf16[2,128,128]{2,1,0:T(8,128)(2,1)S(1)} collective-permute-done((bf16[2,128,128]{2,1,0:T(8,128)(2,1)}, bf16[2,128,128]{2,1,0:T(8,128)(2,1)S(1)}, u32[]{:S(2)}, u32[]{:S(2)}) %collective-permute-start) | collective-permute-done | bytes 65568 | tf_op jit(solution)/shard_map/ppermute | solution.py:198
  10.4 0.9 %pad_maximum_fusion.2 = bf16[4,128,128]{2,1,0:T(8,128)(2,1)S(1)} fusion(bf16[2,128,128]{2,1,0:T(8,128)(2,1)S(1)} %collective-permute-done, bf16[2,128,128]{2,1,0:T(8,128)(2,1)} %template_spectra.1), kind=kLoop, calls=%fused_computation.3 | loop fusion | flops 65536 | bytes 262144 | tf_op jit(solution)/shard_map/concatenate | solution.py:199
  11.2 0.7 %collective-permute-start.1 = (bf16[4,128,128]{2,1,0:T(8,128)(2,1)S(1)}, bf16[4,128,128]{2,1,0:T(8,128)(2,1)S(1)}, u32[]{:S(2)}, u32[]{:S(2)}) collective-permute-start(bf16[4,128,128]{2,1,0:T(8,128)(2,1)S(1)} %pad_maximum_fusion.2), channel_id=1, source_target_pairs={{0,4},{1,5},{2,6},{3,7},{4,0},{5,1},{6,2},{7,3},{8,12},{9,13},{10,... | collective-permute-start | bytes 393224 | tf_op jit(solution)/shard_map/ppermute | solution.py:198
  12.0 0.8 %fusion.1 = (bf16[1,64,256]{2,1,0:T(8,128)(2,1)S(1)}, bf16[1,64,256]{2,1,0:T(8,128)(2,1)S(1)}) fusion(bf16[96,64,256]{2,1,0:T(8,128)(2,1)} %pat_ref.1), kind=kLoop, calls=%fused_computation.14 | loop fusion | bytes 131072 | tf_op jit(solution)/shard_map/slice | solution.py:193
  12.8 1.3 %collective-permute-start.5 = (bf16[1,64,256]{2,1,0:T(8,128)(2,1)S(1)}, bf16[1,64,256]{2,1,0:T(8,128)(2,1)S(1)}, u32[]{:S(2)}, u32[]{:S(2)}) collective-permute-start(bf16[1,64,256]{2,1,0:T(8,128)(2,1)S(1)} %get-tuple-element.6), channel_id=1, source_target_pairs={{1,0},{2,1},{3,2},{4,3},{5,4},{6,5},{7,6},{8,7},{9,8},{10,9},{11,1... | collective-permute-start | bytes 98312 | tf_op jit(solution)/shard_map/ppermute | solution.py:193
  14.0 3.0 %collective-permute-start.4 = (bf16[1,64,256]{2,1,0:T(8,128)(2,1)S(1)}, bf16[1,64,256]{2,1,0:T(8,128)(2,1)S(1)}, u32[]{:S(2)}, u32[]{:S(2)}) collective-permute-start(bf16[1,64,256]{2,1,0:T(8,128)(2,1)S(1)} %get-tuple-element.7), channel_id=1, source_target_pairs={{0,1},{1,2},{2,3},{3,4},{4,5},{5,6},{6,7},{7,8},{8,9},{9,10},{10,1... | collective-permute-start | bytes 98312 | tf_op jit(solution)/shard_map/ppermute | solution.py:192
  17.1 0.0 collective-permute-done.1
  17.1 0.9 %pad_maximum_fusion.1 = bf16[8,128,128]{2,1,0:T(8,128)(2,1)S(1)} fusion(bf16[4,128,128]{2,1,0:T(8,128)(2,1)S(1)} %collective-permute-done.1, bf16[2,128,128]{2,1,0:T(8,128)(2,1)S(1)} %collective-permute-done, bf16[2,128,128]{2,1,0:T(8,128)(2,1)} %template_spectra.1), kind=kLoop, calls=%fused_computation.2 | loop fusion | flops 262144 | bytes 524288 | tf_op jit(solution)/shard_map/concatenate | solution.py:199
  18.0 1.6 %collective-permute-start.2 = (bf16[8,128,128]{2,1,0:T(8,128)(2,1)S(1)}, bf16[8,128,128]{2,1,0:T(8,128)(2,1)S(1)}, u32[]{:S(2)}, u32[]{:S(2)}) collective-permute-start(bf16[8,128,128]{2,1,0:T(8,128)(2,1)S(1)} %pad_maximum_fusion.1), channel_id=1, source_target_pairs={{0,2},{1,3},{2,0},{3,1},{4,6},{5,7},{6,4},{7,5},{8,10},{9,11},{10,... | collective-permute-start | bytes 786440 | tf_op jit(solution)/shard_map/ppermute | solution.py:198
  19.6 1.3 %gather_fusion = s32[16]{0:T(128)S(1)} fusion(s32[16]{0:T(128)} %constant.18.clone, s32[1024]{0:T(1024)S(1)} %pad_clamp_fusion), kind=kCustom, calls=%fused_computation | custom fusion | bytes 192 | tf_op jit(solution)/shard_map/gather | solution.py:205
  20.9 6.2 %collective-permute-done.2 = bf16[8,128,128]{2,1,0:T(8,128)(2,1)S(1)} collective-permute-done((bf16[8,128,128]{2,1,0:T(8,128)(2,1)S(1)}, bf16[8,128,128]{2,1,0:T(8,128)(2,1)S(1)}, u32[]{:S(2)}, u32[]{:S(2)}) %collective-permute-start.2) | collective-permute-done | bytes 262176 | tf_op jit(solution)/shard_map/ppermute | solution.py:198
  27.0 0.9 %pad_maximum_fusion = bf16[16,128,128]{2,1,0:T(8,128)(2,1)S(1)} fusion(bf16[8,128,128]{2,1,0:T(8,128)(2,1)S(1)} %collective-permute-done.2, bf16[4,128,128]{2,1,0:T(8,128)(2,1)S(1)} %collective-permute-done.1, bf16[2,128,128]{2,1,0:T(8,128)(2,1)S(1)} %collective-permute-done, bf16[2,128,128]{2,1,0:T(8,128)(2,1)} %template_spectra.1), kind=kLoop, calls=%fused_computation.1 | loop fusion | flops 786432 | bytes 1048576 | tf_op jit(solution)/shard_map/concatenate | solution.py:199
  27.9 0.2 collective-permute-start.3
  28.1 0.1 iota_add_fusion
  28.2 0.8 %constant_dynamic-update-slice_fusion.4 = bf16[32,128,128]{2,1,0:T(8,128)(2,1)S(1)} fusion(bf16[2,128,128]{2,1,0:T(8,128)(2,1)} %template_spectra.1), kind=kLoop, calls=%fused_computation.8 | loop fusion | bytes 131072
  29.0 0.6 add.31.order_ref
  29.6 1.3 %copy.13.orient_ref = s32[32,1]{1,0:T(8,128)} copy(s32[32,1]{0,1:T(1,128)} %param.12) | data formatting | bytes 256 | tf_op args[4]
  31.0 0.0 collective-permute-done.5.after_ref
  31.0 0.0 copy-start.1
  31.0 0.0 collective-permute-done.4.before_ref
  31.0 0.6 copy-done.1
  31.6 0.0 copy-start.2
  31.6 0.6 copy-done.2
  32.2 20.1 %pattern_spectra.1.pat_ref = bf16[128,128,128]{2,1,0:T(8,128)(2,1)} custom-call(s32[64]{0:T(128)} %bin_ref.1, f32[8]{0:T(128)} %gain_ref.1, bf16[96,64,256]{2,1,0:T(8,128)(2,1)} %pat_ref.1, bf16[1,64,256]{2,1,0:T(8,128)(2,1)} %copy-done.2, bf16[1,64,256]{2,1,0:T(8,128)(2,1)} %copy-done.1, bf16[256,256]{1,0:T(8,128)(2,1)} %constant.16.clone.table_ref), custom_call_target="tpu_custom_call" | custom-call | tf_op jit(solution)/shard_map/pattern_spectra/pallas_call | solution.py:155
  52.4 0.0 collective-permute-done.3
  52.4 0.1 constant_dynamic-update-slice_fusion.tmpl_ref
  52.5 0.0 copy-start
  52.5 0.9 %copy-done = bf16[32,128,128]{2,1,0:T(8,128)(2,1)} copy-done((bf16[32,128,128]{2,1,0:T(8,128)(2,1)}, bf16[32,128,128]{2,1,0:T(8,128)(2,1)S(1)}, u32[]{:S(2)}) %copy-start) | copy-done | bytes 1048600
  53.4 15.7 %match.1 = (f32[96,32]{1,0:T(8,128)}, f32[96,16]{1,0:T(8,128)}) custom-call(s32[32]{0:T(128)} %add.31.order_ref, bf16[32,128,128]{2,1,0:T(8,128)(2,1)} %copy-done, bf16[128,128,128]{2,1,0:T(8,128)(2,1)} %pattern_spectra.1.pat_ref, bf16[256,256]{1,0:T(8,128)(2,1)} %constant.17.clone.inv_ref, s32[32,1]{1,0:T(8,128)} %copy.13.orient_ref), custom_call_target="tpu_custom_call" | custom-call | tf_op jit(solution)/shard_map/match/pallas_call | solution.py:167
  69.2 1.5 %copy.14 = f32[96,32]{0,1:T(8,128)} copy(f32[96,32]{1,0:T(8,128)} %get-tuple-element.4) | data formatting | bytes 24576 | tf_op jit(solution)/shard_map/match/pallas_call | solution.py:167
  70.6 1.5 %copy.15 = f32[96,16]{0,1:T(8,128)} copy(f32[96,16]{1,0:T(8,128)} %get-tuple-element.5) | data formatting | bytes 12288 | tf_op jit(solution)/shard_map/match/pallas_call | solution.py:167
  (6 shorter events, 0.1 us)
Async XLA Ops:
  2.5 7.9 %collective-permute-start = (bf16[2,128,128]{2,1,0:T(8,128)(2,1)}, bf16[2,128,128]{2,1,0:T(8,128)(2,1)S(1)}, u32[]{:S(2)}, u32[]{:S(2)}) collective-permute-start(bf16[2,128,128]{2,1,0:T(8,128)(2,1)} %template_spectra.1), channel_id=1, source_target_pairs={{0,8},{1,9},{2,10},{3,11},{4,12},{5,13},{6,14},{7,15},{8,0},{9,1},... | collective-permute-start | bytes 196616 | tf_op jit(solution)/shard_map/ppermute | solution.py:198
  11.2 5.9 %collective-permute-start.1 = (bf16[4,128,128]{2,1,0:T(8,128)(2,1)S(1)}, bf16[4,128,128]{2,1,0:T(8,128)(2,1)S(1)}, u32[]{:S(2)}, u32[]{:S(2)}) collective-permute-start(bf16[4,128,128]{2,1,0:T(8,128)(2,1)S(1)} %pad_maximum_fusion.2), channel_id=1, source_target_pairs={{0,4},{1,5},{2,6},{3,7},{4,0},{5,1},{6,2},{7,3},{8,12},{9,13},{10,... | collective-permute-start | bytes 393224 | tf_op jit(solution)/shard_map/ppermute | solution.py:198
  12.8 18.2 %collective-permute-start.5 = (bf16[1,64,256]{2,1,0:T(8,128)(2,1)S(1)}, bf16[1,64,256]{2,1,0:T(8,128)(2,1)S(1)}, u32[]{:S(2)}, u32[]{:S(2)}) collective-permute-start(bf16[1,64,256]{2,1,0:T(8,128)(2,1)S(1)} %get-tuple-element.6), channel_id=1, source_target_pairs={{1,0},{2,1},{3,2},{4,3},{5,4},{6,5},{7,6},{8,7},{9,8},{10,9},{11,1... | collective-permute-start | bytes 98312 | tf_op jit(solution)/shard_map/ppermute | solution.py:193
  14.0 16.9 %collective-permute-start.4 = (bf16[1,64,256]{2,1,0:T(8,128)(2,1)S(1)}, bf16[1,64,256]{2,1,0:T(8,128)(2,1)S(1)}, u32[]{:S(2)}, u32[]{:S(2)}) collective-permute-start(bf16[1,64,256]{2,1,0:T(8,128)(2,1)S(1)} %get-tuple-element.7), channel_id=1, source_target_pairs={{0,1},{1,2},{2,3},{3,4},{4,5},{5,6},{6,7},{7,8},{8,9},{9,10},{10,1... | collective-permute-start | bytes 98312 | tf_op jit(solution)/shard_map/ppermute | solution.py:192
  18.0 9.1 %collective-permute-start.2 = (bf16[8,128,128]{2,1,0:T(8,128)(2,1)S(1)}, bf16[8,128,128]{2,1,0:T(8,128)(2,1)S(1)}, u32[]{:S(2)}, u32[]{:S(2)}) collective-permute-start(bf16[8,128,128]{2,1,0:T(8,128)(2,1)S(1)} %pad_maximum_fusion.1), channel_id=1, source_target_pairs={{0,2},{1,3},{2,0},{3,1},{4,6},{5,7},{6,4},{7,5},{8,10},{9,11},{10,... | collective-permute-start | bytes 786440 | tf_op jit(solution)/shard_map/ppermute | solution.py:198
  27.9 24.4 %collective-permute-start.3 = (bf16[16,128,128]{2,1,0:T(8,128)(2,1)S(1)}, bf16[16,128,128]{2,1,0:T(8,128)(2,1)S(1)}, u32[]{:S(2)}, u32[]{:S(2)}) collective-permute-start(bf16[16,128,128]{2,1,0:T(8,128)(2,1)S(1)} %pad_maximum_fusion), channel_id=1, source_target_pairs={{0,1},{1,0},{2,3},{3,2},{4,5},{5,4},{6,7},{7,6},{8,9},{9,8},{10,11... | collective-permute-start | bytes 1572872 | tf_op jit(solution)/shard_map/ppermute | solution.py:198
  31.0 0.6 copy-start.1
  31.6 0.6 copy-start.2
  52.5 1.0 %copy-start = (bf16[32,128,128]{2,1,0:T(8,128)(2,1)}, bf16[32,128,128]{2,1,0:T(8,128)(2,1)S(1)}, u32[]{:S(2)}) copy-start(bf16[32,128,128]{2,1,0:T(8,128)(2,1)S(1)} %constant_dynamic-update-slice_fusion.tmpl_ref) | copy-start | bytes 3145732

commit v2 on v1

v2 whole, which is shorter than its diff:
```python
import functools
import math

import jax
import jax.numpy as jnp
import numpy as np
from jax import lax
from jax.experimental import pallas as pl
from jax.experimental.pallas import tpu as pltpu
from jax.sharding import PartitionSpec as P

RADII = 64
ANGLES = 256
HALF = ANGLES // 2
GAINS = 8
TMPL_PER_GROUP = 2
LANES = 128
BLOCK = 32
PER_DEVICE = 2
F32 = jnp.float32
BF16 = jnp.bfloat16
CONTRACT_LAST = (((1,), (1,)), ((), ()))


def make_tables():
    along = np.arange(ANGLES, dtype=np.int32)
    modes = np.arange(HALF + 1, dtype=np.int32)
    scale = np.float32(2.0 * math.pi / ANGLES)
    phase = scale * (along[:, None] * modes[None, :] % ANGLES).astype(np.float32)
    cos, sin = np.cos(phase), np.sin(phase)
    basis = np.concatenate([cos, sin[:, 1:HALF]], axis=1)
    norm = np.float32(1.0 / (ANGLES * math.sqrt(RADII * ANGLES)))
    weight = np.where((modes == 0) | (modes == HALF), 1.0, 2.0).astype(np.float32)
    inv_cos = weight[None, :] * cos * norm
    inv_sin = -weight[None, :] * sin * norm
    inverse = np.concatenate([inv_cos, inv_sin[:, 1:HALF]], axis=1)
    return basis.T.astype(jnp.bfloat16), inverse.astype(jnp.bfloat16)


PITCH = LANES + 8
SIDE = 2 * BLOCK + 8


def pattern_kernel(bin_ref, gain_ref, pat_ref, before_ref, after_ref, table_ref, out_ref, raw_ref, spec_ref, *, first):
    count = pat_ref.shape[0]
    radii = out_ref.shape[1] // 2
    pitch = 2 * radii + 8
    zero = jnp.zeros((LANES - count, LANES), F32)

    def put(pos, rows):
        wide = rows.astype(F32)
        raw_ref[0, pl.ds(pos, radii, stride=PITCH), :] = wide[:, :LANES]
        raw_ref[1, pl.ds(pos, radii, stride=PITCH), :] = wide[:, LANES:]

    for r in range(radii):
        raw_ref[0, pl.ds(r * PITCH + count, LANES - count), :] = zero
        raw_ref[1, pl.ds(r * PITCH + count, LANES - count), :] = zero

    def place(p, carry):
        put(p, pat_ref[p, pl.ds(first, radii)])
        return carry

    lax.fori_loop(0, count, place, 0, unroll=16)
    put(count, after_ref[0, pl.ds(first, radii)])
    put(LANES - 1, before_ref[0, pl.ds(first, radii)])

    def step(r, carry):
        begin = pl.multiple_of(r * PITCH, 8)
        rows = jnp.concatenate(
            [raw_ref[0, pl.ds(begin, LANES), :], raw_ref[1, pl.ds(begin, LANES), :]], axis=1
        ).astype(BF16)
        spec = lax.dot_general(table_ref[...], rows, CONTRACT_LAST, preferred_element_type=F32)
        spec = spec * gain_ref[bin_ref[first + r]]
        spec_ref[pl.ds(r, HALF, stride=pitch), :] = spec[:HALF]
        spec_ref[pl.ds(radii + r, HALF, stride=pitch), :] = spec[HALF:]
        return carry

    lax.fori_loop(0, radii, step, 0, unroll=16)

    def narrow(k, carry):
        out_ref[k] = spec_ref[pl.ds(pl.multiple_of(k * pitch, 8), 2 * radii), :].astype(BF16)
        return carry

    lax.fori_loop(0, HALF, narrow, 0, unroll=16)


def match_kernel(
    index_ref, orient_ref, tmpl_ref, low_ref, high_ref, table_ref, inv_ref, corr_ref, smooth_ref, side_ref, cross_ref, best_ref
):
    total = tmpl_ref.shape[0]
    count = corr_ref.shape[1]
    bits = (total // PER_DEVICE).bit_length() - 1
    best_ref[...] = jnp.full(best_ref.shape, -jnp.inf, F32)
    low = lax.broadcasted_iota(jnp.int32, (HALF, LANES), 1) < RADII
    low_edge = lax.broadcasted_iota(jnp.int32, (BLOCK, LANES), 1) < RADII

    def chunk(begin):
        for t in range(0, BLOCK, 2):
            pair = tmpl_ref[pl.ds(begin + t, 2)].reshape(2 * RADII, ANGLES)
            spec = lax.dot_general(table_ref[...], pair, CONTRACT_LAST, preferred_element_type=F32)
            cos, sin = spec[:HALF], spec[HALF:]
            turned_cos, turned_sin = pltpu.roll(cos, RADII, 1), pltpu.roll(sin, RADII, 1)
            side_ref[pl.ds(t, HALF, stride=SIDE), :] = jnp.where(low, cos, turned_sin)
            side_ref[pl.ds(t + 1, HALF, stride=SIDE), :] = jnp.where(low, turned_cos, sin)
            side_ref[pl.ds(BLOCK + t, HALF, stride=SIDE), :] = jnp.where(low, sin, -turned_cos)
            side_ref[pl.ds(BLOCK + t + 1, HALF, stride=SIDE), :] = jnp.where(low, turned_sin, -cos)
        for k in range(HALF):
            if k:
                left = side_ref[pl.ds(k * SIDE, 2 * BLOCK), :]
            else:
                edge = side_ref[pl.ds(0, BLOCK), :]
                left = jnp.concatenate([jnp.where(low_edge, edge, 0.0), jnp.where(low_edge, 0.0, edge)], axis=0)
            lower, upper = low_ref[k], high_ref[k]
            half = RADII // 2
            right = jnp.concatenate([lower[:half], upper[:half], lower[half:], upper[half:]], axis=0)
            cross_ref[pl.ds(k * SIDE, 2 * BLOCK), :] = jnp.dot(left.astype(BF16), right, preferred_element_type=F32)
        rows = []
        for t in range(BLOCK):
            real = cross_ref[pl.ds(t, HALF, stride=SIDE), :]
            imag = cross_ref[pl.ds(BLOCK + t, HALF, stride=SIDE), :]
            cross = jnp.concatenate([real, imag], axis=0).astype(BF16)
            shifted = jnp.dot(inv_ref[...], cross, preferred_element_type=F32)
            rows.append(jnp.max(shifted, axis=0, keepdims=True))
        for t in range(BLOCK):
            place = begin + t
            held = place // PER_DEVICE
            device = index_ref[0]
            for b in range(bits):
                device = device ^ (((held >> b) & 1) << (bits - 1 - b))
            where = device * PER_DEVICE + place % PER_DEVICE
            corr_ref[pl.ds(where, 1), :] = rows[t][:, :count]
            group = orient_ref[where]
            best_ref[pl.ds(group, 1), :] = jnp.maximum(best_ref[pl.ds(group, 1), :], rows[t])

    chunk(0)
    if total > BLOCK:

        def more(i, carry):
            chunk(i * BLOCK)
            return carry

        lax.fori_loop(1, total // BLOCK, more, 0)
    best = best_ref[...]
    smooth = 0.25 * (pltpu.roll(best, 1, 1) + 2.0 * best + pltpu.roll(best, LANES - 1, 1))
    smooth_ref[...] = smooth[:, :count]


VMEM = pl.BlockSpec(memory_space=pltpu.VMEM)
SMEM = pl.BlockSpec(memory_space=pltpu.SMEM)
HBM = pl.BlockSpec(memory_space=pl.ANY)


def pattern_spectra(first, radii, bins, gains, patterns, before, after, table):
    return pl.pallas_call(
        functools.partial(pattern_kernel, first=first),
        out_shape=jax.ShapeDtypeStruct((HALF, 2 * radii, LANES), BF16),
        in_specs=[SMEM] * 2 + [VMEM] * 4,
        out_specs=VMEM,
        scratch_shapes=[
            pltpu.VMEM((2, radii * PITCH, LANES), F32),
            pltpu.VMEM((HALF * (2 * radii + 8), LANES), F32),
        ],
        compiler_params=pltpu.CompilerParams(vmem_limit_bytes=24 << 20),
        name="pattern_spectra",
    )(bins, gains, patterns, before, after, table)


def match(index, orientation, templates, lower, upper, table, inverse, count, groups):
    total = templates.shape[0]
    return pl.pallas_call(
        match_kernel,
        out_shape=(jax.ShapeDtypeStruct((total, count), F32), jax.ShapeDtypeStruct((groups, count), F32)),
        in_specs=[SMEM] * 2 + [VMEM] * 5,
        out_specs=(VMEM, VMEM),
        scratch_shapes=[
            pltpu.VMEM((HALF * SIDE, LANES), F32),
            pltpu.VMEM((HALF * SIDE, LANES), F32),
            pltpu.VMEM((groups, LANES), F32),
        ],
        compiler_params=pltpu.CompilerParams(vmem_limit_bytes=32 << 20),
        name="match",
    )(index, orientation, templates, lower, upper, table, inverse)


def on_device(patterns, templates, radius_bin, radial_gain, orientation):
    table, inverse = make_tables()
    table, inverse = jnp.asarray(table), jnp.asarray(inverse)
    count = patterns.shape[0]
    size = lax.axis_size("scan")
    mine = templates.shape[0]
    groups = mine * size // TMPL_PER_GROUP
    up = [(i, i + 1) for i in range(size - 1)]
    down = [(j, i) for i, j in up]
    steps = [1 << b for b in reversed(range(size.bit_length() - 1))]
    before = lax.ppermute(patterns[count - 1 :], "scan", up)
    after = lax.ppermute(patterns[:1], "scan", down)
    gathered = templates
    halves = []
    for number, bit in enumerate(steps):
        length = gathered.shape[0]
        other = lax.ppermute(gathered, "scan", [(i, i ^ bit) for i in range(size)])
        room = lax.optimization_barrier(
            lax.dynamic_update_slice(jnp.zeros((2 * length,) + gathered.shape[1:], BF16), gathered, (0, 0, 0))
        )
        gathered = lax.dynamic_update_slice(room, other, (length, 0, 0))
        if number == 0:
            gathered, before, after = lax.optimization_barrier((gathered, before, after))
        elif number <= 2:
            half = pattern_spectra(
                (number - 1) * (RADII // 2), RADII // 2, radius_bin, radial_gain, patterns, before, after, table
            )
            gathered, half, before, after = lax.optimization_barrier((gathered, half, before, after))
            halves.append(half)
        else:
            gathered = lax.optimization_barrier(gathered)
    index = lax.axis_index("scan").astype(jnp.int32).reshape(1)
    corr, smooth = match(index, orientation.reshape(-1), gathered, *halves, table, inverse, count, groups)
    return corr.T, smooth.T


def solution(mesh):
    placed = (P(("grp", "scan"), None, None), P("scan", None, None), P(), P(), P())
    return jax.shard_map(
        on_device,
        mesh=mesh,
        in_specs=placed,
        out_specs=(P(("grp", "scan"), None), P(("grp", "scan"), None)),
        check_vma=False,
    )
```

time: 72.7 us -> 38.4 us (0.53)
  Pallas kernels: 37.7 us -> 10.9 us
  local copies, waits for them, and re-layouts: 10.1 us -> 7.3 us
  other arithmetic: 2.7 us -> 0 us
  waiting for transfers between devices: 10 us -> 7.91 us
    pallas_call x3, Pallas kernels: 37.7 us -> 10.9 us  [the longest x2 5.99 us: pattern_spectra(): pl.pallas_call(functools.partial(pattern_kernel, first=first), out_shape=...]
    ppermute x4, waiting for transfers between devices: 10 us -> 5.41 us  [on_device(): other = lax.ppermute(gathered, 'scan', [(i, i ^ bit) for i in range(size)])]
    pallas_call x2 -> x0, local copies, waits for them, and re-layouts: 2.94 us -> none  [match(): pl.pallas_call(match_kernel, out_shape=(jax.ShapeDtypeStruct((count, tota...]
    concatenate x3 -> x0, other arithmetic: 2.61 us -> none  [on_device(): gathered = jnp.concatenate([gathered, other], axis=0)]
    ppermute x1, waiting for transfers between devices: 0.01 us -> 2.5 us  [on_device(): after = lax.ppermute(patterns[:1], 'scan', down)]
    ppermute x4, starting transfers between devices: 6.54 us -> 8.33 us  [on_device(): other = lax.ppermute(gathered, 'scan', [(i, i ^ bit) for i in range(size)])]
    ppermute x1, starting transfers between devices: 3.03 us -> 1.45 us  [on_device(): before = lax.ppermute(patterns[count - 1:], 'scan', up)]
    gather x1 -> x0, local copies, waits for them, and re-layouts: 1.31 us -> none  [on_device(): jnp.asarray(slot)[which][:, None] * mine + jnp.arange(mine, dtype=jnp.int32)]
  transfers between devices with their start and end apart: 6 -> 6, of which waited for: 2 -> 3; matrix products, arithmetic and copies ran while one was open for 9% -> 5% of each run, Pallas kernels for 28% -> 16%
where the time goes in v2:
time: 38.4 us; the launch traced here: 38 us
  starting transfers between devices  11.1 us (29%)
  Pallas kernels  10.9 us (28%)
  waiting for transfers between devices  7.91 us (21%)
  local copies, waits for them, and re-layouts  7.3 us (19%)
  between operations  0.83 us (2%)
    ppermute x4, starting transfers between devices, on_device(): other = lax.ppermute(gathered, 'scan', [(i, i ^ bit) for i in range(size)])  8.33 us
    pallas_call x2, Pallas kernels, pattern_spectra(): pl.pallas_call(functools.partial(pattern_kernel, first=first), out_shape=...  5.99 us
    unnamed x18, local copies, waits for them, and re-layouts  5.44 us
    ppermute x4, waiting for transfers between devices, on_device(): other = lax.ppermute(gathered, 'scan', [(i, i ^ bit) for i in range(size)])  5.41 us
    pallas_call x1, Pallas kernels, match(): pl.pallas_call(match_kernel, out_shape=(jax.ShapeDtypeStruct((total, coun...  4.96 us
    ppermute x1, waiting for transfers between devices, on_device(): after = lax.ppermute(patterns[:1], 'scan', down)  2.5 us
    ppermute x1, starting transfers between devices, on_device(): before = lax.ppermute(patterns[count - 1:], 'scan', up)  1.45 us
    ppermute x1, starting transfers between devices, on_device(): after = lax.ppermute(patterns[:1], 'scan', down)  1.29 us
  transfers between devices with their start and end apart: 6, of which 3 were waited for; matrix products, arithmetic and copies ran while one was open for 5% of the time, Pallas kernels for 16%

profile of v2, /device:TPU:0, one launch (start us, length us, event | category | flops | bytes accessed | tf_op | source)
XLA Modules:
  0.0 38.0 jit_solution(3878297190437875257)
XLA Ops:
  0.6 4.1 %collective-permute-start = (bf16[2,64,256]{2,1,0:T(8,128)(2,1)}, bf16[2,64,256]{2,1,0:T(8,128)(2,1)S(1)}, u32[]{:S(2)}, u32[]{:S(2)}) collective-permute-start(bf16[2,64,256]{2,1,0:T(8,128)(2,1)} %param.8), channel_id=1, source_target_pairs={{0,8},{1,9},{2,10},{3,11},{4,12},{5,13},{6,14},{7,15},{8,0},{9,1},... | collective-permute-start | bytes 196616 | tf_op jit(solution)/shard_map/ppermute | solution.py:201
  4.7 0.8 %fusion = (bf16[1,64,256]{2,1,0:T(8,128)(2,1)S(1)}, bf16[1,64,256]{2,1,0:T(8,128)(2,1)S(1)}) fusion(bf16[96,64,256]{2,1,0:T(8,128)(2,1)} %pat_ref.3), kind=kLoop, calls=%fused_computation.4 | loop fusion | bytes 131072 | tf_op jit(solution)/shard_map/slice | solution.py:196
  5.5 1.4 %collective-permute-start.1 = (bf16[1,64,256]{2,1,0:T(8,128)(2,1)S(1)}, bf16[1,64,256]{2,1,0:T(8,128)(2,1)S(1)}, u32[]{:S(2)}, u32[]{:S(2)}) collective-permute-start(bf16[1,64,256]{2,1,0:T(8,128)(2,1)S(1)} %get-tuple-element.25), channel_id=1, source_target_pairs={{0,1},{1,2},{2,3},{3,4},{4,5},{5,6},{6,7},{7,8},{8,9},{9,10},{10,1... | collective-permute-start | bytes 98312 | tf_op jit(solution)/shard_map/ppermute | solution.py:195
  7.0 1.3 %collective-permute-start.2 = (bf16[1,64,256]{2,1,0:T(8,128)(2,1)S(1)}, bf16[1,64,256]{2,1,0:T(8,128)(2,1)S(1)}, u32[]{:S(2)}, u32[]{:S(2)}) collective-permute-start(bf16[1,64,256]{2,1,0:T(8,128)(2,1)S(1)} %get-tuple-element.24), channel_id=1, source_target_pairs={{1,0},{2,1},{3,2},{4,3},{5,4},{6,5},{7,6},{8,7},{9,8},{10,9},{11,1... | collective-permute-start | bytes 98312 | tf_op jit(solution)/shard_map/ppermute | solution.py:196
  8.3 0.9 %dynamic_update_slice.24 = bf16[4,64,256]{2,1,0:T(8,128)(2,1)S(1)} pad(bf16[2,64,256]{2,1,0:T(8,128)(2,1)} %param.8, bf16[]{:T(256)} %constant.10.clone.1), padding=0_2x0_0x0_0 | pad | bytes 196610 | tf_op jit(solution)/shard_map/dynamic_update_slice | solution.py:203
  9.1 0.0 collective-permute-done
  9.1 0.0 collective-permute-done.1.before_ref
  9.2 2.5 %collective-permute-done.2.after_ref = bf16[1,64,256]{2,1,0:T(8,128)(2,1)S(1)} collective-permute-done((bf16[1,64,256]{2,1,0:T(8,128)(2,1)S(1)}, bf16[1,64,256]{2,1,0:T(8,128)(2,1)S(1)}, u32[]{:S(2)}, u32[]{:S(2)}) %collective-permute-start.2) | collective-permute-done | bytes 32800 | tf_op jit(solution)/shard_map/ppermute | solution.py:196
  11.7 3.5 %collective-permute-start.3 = (bf16[4,64,256]{2,1,0:T(8,128)(2,1)S(1)}, bf16[4,64,256]{2,1,0:T(8,128)(2,1)S(1)}, u32[]{:S(2)}, u32[]{:S(2)}) collective-permute-start(bf16[4,64,256]{2,1,0:T(8,128)(2,1)S(1)} %constant_dynamic-update-slice_fusion.3), channel_id=1, source_target_pairs={{0,4},{1,5},{2,6},{3,7},{4,0},{5,1},{6,2},{7,3},{8,12},{9,13},{10,... | collective-permute-start | bytes 393224 | tf_op jit(solution)/shard_map/ppermute | solution.py:201
  15.1 0.0 copy-start
  15.2 1.9 %copy-done = bf16[96,64,256]{2,1,0:T(8,128)(2,1)S(1)} copy-done((bf16[96,64,256]{2,1,0:T(8,128)(2,1)S(1)}, bf16[96,64,256]{2,1,0:T(8,128)(2,1)}, u32[]{:S(2)}) %copy-start) | copy-done | bytes 3145752
  17.0 0.0 copy-start.3
  17.0 0.9 %copy-done.3 = bf16[256,256]{1,0:T(8,128)(2,1)S(1)} copy-done((bf16[256,256]{1,0:T(8,128)(2,1)S(1)}, bf16[256,256]{1,0:T(8,128)(2,1)}, u32[]{:S(2)}) %copy-start.3) | copy-done | bytes 131096
  17.9 0.0 copy-start.6
  17.9 0.7 %copy-done.6 = s32[64]{0:T(128)S(1)} copy-done((s32[64]{0:T(128)S(1)}, s32[64]{0:T(128)}, u32[]{:S(2)}) %copy-start.6) | copy-done | bytes 280
  18.6 0.0 copy-start.7
  18.6 0.7 %copy-done.7 = f32[8]{0:T(128)S(1)} copy-done((f32[8]{0:T(128)S(1)}, f32[8]{0:T(128)}, u32[]{:S(2)}) %copy-start.7) | copy-done | bytes 56
  19.3 3.0 %pattern_spectra.2.low_ref = bf16[128,64,128]{2,1,0:T(8,128)(2,1)S(1)} custom-call(s32[64]{0:T(128)S(1)} %copy-done.6, f32[8]{0:T(128)S(1)} %copy-done.7, bf16[96,64,256]{2,1,0:T(8,128)(2,1)S(1)} %copy-done, bf16[1,64,256]{2,1,0:T(8,128)(2,1)S(1)} %collective-permute-done.1.before_ref, bf16[1,64,256]{2,1,0:T(8,128)(2,1)S(1)} %collective-permute-done.2.after_ref, ...), custom_call_target="tpu_custom_call" | custom-call | tf_op jit(solution)/shard_map/pattern_spectra/pallas_call | solution.py:154
  22.3 0.0 collective-permute-done.3
  22.3 0.7 %collective-permute-start.4 = (bf16[8,64,256]{2,1,0:T(8,128)(2,1)S(1)}, bf16[8,64,256]{2,1,0:T(8,128)(2,1)S(1)}, u32[]{:S(2)}, u32[]{:S(2)}) collective-permute-start(bf16[8,64,256]{2,1,0:T(8,128)(2,1)S(1)} %constant_dynamic-update-slice_fusion.2), channel_id=1, source_target_pairs={{0,2},{1,3},{2,0},{3,1},{4,6},{5,7},{6,4},{7,5},{8,10},{9,11},{10,... | collective-permute-start | bytes 786440 | tf_op jit(solution)/shard_map/ppermute | solution.py:201
  23.0 0.0 copy-start.4
  23.0 0.0 copy-start.5
  23.0 0.0 copy-start.8
  23.1 3.0 %pattern_spectra.3.high_ref = bf16[128,64,128]{2,1,0:T(8,128)(2,1)S(1)} custom-call(s32[64]{0:T(128)S(1)} %copy-done.6, f32[8]{0:T(128)S(1)} %copy-done.7, bf16[96,64,256]{2,1,0:T(8,128)(2,1)S(1)} %copy-done, bf16[1,64,256]{2,1,0:T(8,128)(2,1)S(1)} %collective-permute-done.1.before_ref, bf16[1,64,256]{2,1,0:T(8,128)(2,1)S(1)} %collective-permute-done.2.after_ref, ...), custom_call_target="tpu_custom_call" | custom-call | tf_op jit(solution)/shard_map/pattern_spectra/pallas_call | solution.py:154
  26.1 0.0 copy-start.1
  26.1 1.3 %copy-done.1 = bf16[128,64,128]{2,1,0:T(8,128)(2,1)} copy-done((bf16[128,64,128]{2,1,0:T(8,128)(2,1)}, bf16[128,64,128]{2,1,0:T(8,128)(2,1)S(1)}, u32[]{:S(2)}) %copy-start.1) | copy-done | bytes 2097176
  27.4 3.6 %collective-permute-done.4 = bf16[8,64,256]{2,1,0:T(8,128)(2,1)S(1)} collective-permute-done((bf16[8,64,256]{2,1,0:T(8,128)(2,1)S(1)}, bf16[8,64,256]{2,1,0:T(8,128)(2,1)S(1)}, u32[]{:S(2)}, u32[]{:S(2)}) %collective-permute-start.4) | collective-permute-done | bytes 262176 | tf_op jit(solution)/shard_map/ppermute | solution.py:201
  31.0 0.1 collective-permute-start.5
  31.1 0.0 copy-start.2
  31.1 0.1 dynamic_update_slice.30
  31.2 1.8 %collective-permute-done.5 = bf16[16,64,256]{2,1,0:T(8,128)(2,1)S(1)} collective-permute-done((bf16[16,64,256]{2,1,0:T(8,128)(2,1)S(1)}, bf16[16,64,256]{2,1,0:T(8,128)(2,1)S(1)}, u32[]{:S(2)}, u32[]{:S(2)}) %collective-permute-start.5) | collective-permute-done | bytes 524320 | tf_op jit(solution)/shard_map/ppermute | solution.py:201
  33.1 0.0 copy-done.4
  33.1 0.0 copy-done.5
  33.1 0.0 copy-done.8
  33.1 0.0 copy-done.2
  33.1 5.0 %match.1 = (f32[32,96]{1,0:T(8,128)}, f32[16,96]{1,0:T(8,128)}) custom-call(s32[1]{0:T(128)} %bitcast.index_ref, s32[32]{0:T(128)S(1)} %bitcast.4, bf16[32,64,256]{2,1,0:T(8,128)(2,1)S(1)} %constant_dynamic-update-slice_fusion.tmpl_ref, bf16[128,64,128]{2,1,0:T(8,128)(2,1)S(1)} %pattern_spectra.2.low_ref, bf16[128,64,128]{2,1,0:T(8,128)(2,1)S(1)} %copy-done.2, ...), custom_call_target="tpu_custom_call" | custom-call | tf_op jit(solution)/shard_map/match/pallas_call | solution.py:170
  (6 shorter events, 0.1 us)
Async XLA Ops:
  0.6 8.5 %collective-permute-start = (bf16[2,64,256]{2,1,0:T(8,128)(2,1)}, bf16[2,64,256]{2,1,0:T(8,128)(2,1)S(1)}, u32[]{:S(2)}, u32[]{:S(2)}) collective-permute-start(bf16[2,64,256]{2,1,0:T(8,128)(2,1)} %param.8), channel_id=1, source_target_pairs={{0,8},{1,9},{2,10},{3,11},{4,12},{5,13},{6,14},{7,15},{8,0},{9,1},... | collective-permute-start | bytes 196616 | tf_op jit(solution)/shard_map/ppermute | solution.py:201
  5.5 3.6 %collective-permute-start.1 = (bf16[1,64,256]{2,1,0:T(8,128)(2,1)S(1)}, bf16[1,64,256]{2,1,0:T(8,128)(2,1)S(1)}, u32[]{:S(2)}, u32[]{:S(2)}) collective-permute-start(bf16[1,64,256]{2,1,0:T(8,128)(2,1)S(1)} %get-tuple-element.25), channel_id=1, source_target_pairs={{0,1},{1,2},{2,3},{3,4},{4,5},{5,6},{6,7},{7,8},{8,9},{9,10},{10,1... | collective-permute-start | bytes 98312 | tf_op jit(solution)/shard_map/ppermute | solution.py:195
  7.0 4.7 %collective-permute-start.2 = (bf16[1,64,256]{2,1,0:T(8,128)(2,1)S(1)}, bf16[1,64,256]{2,1,0:T(8,128)(2,1)S(1)}, u32[]{:S(2)}, u32[]{:S(2)}) collective-permute-start(bf16[1,64,256]{2,1,0:T(8,128)(2,1)S(1)} %get-tuple-element.24), channel_id=1, source_target_pairs={{1,0},{2,1},{3,2},{4,3},{5,4},{6,5},{7,6},{8,7},{9,8},{10,9},{11,1... | collective-permute-start | bytes 98312 | tf_op jit(solution)/shard_map/ppermute | solution.py:196
  11.7 10.6 %collective-permute-start.3 = (bf16[4,64,256]{2,1,0:T(8,128)(2,1)S(1)}, bf16[4,64,256]{2,1,0:T(8,128)(2,1)S(1)}, u32[]{:S(2)}, u32[]{:S(2)}) collective-permute-start(bf16[4,64,256]{2,1,0:T(8,128)(2,1)S(1)} %constant_dynamic-update-slice_fusion.3), channel_id=1, source_target_pairs={{0,4},{1,5},{2,6},{3,7},{4,0},{5,1},{6,2},{7,3},{8,12},{9,13},{10,... | collective-permute-start | bytes 393224 | tf_op jit(solution)/shard_map/ppermute | solution.py:201
  15.1 1.9 %copy-start = (bf16[96,64,256]{2,1,0:T(8,128)(2,1)S(1)}, bf16[96,64,256]{2,1,0:T(8,128)(2,1)}, u32[]{:S(2)}) copy-start(bf16[96,64,256]{2,1,0:T(8,128)(2,1)} %pat_ref.3) | copy-start | bytes 9437188
  17.0 0.9 %copy-start.3 = (bf16[256,256]{1,0:T(8,128)(2,1)S(1)}, bf16[256,256]{1,0:T(8,128)(2,1)}, u32[]{:S(2)}) copy-start(bf16[256,256]{1,0:T(8,128)(2,1)} %constant.6.clone.table_ref) | copy-start | bytes 393220
  17.9 0.7 %copy-start.6 = (s32[64]{0:T(128)S(1)}, s32[64]{0:T(128)}, u32[]{:S(2)}) copy-start(s32[64]{0:T(128)} %bin_ref.3) | copy-start | bytes 772
  18.6 0.7 %copy-start.7 = (f32[8]{0:T(128)S(1)}, f32[8]{0:T(128)}, u32[]{:S(2)}) copy-start(f32[8]{0:T(128)} %gain_ref.3) | copy-start | bytes 100
  22.3 8.7 %collective-permute-start.4 = (bf16[8,64,256]{2,1,0:T(8,128)(2,1)S(1)}, bf16[8,64,256]{2,1,0:T(8,128)(2,1)S(1)}, u32[]{:S(2)}, u32[]{:S(2)}) collective-permute-start(bf16[8,64,256]{2,1,0:T(8,128)(2,1)S(1)} %constant_dynamic-update-slice_fusion.2), channel_id=1, source_target_pairs={{0,2},{1,3},{2,0},{3,1},{4,6},{5,7},{6,4},{7,5},{8,10},{9,11},{10,... | collective-permute-start | bytes 786440 | tf_op jit(solution)/shard_map/ppermute | solution.py:201
  23.0 10.0 %copy-start.4 = (bf16[256,256]{1,0:T(8,128)(2,1)S(1)}, bf16[256,256]{1,0:T(8,128)(2,1)}, u32[]{:S(2)}) copy-start(bf16[256,256]{1,0:T(8,128)(2,1)} %constant.6.clone.table_ref) | copy-start | bytes 393220
  23.0 10.0 %copy-start.5 = (bf16[256,256]{1,0:T(8,128)(2,1)S(1)}, bf16[256,256]{1,0:T(8,128)(2,1)}, u32[]{:S(2)}) copy-start(bf16[256,256]{1,0:T(8,128)(2,1)} %constant.7.clone.inv_ref) | copy-start | bytes 393220
  23.0 10.0 %copy-start.8 = (s32[32,1]{0,1:T(1,128)S(1)}, s32[32,1]{0,1:T(1,128)}, u32[]{:S(2)}) copy-start(s32[32,1]{0,1:T(1,128)} %param.11) | copy-start | bytes 388
  26.1 1.3 %copy-start.1 = (bf16[128,64,128]{2,1,0:T(8,128)(2,1)}, bf16[128,64,128]{2,1,0:T(8,128)(2,1)S(1)}, u32[]{:S(2)}) copy-start(bf16[128,64,128]{2,1,0:T(8,128)(2,1)S(1)} %pattern_spectra.3.high_ref) | copy-start | bytes 6291460
  31.0 2.0 %collective-permute-start.5 = (bf16[16,64,256]{2,1,0:T(8,128)(2,1)S(1)}, bf16[16,64,256]{2,1,0:T(8,128)(2,1)S(1)}, u32[]{:S(2)}, u32[]{:S(2)}) collective-permute-start(bf16[16,64,256]{2,1,0:T(8,128)(2,1)S(1)} %constant_dynamic-update-slice_fusion.1), channel_id=1, source_target_pairs={{0,1},{1,0},{2,3},{3,2},{4,5},{5,4},{6,7},{7,6},{8,9},{9,8},{10,11... | collective-permute-start | bytes 1572872 | tf_op jit(solution)/shard_map/ppermute | solution.py:201
  31.1 2.0 %copy-start.2 = (bf16[128,64,128]{2,1,0:T(8,128)(2,1)S(1)}, bf16[128,64,128]{2,1,0:T(8,128)(2,1)}, u32[]{:S(2)}) copy-start(bf16[128,64,128]{2,1,0:T(8,128)(2,1)} %copy-done.1) | copy-start | bytes 6291460

commit v3 on v2

v3 whole, which is shorter than its diff:
```python
import functools
import math

import jax
import jax.numpy as jnp
import numpy as np
from jax import lax
from jax.experimental import pallas as pl
from jax.experimental.pallas import tpu as pltpu
from jax.sharding import PartitionSpec as P

RADII = 64
ANGLES = 256
HALF = ANGLES // 2
GAINS = 8
TMPL_PER_GROUP = 2
LANES = 128
BLOCK = 32
ROWS = 16
PER_DEVICE = 2
F32 = jnp.float32
BF16 = jnp.bfloat16
CONTRACT_LAST = (((1,), (1,)), ((), ()))


def make_tables():
    along = np.arange(ANGLES, dtype=np.int32)
    modes = np.arange(HALF + 1, dtype=np.int32)
    scale = np.float32(2.0 * math.pi / ANGLES)
    phase = scale * (along[:, None] * modes[None, :] % ANGLES).astype(np.float32)
    cos, sin = np.cos(phase), np.sin(phase)
    basis = np.concatenate([cos, sin[:, 1:HALF]], axis=1)
    norm = np.float32(1.0 / (ANGLES * math.sqrt(RADII * ANGLES)))
    weight = np.where((modes == 0) | (modes == HALF), 1.0, 2.0).astype(np.float32)
    inv_cos = weight[None, :] * cos * norm
    inv_sin = -weight[None, :] * sin * norm
    inverse = np.concatenate([inv_cos, inv_sin[:, 1:HALF]], axis=1)
    return basis.T.astype(jnp.bfloat16), inverse.astype(jnp.bfloat16)


PITCH = LANES + 8
SIDE = 2 * BLOCK + 8


def arrange_kernel(pat_hbm, tmpl_hbm, table_hbm, out_ref, own_ref, table_ref, pat_ref, raw_ref, sem, side_sem):
    chunks = pat_ref.shape[0] // ROWS

    def fetch(c):
        part = pl.ds(c * ROWS, ROWS)
        return pltpu.make_async_copy(pat_hbm.at[part], pat_ref.at[part], sem.at[c])

    sides = [
        pltpu.make_async_copy(tmpl_hbm, own_ref, side_sem.at[0]),
        pltpu.make_async_copy(table_hbm, table_ref, side_sem.at[1]),
    ]
    for c in range(chunks):
        fetch(c).start()
    for copy in sides:
        copy.start()
    for c in range(chunks):
        fetch(c).wait()
        for p in range(ROWS):
            wide = pat_ref[c * ROWS + p].astype(F32)
            raw_ref[c % 2, 0, pl.ds(p, RADII, stride=ROWS + 8), :] = wide[:, :LANES]
            raw_ref[c % 2, 1, pl.ds(p, RADII, stride=ROWS + 8), :] = wide[:, LANES:]
        for r in range(RADII):
            at = pl.ds(r * (ROWS + 8), ROWS)
            out_ref[r, pl.ds(c * ROWS, ROWS), :] = jnp.concatenate(
                [raw_ref[c % 2, 0, at, :], raw_ref[c % 2, 1, at, :]], axis=1
            ).astype(BF16)
    for copy in sides:
        copy.wait()


def pattern_kernel(bin_ref, gain_ref, rows_ref, inner_ref, outer_ref, table_ref, out_ref, edge_ref, weight_ref, spec_ref):
    count = rows_ref.shape[1]
    spare = LANES - count
    pitch = spare + 8
    even = lax.axis_index("scan") % 2 == 0
    edge_ref[...] = jnp.zeros(edge_ref.shape, F32)
    inner, outer = inner_ref[0].astype(F32), outer_ref[0].astype(F32)
    for at, wide in ((0, jnp.where(even, inner, outer)), (spare - 1, jnp.where(even, outer, inner))):
        edge_ref[0, pl.ds(at, RADII, stride=pitch), :] = wide[:, :LANES]
        edge_ref[1, pl.ds(at, RADII, stride=pitch), :] = wide[:, LANES:]
    for r in range(RADII):
        weight_ref[pl.ds(r, 1), :] = jnp.full((1, LANES), gain_ref[bin_ref[r]], F32)
    for r in range(RADII):
        at = pl.ds(r * pitch, spare)
        edge = jnp.concatenate([edge_ref[0, at, :], edge_ref[1, at, :]], axis=1).astype(BF16)
        rows = jnp.concatenate([rows_ref[r], edge], axis=0)
        spec = lax.dot_general(table_ref[...], rows, CONTRACT_LAST, preferred_element_type=F32)
        spec = spec * weight_ref[pl.ds(r, 1), :]
        spec_ref[pl.ds(r, HALF, stride=PITCH), :] = spec[:HALF]
        spec_ref[pl.ds(RADII + r, HALF, stride=PITCH), :] = spec[HALF:]
    for k in range(HALF):
        out_ref[k] = spec_ref[pl.ds(k * PITCH, LANES), :].astype(BF16)


def match_kernel(orient_ref, pat_ref, table_ref, inv_ref, *refs, held):
    parts = refs[: len(held)]
    corr_ref, smooth_ref, side_ref, cross_ref, best_ref = refs[len(held) :]
    count = corr_ref.shape[1]
    index = lax.axis_index("scan")
    blocks = [(part, i, mask) for part, masks in zip(parts, held) for i, mask in enumerate(masks)]
    best_ref[...] = jnp.full(best_ref.shape, -jnp.inf, F32)
    low = lax.broadcasted_iota(jnp.int32, (HALF, LANES), 1) < RADII
    low_edge = lax.broadcasted_iota(jnp.int32, (BLOCK, LANES), 1) < RADII
    for begin in range(0, len(blocks), BLOCK // PER_DEVICE):
        chunk = blocks[begin : begin + BLOCK // PER_DEVICE]
        for number, (part, i, _) in enumerate(chunk):
            t = number * PER_DEVICE
            pair = part[pl.ds(i * PER_DEVICE, PER_DEVICE)].reshape(PER_DEVICE * RADII, ANGLES)
            spec = lax.dot_general(table_ref[...], pair, CONTRACT_LAST, preferred_element_type=F32)
            cos, sin = spec[:HALF], spec[HALF:]
            turned_cos, turned_sin = pltpu.roll(cos, RADII, 1), pltpu.roll(sin, RADII, 1)
            side_ref[pl.ds(t, HALF, stride=SIDE), :] = jnp.where(low, cos, turned_sin)
            side_ref[pl.ds(t + 1, HALF, stride=SIDE), :] = jnp.where(low, turned_cos, sin)
            side_ref[pl.ds(BLOCK + t, HALF, stride=SIDE), :] = jnp.where(low, sin, -turned_cos)
            side_ref[pl.ds(BLOCK + t + 1, HALF, stride=SIDE), :] = jnp.where(low, turned_sin, -cos)
        for k in range(HALF):
            if k:
                left = side_ref[pl.ds(k * SIDE, 2 * BLOCK), :]
            else:
                edge = side_ref[pl.ds(0, BLOCK), :]
                left = jnp.concatenate([jnp.where(low_edge, edge, 0.0), jnp.where(low_edge, 0.0, edge)], axis=0)
            cross_ref[pl.ds(k * SIDE, 2 * BLOCK), :] = jnp.dot(
                left.astype(BF16), pat_ref[k], preferred_element_type=F32
            )
        rows = []
        for t in range(0, len(chunk) * PER_DEVICE, 2):
            cross = [
                jnp.concatenate(
                    [cross_ref[pl.ds(u, HALF, stride=SIDE), :], cross_ref[pl.ds(BLOCK + u, HALF, stride=SIDE), :]], axis=0
                ).astype(BF16)
                for u in (t, t + 1)
            ]
            shifted = jnp.dot(inv_ref[...], jnp.concatenate(cross, axis=1), preferred_element_type=F32)
            top = jnp.max(shifted, axis=0, keepdims=True)
            rows += [top[:, :LANES], top[:, LANES:]]
        for number, (_, _, mask) in enumerate(chunk):
            for e in range(PER_DEVICE):
                row = rows[number * PER_DEVICE + e]
                where = (index ^ mask) * PER_DEVICE + e
                corr_ref[pl.ds(where, 1), :] = row[:, :count]
                group = orient_ref[where]
                best_ref[pl.ds(group, 1), :] = jnp.maximum(best_ref[pl.ds(group, 1), :], row)
    best = best_ref[...]
    smooth = 0.25 * (pltpu.roll(best, 1, 1) + 2.0 * best + pltpu.roll(best, LANES - 1, 1))
    smooth_ref[...] = smooth[:, :count]


VMEM = pl.BlockSpec(memory_space=pltpu.VMEM)
SMEM = pl.BlockSpec(memory_space=pltpu.SMEM)
HBM = pl.BlockSpec(memory_space=pltpu.HBM)


def arrange(patterns, templates, table):
    count = patterns.shape[0]
    args = (patterns, templates, table)
    return pl.pallas_call(
        arrange_kernel,
        out_shape=(
            jax.ShapeDtypeStruct((RADII, count, ANGLES), BF16),
            jax.ShapeDtypeStruct(templates.shape, BF16),
            jax.ShapeDtypeStruct(table.shape, BF16),
        ),
        in_specs=[HBM] * 3,
        out_specs=(VMEM,) * 3,
        scratch_shapes=[
            pltpu.VMEM(patterns.shape, BF16),
            pltpu.VMEM((2, 2, RADII * (ROWS + 8), LANES), F32),
            pltpu.SemaphoreType.DMA((count // ROWS,)),
            pltpu.SemaphoreType.DMA((2,)),
        ],
        compiler_params=pltpu.CompilerParams(vmem_limit_bytes=16 << 20),
        name="arrange",
    )(*(pltpu.with_memory_space_constraint(x, pltpu.HBM) for x in args))


def pattern_spectra(bins, gains, rows, inner, outer, table):
    spare = LANES - rows.shape[1]
    return pl.pallas_call(
        pattern_kernel,
        out_shape=jax.ShapeDtypeStruct((HALF, LANES, LANES), BF16),
        in_specs=[SMEM] * 2 + [VMEM] * 4,
        out_specs=VMEM,
        scratch_shapes=[
            pltpu.VMEM((2, RADII * (spare + 8), LANES), F32),
            pltpu.VMEM((RADII, LANES), F32),
            pltpu.VMEM((HALF * PITCH, LANES), F32),
        ],
        compiler_params=pltpu.CompilerParams(vmem_limit_bytes=16 << 20),
        name="pattern_spectra",
    )(bins, gains, rows, inner, outer, table)


def match(orientation, pat_spec, table, inverse, parts, held, count, groups):
    total = orientation.shape[0]
    return pl.pallas_call(
        functools.partial(match_kernel, held=held),
        out_shape=(jax.ShapeDtypeStruct((total, count), F32), jax.ShapeDtypeStruct((groups, count), F32)),
        in_specs=[SMEM] + [VMEM] * (3 + len(parts)),
        out_specs=(VMEM, VMEM),
        scratch_shapes=[
            pltpu.VMEM((HALF * SIDE, LANES), F32),
            pltpu.VMEM((HALF * SIDE, LANES), F32),
            pltpu.VMEM((groups, LANES), F32),
        ],
        compiler_params=pltpu.CompilerParams(vmem_limit_bytes=24 << 20),
        name="match",
    )(orientation, pat_spec, table, inverse, *parts)


def swap_edges(patterns, size):
    even = lax.axis_index("scan") % 2 == 0
    leading, last = patterns[:1], patterns[patterns.shape[0] - 1 :]
    inner, outer = jnp.where(even, last, leading), jnp.where(even, leading, last)
    inner = lax.ppermute(inner, "scan", [(i, i ^ 1) for i in range(size)])
    pairs = [(i, i + 1) for i in range(1, size - 1, 2)]
    outer = lax.ppermute(outer, "scan", pairs + [(j, i) for i, j in pairs])
    return inner, outer


def on_device(patterns, templates, radius_bin, radial_gain, orientation):
    table, inverse = make_tables()
    table, inverse = jnp.asarray(table), jnp.asarray(inverse)
    count = patterns.shape[0]
    size = lax.axis_size("scan")
    groups = templates.shape[0] * size // TMPL_PER_GROUP
    bits = [1 << b for b in reversed(range(size.bit_length() - 1))]
    far, near, middle, core = bits[0], bits[1], bits[2:-1], bits[-1]

    def send(part, mask):
        return lax.ppermute(part, "scan", [(i, i ^ mask) for i in range(size)])

    masks = [0, far, far ^ near, near]
    came = [send(templates, mask) for mask in masks[1:]]
    inner, outer = swap_edges(patterns, size)
    rows, own, table = arrange(patterns, templates, table)
    came, rows, own, table, inner, outer = lax.optimization_barrier((came, rows, own, table, inner, outer))
    part = lax.optimization_barrier(jnp.concatenate([own] + came, axis=0))
    parts, held = [part], [masks]
    for mask in middle:
        if mask != middle[0]:
            parts, held = [jnp.concatenate(parts, axis=0)], [held[0] + held[1]]
        parts, held = parts + [send(parts[0], mask)], held + [[m ^ mask for m in held[0]]]
    pat_spec = pattern_spectra(radius_bin, radial_gain, rows, inner, outer, table)
    crossed = send(parts[0], core)
    last, pat_spec = lax.optimization_barrier((parts[-1], pat_spec))
    parts = [parts[0], last, crossed, send(last, core)]
    held = held + [[m ^ core for m in masks] for masks in held]
    corr, smooth = match(orientation.reshape(-1), pat_spec, table, inverse, parts, held, count, groups)
    return corr.T, smooth.T


def solution(mesh):
    placed = (P(("grp", "scan"), None, None), P("scan", None, None), P(), P(), P())
    return jax.shard_map(
        on_device,
        mesh=mesh,
        in_specs=placed,
        out_specs=(P(("grp", "scan"), None), P(("grp", "scan"), None)),
        check_vma=False,
    )
```

time: 38.4 us -> 27.6 us (0.72)
  local copies, waits for them, and re-layouts: 7.3 us -> 0.02 us
  waiting for transfers between devices: 7.91 us -> 3.6 us
  other arithmetic: 0 us -> 0.82 us
    unnamed x18 -> x8, local copies, waits for them, and re-layouts: 5.44 us -> 0.02 us
    ppermute x6 -> x8, waiting for transfers between devices: 7.91 us -> 3.6 us  [the longest x6 3.6 us: send(): return lax.ppermute(part, 'scan', [(i, i ^ mask) for i in range(size)])]
    dynamic_update_slice x8 -> x0, local copies, waits for them, and re-layouts: 1.07 us -> none  [the longest x4 1 us: on_device(): lax.dynamic_update_slice(jnp.zeros((2 * length,) + gathered.shape[1:], BF...]
    select_n x0 -> x1, other arithmetic: none -> 0.78 us  [swap_edges(): jnp.where(even, leading, last)]
    slice x1 -> x0, local copies, waits for them, and re-layouts: 0.78 us -> none  [on_device(): after = lax.ppermute(patterns[:1], 'scan', down)]
    ppermute x6 -> x8, starting transfers between devices: 11.1 us -> 10.9 us  [the longest x6 10.1 us: send(): return lax.ppermute(part, 'scan', [(i, i ^ mask) for i in range(size)])]
  transfers between devices with their start and end apart: 6 -> 8, of which waited for: 3 -> 4; matrix products, arithmetic and copies ran while one was open for 5% -> 3% of each run, Pallas kernels for 16% -> 24%
where the time goes in v3:
time: 27.6 us; the launch traced here: 27.3 us
  Pallas kernels  11.2 us (41%)
  starting transfers between devices  10.9 us (39%)
  waiting for transfers between devices  3.6 us (13%)
  other arithmetic  0.82 us (3%)
  between operations  0.73 us (3%)
    ppermute x6, starting transfers between devices, send(): return lax.ppermute(part, 'scan', [(i, i ^ mask) for i in range(size)])  10.1 us
    pallas_call x1, Pallas kernels, match(): pl.pallas_call(functools.partial(match_kernel, held=held), out_shape=(jax...  4.58 us
    ppermute x6, waiting for transfers between devices, send(): return lax.ppermute(part, 'scan', [(i, i ^ mask) for i in range(size)])  3.6 us
    pallas_call x1, Pallas kernels, pattern_spectra(): pl.pallas_call(pattern_kernel, out_shape=jax.ShapeDtypeStruct((HALF, LANE...  3.57 us
    pallas_call x1, Pallas kernels, arrange(): pl.pallas_call(arrange_kernel, out_shape=(jax.ShapeDtypeStruct((RADII, co...  3.08 us
    select_n x1, other arithmetic, swap_edges(): jnp.where(even, leading, last)  0.78 us
    ppermute x1, starting transfers between devices, swap_edges(): outer = lax.ppermute(outer, 'scan', pairs + [(j, i) for i, j in pairs])  0.66 us
  transfers between devices with their start and end apart: 8, of which 4 were waited for; matrix products, arithmetic and copies ran while one was open for 3% of the time, Pallas kernels for 24%

profile of v3, /device:TPU:0, one launch (start us, length us, event | category | flops | bytes accessed | tf_op | source)
XLA Modules:
  0.0 27.3 jit_solution(14631821748386179526)
XLA Ops:
  0.6 0.0 copy-start.2
  0.6 0.0 copy-start.1
  0.6 4.1 %collective-permute-start = (bf16[2,64,256]{2,1,0:T(8,128)(2,1)}, bf16[2,64,256]{2,1,0:T(8,128)(2,1)S(1)}, u32[]{:S(2)}, u32[]{:S(2)}) collective-permute-start(bf16[2,64,256]{2,1,0:T(8,128)(2,1)} %tmpl_hbm.1), channel_id=1, source_target_pairs={{0,8},{1,9},{2,10},{3,11},{4,12},{5,13},{6,14},{7,15},{8,0},{9,1},... | collective-permute-start | bytes 196616 | tf_op jit(solution)/shard_map/ppermute | solution.py:234
  4.8 1.3 %collective-permute-start.1 = (bf16[2,64,256]{2,1,0:T(8,128)(2,1)}, bf16[2,64,256]{2,1,0:T(8,128)(2,1)S(1)}, u32[]{:S(2)}, u32[]{:S(2)}) collective-permute-start(bf16[2,64,256]{2,1,0:T(8,128)(2,1)} %tmpl_hbm.1), channel_id=1, source_target_pairs={{0,12},{1,13},{2,14},{3,15},{4,8},{5,9},{6,10},{7,11},{8,4},{9,5},... | collective-permute-start | bytes 196616 | tf_op jit(solution)/shard_map/ppermute | solution.py:234
  6.1 0.2 collective-permute-start.2
  6.3 0.8 %broadcast_select_fusion = (bf16[1,64,256]{2,1,0:T(8,128)(2,1)S(1)}, bf16[1,64,256]{2,1,0:T(8,128)(2,1)S(1)}) fusion(pred[]{:T(512)S(6)} %eq.5, bf16[96,64,256]{2,1,0:T(8,128)(2,1)} %pat_hbm.1), kind=kLoop, calls=%fused_computation.1 | loop fusion | flops 32768 | bytes 131073 | tf_op jit(solution)/shard_map/jit(_where)/select_n | solution.py:217
  7.1 0.1 collective-permute-start.3
  7.2 0.7 %collective-permute-start.4 = (bf16[1,64,256]{2,1,0:T(8,128)(2,1)S(1)}, bf16[1,64,256]{2,1,0:T(8,128)(2,1)S(1)}, u32[]{:S(2)}, u32[]{:S(2)}) collective-permute-start(bf16[1,64,256]{2,1,0:T(8,128)(2,1)S(1)} %get-tuple-element.32), channel_id=1, source_target_pairs={{1,2},{3,4},{5,6},{7,8},{9,10},{11,12},{13,14},{2,1},{4,3},{6,5},{... | collective-permute-start | bytes 98312 | tf_op jit(solution)/shard_map/ppermute | solution.py:220
  7.9 3.1 %arrange.1 = (bf16[64,96,256]{2,1,0:T(8,128)(2,1)S(1)}, bf16[2,64,256]{2,1,0:T(8,128)(2,1)S(1)}, bf16[256,256]{1,0:T(8,128)(2,1)S(1)}) custom-call(bf16[96,64,256]{2,1,0:T(8,128)(2,1)} %pat_hbm.1, bf16[2,64,256]{2,1,0:T(8,128)(2,1)} %tmpl_hbm.1, bf16[256,256]{1,0:T(8,128)(2,1)} %constant.22.clone.table_hbm), custom_call_target="tpu_custom_call" | custom-call | tf_op jit(solution)/shard_map/arrange/pallas_call | solution.py:160
  10.9 0.0 collective-permute-done.3.inner_ref
  11.0 0.0 collective-permute-done.4.outer_ref
  11.0 0.0 collective-permute-done
  11.0 0.2 collective-permute-done.1
  11.2 0.1 collective-permute-done.2
  11.3 0.0 copy-start
  11.3 0.0 copy-start.3
  11.3 3.2 %collective-permute-start.5 = (bf16[8,64,256]{2,1,0:T(8,128)(2,1)S(1)}, bf16[8,64,256]{2,1,0:T(8,128)(2,1)S(1)}, u32[]{:S(2)}, u32[]{:S(2)}) collective-permute-start(bf16[8,64,256]{2,1,0:T(8,128)(2,1)S(1)} %pad_maximum_fusion.refs_0_), channel_id=1, source_target_pairs={{0,2},{1,3},{2,0},{3,1},{4,6},{5,7},{6,4},{7,5},{8,10},{9,11},{10,... | collective-permute-start | bytes 786440 | tf_op jit(solution)/shard_map/ppermute | solution.py:234
  14.5 1.0 %collective-permute-start.6 = (bf16[8,64,256]{2,1,0:T(8,128)(2,1)S(1)}, bf16[8,64,256]{2,1,0:T(8,128)(2,1)S(1)}, u32[]{:S(2)}, u32[]{:S(2)}) collective-permute-start(bf16[8,64,256]{2,1,0:T(8,128)(2,1)S(1)} %pad_maximum_fusion.refs_0_), channel_id=1, source_target_pairs={{0,1},{1,0},{2,3},{3,2},{4,5},{5,4},{6,7},{7,6},{8,9},{9,8},{10,11... | collective-permute-start | bytes 786440 | tf_op jit(solution)/shard_map/ppermute | solution.py:234
  15.5 0.0 copy-done.2
  15.5 0.0 copy-done.1
  15.5 3.6 %pattern_spectra.1.pat_ref = bf16[128,128,128]{2,1,0:T(8,128)(2,1)S(1)} custom-call(s32[64]{0:T(128)S(1)} %copy-done.1, f32[8]{0:T(128)S(1)} %copy-done.2, bf16[64,96,256]{2,1,0:T(8,128)(2,1)S(1)} %get-tuple-element.24.rows_ref, bf16[1,64,256]{2,1,0:T(8,128)(2,1)S(1)} %collective-permute-done.3.inner_ref, ...), custom_call_target="tpu_custom_call" | custom-call | tf_op jit(solution)/shard_map/pattern_spectra/pallas_call | solution.py:182
  19.1 2.1 %collective-permute-done.5.refs_1_ = bf16[8,64,256]{2,1,0:T(8,128)(2,1)S(1)} collective-permute-done((bf16[8,64,256]{2,1,0:T(8,128)(2,1)S(1)}, bf16[8,64,256]{2,1,0:T(8,128)(2,1)S(1)}, u32[]{:S(2)}, u32[]{:S(2)}) %collective-permute-start.5) | collective-permute-done | bytes 262176 | tf_op jit(solution)/shard_map/ppermute | solution.py:234
  21.1 0.3 %collective-permute-start.7 = (bf16[8,64,256]{2,1,0:T(8,128)(2,1)S(1)}, bf16[8,64,256]{2,1,0:T(8,128)(2,1)S(1)}, u32[]{:S(2)}, u32[]{:S(2)}) collective-permute-start(bf16[8,64,256]{2,1,0:T(8,128)(2,1)S(1)} %collective-permute-done.5.refs_1_), channel_id=1, source_target_pairs={{0,1},{1,0},{2,3},{3,2},{4,5},{5,4},{6,7},{7,6},{8,9},{9,8},{10,11... | collective-permute-start | bytes 786440 | tf_op jit(solution)/shard_map/ppermute | solution.py:234
  21.5 0.0 collective-permute-done.6.refs_2_
  21.5 1.2 %collective-permute-done.7.refs_3_ = bf16[8,64,256]{2,1,0:T(8,128)(2,1)S(1)} collective-permute-done((bf16[8,64,256]{2,1,0:T(8,128)(2,1)S(1)}, bf16[8,64,256]{2,1,0:T(8,128)(2,1)S(1)}, u32[]{:S(2)}, u32[]{:S(2)}) %collective-permute-start.7) | collective-permute-done | bytes 262176 | tf_op jit(solution)/shard_map/ppermute | solution.py:234
  22.7 0.0 copy-done
  22.7 0.0 copy-done.3
  22.7 4.6 %match.1 = (f32[32,96]{1,0:T(8,128)}, f32[16,96]{1,0:T(8,128)}) custom-call(s32[32]{0:T(128)S(1)} %bitcast.3, bf16[128,128,128]{2,1,0:T(8,128)(2,1)S(1)} %pattern_spectra.1.pat_ref, bf16[256,256]{1,0:T(8,128)(2,1)S(1)} %get-tuple-element.27.table_ref, bf16[256,256]{1,0:T(8,128)(2,1)S(1)} %copy-done, bf16[8,64,256]{2,1,0:T(8,128)(2,1)S(1)} %pad_maximum_fusion.refs_0_, ...), custom_call_target="tpu_custom_call" | custom-call | tf_op jit(solution)/shard_map/match/pallas_call | solution.py:199
  (1 shorter events, 0.0 us)
Async XLA Ops:
  0.6 14.8 %copy-start.2 = (f32[8]{0:T(128)S(1)}, f32[8]{0:T(128)}, u32[]{:S(2)}) copy-start(f32[8]{0:T(128)} %gain_ref.1) | copy-start | bytes 100
  0.6 14.8 %copy-start.1 = (s32[64]{0:T(128)S(1)}, s32[64]{0:T(128)}, u32[]{:S(2)}) copy-start(s32[64]{0:T(128)} %bin_ref.1) | copy-start | bytes 772
  0.6 10.3 %collective-permute-start = (bf16[2,64,256]{2,1,0:T(8,128)(2,1)}, bf16[2,64,256]{2,1,0:T(8,128)(2,1)S(1)}, u32[]{:S(2)}, u32[]{:S(2)}) collective-permute-start(bf16[2,64,256]{2,1,0:T(8,128)(2,1)} %tmpl_hbm.1), channel_id=1, source_target_pairs={{0,8},{1,9},{2,10},{3,11},{4,12},{5,13},{6,14},{7,15},{8,0},{9,1},... | collective-permute-start | bytes 196616 | tf_op jit(solution)/shard_map/ppermute | solution.py:234
  4.8 6.4 %collective-permute-start.1 = (bf16[2,64,256]{2,1,0:T(8,128)(2,1)}, bf16[2,64,256]{2,1,0:T(8,128)(2,1)S(1)}, u32[]{:S(2)}, u32[]{:S(2)}) collective-permute-start(bf16[2,64,256]{2,1,0:T(8,128)(2,1)} %tmpl_hbm.1), channel_id=1, source_target_pairs={{0,12},{1,13},{2,14},{3,15},{4,8},{5,9},{6,10},{7,11},{8,4},{9,5},... | collective-permute-start | bytes 196616 | tf_op jit(solution)/shard_map/ppermute | solution.py:234
  6.1 5.2 %collective-permute-start.2 = (bf16[2,64,256]{2,1,0:T(8,128)(2,1)}, bf16[2,64,256]{2,1,0:T(8,128)(2,1)S(1)}, u32[]{:S(2)}, u32[]{:S(2)}) collective-permute-start(bf16[2,64,256]{2,1,0:T(8,128)(2,1)} %tmpl_hbm.1), channel_id=1, source_target_pairs={{0,4},{1,5},{2,6},{3,7},{4,0},{5,1},{6,2},{7,3},{8,12},{9,13},{10,... | collective-permute-start | bytes 196616 | tf_op jit(solution)/shard_map/ppermute | solution.py:234
  7.1 3.8 %collective-permute-start.3 = (bf16[1,64,256]{2,1,0:T(8,128)(2,1)S(1)}, bf16[1,64,256]{2,1,0:T(8,128)(2,1)S(1)}, u32[]{:S(2)}, u32[]{:S(2)}) collective-permute-start(bf16[1,64,256]{2,1,0:T(8,128)(2,1)S(1)} %get-tuple-element.33), channel_id=1, source_target_pairs={{0,1},{1,0},{2,3},{3,2},{4,5},{5,4},{6,7},{7,6},{8,9},{9,8},{10,11... | collective-permute-start | bytes 98312 | tf_op jit(solution)/shard_map/ppermute | solution.py:218
  7.2 3.8 %collective-permute-start.4 = (bf16[1,64,256]{2,1,0:T(8,128)(2,1)S(1)}, bf16[1,64,256]{2,1,0:T(8,128)(2,1)S(1)}, u32[]{:S(2)}, u32[]{:S(2)}) collective-permute-start(bf16[1,64,256]{2,1,0:T(8,128)(2,1)S(1)} %get-tuple-element.32), channel_id=1, source_target_pairs={{1,2},{3,4},{5,6},{7,8},{9,10},{11,12},{13,14},{2,1},{4,3},{6,5},{... | collective-permute-start | bytes 98312 | tf_op jit(solution)/shard_map/ppermute | solution.py:220
  11.3 11.4 %copy-start = (bf16[256,256]{1,0:T(8,128)(2,1)S(1)}, bf16[256,256]{1,0:T(8,128)(2,1)}, u32[]{:S(2)}) copy-start(bf16[256,256]{1,0:T(8,128)(2,1)} %constant.23.clone.inv_ref) | copy-start | bytes 393220
  11.3 11.4 %copy-start.3 = (s32[32,1]{0,1:T(1,128)S(1)}, s32[32,1]{0,1:T(1,128)}, u32[]{:S(2)}) copy-start(s32[32,1]{0,1:T(1,128)} %param.11) | copy-start | bytes 388
  11.3 9.8 %collective-permute-start.5 = (bf16[8,64,256]{2,1,0:T(8,128)(2,1)S(1)}, bf16[8,64,256]{2,1,0:T(8,128)(2,1)S(1)}, u32[]{:S(2)}, u32[]{:S(2)}) collective-permute-start(bf16[8,64,256]{2,1,0:T(8,128)(2,1)S(1)} %pad_maximum_fusion.refs_0_), channel_id=1, source_target_pairs={{0,2},{1,3},{2,0},{3,1},{4,6},{5,7},{6,4},{7,5},{8,10},{9,11},{10,... | collective-permute-start | bytes 786440 | tf_op jit(solution)/shard_map/ppermute | solution.py:234
  14.5 7.0 %collective-permute-start.6 = (bf16[8,64,256]{2,1,0:T(8,128)(2,1)S(1)}, bf16[8,64,256]{2,1,0:T(8,128)(2,1)S(1)}, u32[]{:S(2)}, u32[]{:S(2)}) collective-permute-start(bf16[8,64,256]{2,1,0:T(8,128)(2,1)S(1)} %pad_maximum_fusion.refs_0_), channel_id=1, source_target_pairs={{0,1},{1,0},{2,3},{3,2},{4,5},{5,4},{6,7},{7,6},{8,9},{9,8},{10,11... | collective-permute-start | bytes 786440 | tf_op jit(solution)/shard_map/ppermute | solution.py:234
  21.1 1.5 %collective-permute-start.7 = (bf16[8,64,256]{2,1,0:T(8,128)(2,1)S(1)}, bf16[8,64,256]{2,1,0:T(8,128)(2,1)S(1)}, u32[]{:S(2)}, u32[]{:S(2)}) collective-permute-start(bf16[8,64,256]{2,1,0:T(8,128)(2,1)S(1)} %collective-permute-done.5.refs_1_), channel_id=1, source_target_pairs={{0,1},{1,0},{2,3},{3,2},{4,5},{5,4},{6,7},{7,6},{8,9},{9,8},{10,11... | collective-permute-start | bytes 786440 | tf_op jit(solution)/shard_map/ppermute | solution.py:234

commit v4 on v3

--- a/solution.py
+++ b/solution.py
@@ -15,7 +15,7 @@
 GAINS = 8
 TMPL_PER_GROUP = 2
 LANES = 128
-BLOCK = 32
+BLOCK = 16
 ROWS = 16
 PER_DEVICE = 2
 F32 = jnp.float32
@@ -84,39 +84,52 @@
         edge_ref[1, pl.ds(at, RADII, stride=pitch), :] = wide[:, LANES:]
     for r in range(RADII):
         weight_ref[pl.ds(r, 1), :] = jnp.full((1, LANES), gain_ref[bin_ref[r]], F32)
-    for r in range(RADII):
-        at = pl.ds(r * pitch, spare)
-        edge = jnp.concatenate([edge_ref[0, at, :], edge_ref[1, at, :]], axis=1).astype(BF16)
-        rows = jnp.concatenate([rows_ref[r], edge], axis=0)
-        spec = lax.dot_general(table_ref[...], rows, CONTRACT_LAST, preferred_element_type=F32)
-        spec = spec * weight_ref[pl.ds(r, 1), :]
-        spec_ref[pl.ds(r, HALF, stride=PITCH), :] = spec[:HALF]
-        spec_ref[pl.ds(RADII + r, HALF, stride=PITCH), :] = spec[HALF:]
+    for r in range(0, RADII, 2):
+        rows = []
+        for u in (r, r + 1):
+            at = pl.ds(u * pitch, spare)
+            rows += [rows_ref[u], jnp.concatenate([edge_ref[0, at, :], edge_ref[1, at, :]], axis=1).astype(BF16)]
+        spec = lax.dot_general(
+            table_ref[...], jnp.concatenate(rows, axis=0), CONTRACT_LAST, preferred_element_type=F32
+        )
+        for u in (r, r + 1):
+            one = spec[:, (u - r) * LANES : (u - r + 1) * LANES] * weight_ref[pl.ds(u, 1), :]
+            spec_ref[pl.ds(u, HALF, stride=PITCH), :] = one[:HALF]
+            spec_ref[pl.ds(RADII + u, HALF, stride=PITCH), :] = one[HALF:]
     for k in range(HALF):
         out_ref[k] = spec_ref[pl.ds(k * PITCH, LANES), :].astype(BF16)
 
 
-def match_kernel(orient_ref, pat_ref, table_ref, inv_ref, *refs, held):
-    parts = refs[: len(held)]
-    corr_ref, smooth_ref, side_ref, cross_ref, best_ref = refs[len(held) :]
+def match_kernel(orient_ref, pat_ref, table_ref, inv_ref, *refs, held, more):
+    parts, refs = refs[: len(held)], refs[len(held) :]
+    if more:
+        corr_ref, best_ref, side_ref, cross_ref = refs
+        best_ref[...] = jnp.full(best_ref.shape, -jnp.inf, F32)
+    else:
+        corr_in, best_in, corr_ref, smooth_ref, side_ref, cross_ref, best_ref = refs
+        corr_ref[...] = corr_in[...]
+        best_ref[...] = best_in[...]
     count = corr_ref.shape[1]
     index = lax.axis_index("scan")
     blocks = [(part, i, mask) for part, masks in zip(parts, held) for i, mask in enumerate(masks)]
-    best_ref[...] = jnp.full(best_ref.shape, -jnp.inf, F32)
     low = lax.broadcasted_iota(jnp.int32, (HALF, LANES), 1) < RADII
     low_edge = lax.broadcasted_iota(jnp.int32, (BLOCK, LANES), 1) < RADII
     for begin in range(0, len(blocks), BLOCK // PER_DEVICE):
         chunk = blocks[begin : begin + BLOCK // PER_DEVICE]
-        for number, (part, i, _) in enumerate(chunk):
-            t = number * PER_DEVICE
-            pair = part[pl.ds(i * PER_DEVICE, PER_DEVICE)].reshape(PER_DEVICE * RADII, ANGLES)
-            spec = lax.dot_general(table_ref[...], pair, CONTRACT_LAST, preferred_element_type=F32)
-            cos, sin = spec[:HALF], spec[HALF:]
-            turned_cos, turned_sin = pltpu.roll(cos, RADII, 1), pltpu.roll(sin, RADII, 1)
-            side_ref[pl.ds(t, HALF, stride=SIDE), :] = jnp.where(low, cos, turned_sin)
-            side_ref[pl.ds(t + 1, HALF, stride=SIDE), :] = jnp.where(low, turned_cos, sin)
-            side_ref[pl.ds(BLOCK + t, HALF, stride=SIDE), :] = jnp.where(low, sin, -turned_cos)
-            side_ref[pl.ds(BLOCK + t + 1, HALF, stride=SIDE), :] = jnp.where(low, turned_sin, -cos)
+        for number in range(0, len(chunk), 2):
+            (part, i, _), (other, j, _) = chunk[number : number + 2]
+            raw = jnp.concatenate([part[pl.ds(i * PER_DEVICE, PER_DEVICE)], other[pl.ds(j * PER_DEVICE, PER_DEVICE)]])
+            raw = raw.reshape(2 * PER_DEVICE * RADII, ANGLES)
+            both = lax.dot_general(table_ref[...], raw, CONTRACT_LAST, preferred_element_type=F32)
+            for u in (0, 1):
+                t = (number + u) * PER_DEVICE
+                spec = both[:, u * LANES : (u + 1) * LANES]
+                cos, sin = spec[:HALF], spec[HALF:]
+                turned_cos, turned_sin = pltpu.roll(cos, RADII, 1), pltpu.roll(sin, RADII, 1)
+                side_ref[pl.ds(t, HALF, stride=SIDE), :] = jnp.where(low, cos, turned_sin)
+                side_ref[pl.ds(t + 1, HALF, stride=SIDE), :] = jnp.where(low, turned_cos, sin)
+                side_ref[pl.ds(BLOCK + t, HALF, stride=SIDE), :] = jnp.where(low, sin, -turned_cos)
+                side_ref[pl.ds(BLOCK + t + 1, HALF, stride=SIDE), :] = jnp.where(low, turned_sin, -cos)
         for k in range(HALF):
             if k:
                 left = side_ref[pl.ds(k * SIDE, 2 * BLOCK), :]
@@ -144,6 +157,8 @@
                 corr_ref[pl.ds(where, 1), :] = row[:, :count]
                 group = orient_ref[where]
                 best_ref[pl.ds(group, 1), :] = jnp.maximum(best_ref[pl.ds(group, 1), :], row)
+    if more:
+        return
     best = best_ref[...]
     smooth = 0.25 * (pltpu.roll(best, 1, 1) + 2.0 * best + pltpu.roll(best, LANES - 1, 1))
     smooth_ref[...] = smooth[:, :count]
@@ -194,31 +209,20 @@
     )(bins, gains, rows, inner, outer, table)
 
 
-def match(orientation, pat_spec, table, inverse, parts, held, count, groups):
-    total = orientation.shape[0]
+def match(orientation, pat_spec, table, inverse, parts, held, carry, count, groups):
+    corr = jax.ShapeDtypeStruct((orientation.shape[0], count), F32)
+    best = pltpu.VMEM((groups, LANES), F32)
+    scratch = [pltpu.VMEM((HALF * SIDE, LANES), F32), pltpu.VMEM((HALF * SIDE, LANES), F32)]
+    second = jax.ShapeDtypeStruct((groups, count if carry else LANES), F32)
     return pl.pallas_call(
-        functools.partial(match_kernel, held=held),
-        out_shape=(jax.ShapeDtypeStruct((total, count), F32), jax.ShapeDtypeStruct((groups, count), F32)),
-        in_specs=[SMEM] + [VMEM] * (3 + len(parts)),
+        functools.partial(match_kernel, held=held, more=not carry),
+        out_shape=(corr, second),
+        in_specs=[SMEM] + [VMEM] * (3 + len(parts) + len(carry)),
         out_specs=(VMEM, VMEM),
-        scratch_shapes=[
-            pltpu.VMEM((HALF * SIDE, LANES), F32),
-            pltpu.VMEM((HALF * SIDE, LANES), F32),
-            pltpu.VMEM((groups, LANES), F32),
-        ],
-        compiler_params=pltpu.CompilerParams(vmem_limit_bytes=24 << 20),
+        scratch_shapes=scratch + [best] * bool(carry),
+        compiler_params=pltpu.CompilerParams(vmem_limit_bytes=16 << 20),
         name="match",
-    )(orientation, pat_spec, table, inverse, *parts)
-
-
-def swap_edges(patterns, size):
-    even = lax.axis_index("scan") % 2 == 0
-    leading, last = patterns[:1], patterns[patterns.shape[0] - 1 :]
-    inner, outer = jnp.where(even, last, leading), jnp.where(even, leading, last)
-    inner = lax.ppermute(inner, "scan", [(i, i ^ 1) for i in range(size)])
-    pairs = [(i, i + 1) for i in range(1, size - 1, 2)]
-    outer = lax.ppermute(outer, "scan", pairs + [(j, i) for i, j in pairs])
-    return inner, outer
+    )(orientation, pat_spec, table, inverse, *parts, *carry)
 
 
 def on_device(patterns, templates, radius_bin, radial_gain, orientation):
@@ -227,6 +231,7 @@
     count = patterns.shape[0]
     size = lax.axis_size("scan")
     groups = templates.shape[0] * size // TMPL_PER_GROUP
+    orientation = orientation.reshape(-1)
     bits = [1 << b for b in reversed(range(size.bit_length() - 1))]
     far, near, middle, core = bits[0], bits[1], bits[2:-1], bits[-1]
 
@@ -235,7 +240,12 @@
 
     masks = [0, far, far ^ near, near]
     came = [send(templates, mask) for mask in masks[1:]]
-    inner, outer = swap_edges(patterns, size)
+    even = lax.axis_index("scan") % 2 == 0
+    leading, last = patterns[:1], patterns[count - 1 :]
+    inner, outer = jnp.where(even, last, leading), jnp.where(even, leading, last)
+    pairs = [(i, i + 1) for i in range(1, size - 1, 2)]
+    inner = send(inner, 1)
+    outer = lax.ppermute(outer, "scan", pairs + [(j, i) for i, j in pairs])
     rows, own, table = arrange(patterns, templates, table)
     came, rows, own, table, inner, outer = lax.optimization_barrier((came, rows, own, table, inner, outer))
     part = lax.optimization_barrier(jnp.concatenate([own] + came, axis=0))
@@ -245,11 +255,12 @@
             parts, held = [jnp.concatenate(parts, axis=0)], [held[0] + held[1]]
         parts, held = parts + [send(parts[0], mask)], held + [[m ^ mask for m in held[0]]]
     pat_spec = pattern_spectra(radius_bin, radial_gain, rows, inner, outer, table)
-    crossed = send(parts[0], core)
-    last, pat_spec = lax.optimization_barrier((parts[-1], pat_spec))
-    parts = [parts[0], last, crossed, send(last, core)]
-    held = held + [[m ^ core for m in masks] for masks in held]
-    corr, smooth = match(orientation.reshape(-1), pat_spec, table, inverse, parts, held, count, groups)
+    crossed = [[m ^ core for m in masks] for masks in held]
+    early = [parts[0], send(parts[0], core)]
+    carry = match(orientation, pat_spec, table, inverse, early, [held[0], crossed[0]], [], count, groups)
+    last, pat_spec, carry = lax.optimization_barrier((parts[1], pat_spec, carry))
+    late = [last, send(last, core)]
+    corr, smooth = match(orientation, pat_spec, table, inverse, late, [held[1], crossed[1]], carry, count, groups)
     return corr.T, smooth.T
 
 

time: 27.6 us -> 27.5 us (level)
  Pallas kernels: 11.2 us -> 12.3 us
  waiting for transfers between devices: 3.6 us -> 2.62 us
    pallas_call x1 -> x2, Pallas kernels: 4.58 us -> 6.27 us  [match(): pl.pallas_call(functools.partial(match_kernel, held=held, more=not carry)...]
    ppermute x6 -> x7, waiting for transfers between devices: 3.6 us -> 2.61 us  [send(): return lax.ppermute(part, 'scan', [(i, i ^ mask) for i in range(size)])]
    pallas_call x1, Pallas kernels: 3.57 us -> 2.93 us  [pattern_spectra(): pl.pallas_call(pattern_kernel, out_shape=jax.ShapeDtypeStruct((HALF, LANE...]
    ppermute x2 -> x1, starting transfers between devices: 0.73 us -> 0.66 us  [on_device(): outer = lax.ppermute(outer, 'scan', pairs + [(j, i) for i, j in pairs])]
    ppermute x6 -> x7, starting transfers between devices: 10.1 us -> 10.2 us  [send(): return lax.ppermute(part, 'scan', [(i, i ^ mask) for i in range(size)])]
  transfers between devices with their start and end apart: 8 -> 8, of which waited for: 4 -> 4; matrix products, arithmetic and copies ran while one was open for 3% -> 3% of each run, Pallas kernels for 24% -> 32%
where the time goes in v4:
time: 27.5 us; the launch traced here: 27.3 us
  Pallas kernels  12.3 us (45%)
  starting transfers between devices  10.8 us (39%)
  waiting for transfers between devices  2.62 us (10%)
  other arithmetic  0.82 us (3%)
  between operations  0.76 us (3%)
    ppermute x7, starting transfers between devices, send(): return lax.ppermute(part, 'scan', [(i, i ^ mask) for i in range(size)])  10.2 us
    pallas_call x2, Pallas kernels, match(): pl.pallas_call(functools.partial(match_kernel, held=held, more=not carry)...  6.27 us
    pallas_call x1, Pallas kernels, arrange(): pl.pallas_call(arrange_kernel, out_shape=(jax.ShapeDtypeStruct((RADII, co...  3.08 us
    pallas_call x1, Pallas kernels, pattern_spectra(): pl.pallas_call(pattern_kernel, out_shape=jax.ShapeDtypeStruct((HALF, LANE...  2.93 us
    ppermute x7, waiting for transfers between devices, send(): return lax.ppermute(part, 'scan', [(i, i ^ mask) for i in range(size)])  2.61 us
    select_n x1, other arithmetic, on_device(): jnp.where(even, leading, last)  0.78 us
    ppermute x1, starting transfers between devices, on_device(): outer = lax.ppermute(outer, 'scan', pairs + [(j, i) for i, j in pairs])  0.66 us
  transfers between devices with their start and end apart: 8, of which 4 were waited for; matrix products, arithmetic and copies ran while one was open for 3% of the time, Pallas kernels for 32%

profile of v4, /device:TPU:0, one launch (start us, length us, event | category | flops | bytes accessed | tf_op | source)
XLA Modules:
  0.0 27.3 jit_solution(4944344133197693355)
XLA Ops:
  0.6 0.0 copy-start.3
  0.6 0.0 copy-start.2
  0.6 4.1 %collective-permute-start = (bf16[2,64,256]{2,1,0:T(8,128)(2,1)}, bf16[2,64,256]{2,1,0:T(8,128)(2,1)S(1)}, u32[]{:S(2)}, u32[]{:S(2)}) collective-permute-start(bf16[2,64,256]{2,1,0:T(8,128)(2,1)} %tmpl_hbm.1), channel_id=1, source_target_pairs={{0,8},{1,9},{2,10},{3,11},{4,12},{5,13},{6,14},{7,15},{8,0},{9,1},... | collective-permute-start | bytes 196616 | tf_op jit(solution)/shard_map/ppermute | solution.py:239
  4.8 1.3 %collective-permute-start.1 = (bf16[2,64,256]{2,1,0:T(8,128)(2,1)}, bf16[2,64,256]{2,1,0:T(8,128)(2,1)S(1)}, u32[]{:S(2)}, u32[]{:S(2)}) collective-permute-start(bf16[2,64,256]{2,1,0:T(8,128)(2,1)} %tmpl_hbm.1), channel_id=1, source_target_pairs={{0,12},{1,13},{2,14},{3,15},{4,8},{5,9},{6,10},{7,11},{8,4},{9,5},... | collective-permute-start | bytes 196616 | tf_op jit(solution)/shard_map/ppermute | solution.py:239
  6.1 0.2 collective-permute-start.2
  6.3 0.8 %broadcast_select_fusion = (bf16[1,64,256]{2,1,0:T(8,128)(2,1)S(1)}, bf16[1,64,256]{2,1,0:T(8,128)(2,1)S(1)}) fusion(pred[]{:T(512)S(6)} %eq.5, bf16[96,64,256]{2,1,0:T(8,128)(2,1)} %pat_hbm.1), kind=kLoop, calls=%fused_computation.1 | loop fusion | flops 32768 | bytes 131073 | tf_op jit(solution)/shard_map/jit(_where)/select_n | solution.py:245
  7.1 0.1 collective-permute-start.3
  7.2 0.7 %collective-permute-start.4 = (bf16[1,64,256]{2,1,0:T(8,128)(2,1)S(1)}, bf16[1,64,256]{2,1,0:T(8,128)(2,1)S(1)}, u32[]{:S(2)}, u32[]{:S(2)}) collective-permute-start(bf16[1,64,256]{2,1,0:T(8,128)(2,1)S(1)} %get-tuple-element.40), channel_id=1, source_target_pairs={{1,2},{3,4},{5,6},{7,8},{9,10},{11,12},{13,14},{2,1},{4,3},{6,5},{... | collective-permute-start | bytes 98312 | tf_op jit(solution)/shard_map/ppermute | solution.py:248
  7.9 3.1 %arrange.1 = (bf16[64,96,256]{2,1,0:T(8,128)(2,1)S(1)}, bf16[2,64,256]{2,1,0:T(8,128)(2,1)S(1)}, bf16[256,256]{1,0:T(8,128)(2,1)S(1)}) custom-call(bf16[96,64,256]{2,1,0:T(8,128)(2,1)} %pat_hbm.1, bf16[2,64,256]{2,1,0:T(8,128)(2,1)} %tmpl_hbm.1, bf16[256,256]{1,0:T(8,128)(2,1)} %constant.22.clone.table_hbm), custom_call_target="tpu_custom_call" | custom-call | tf_op jit(solution)/shard_map/arrange/pallas_call | solution.py:175
  10.9 0.0 collective-permute-done.3.inner_ref
  11.0 0.0 collective-permute-done.4.outer_ref
  11.0 0.0 collective-permute-done
  11.0 0.2 collective-permute-done.1
  11.2 0.1 collective-permute-done.2
  11.3 0.0 copy-start
  11.3 0.0 copy-start.1
  11.3 2.7 %collective-permute-start.6 = (bf16[8,64,256]{2,1,0:T(8,128)(2,1)S(1)}, bf16[8,64,256]{2,1,0:T(8,128)(2,1)S(1)}, u32[]{:S(2)}, u32[]{:S(2)}) collective-permute-start(bf16[8,64,256]{2,1,0:T(8,128)(2,1)S(1)} %pad_maximum_fusion.refs_0_), channel_id=1, source_target_pairs={{0,1},{1,0},{2,3},{3,2},{4,5},{5,4},{6,7},{7,6},{8,9},{9,8},{10,11... | collective-permute-start | bytes 786440 | tf_op jit(solution)/shard_map/ppermute | solution.py:239
  14.0 1.7 %collective-permute-start.5 = (bf16[8,64,256]{2,1,0:T(8,128)(2,1)S(1)}, bf16[8,64,256]{2,1,0:T(8,128)(2,1)S(1)}, u32[]{:S(2)}, u32[]{:S(2)}) collective-permute-start(bf16[8,64,256]{2,1,0:T(8,128)(2,1)S(1)} %pad_maximum_fusion.refs_0_), channel_id=1, source_target_pairs={{0,2},{1,3},{2,0},{3,1},{4,6},{5,7},{6,4},{7,5},{8,10},{9,11},{10,... | collective-permute-start | bytes 786440 | tf_op jit(solution)/shard_map/ppermute | solution.py:239
  15.8 0.0 copy-done.3
  15.8 0.0 copy-done.2
  15.8 2.9 %pattern_spectra.1.pat_ref = bf16[128,128,128]{2,1,0:T(8,128)(2,1)S(1)} custom-call(s32[64]{0:T(128)S(1)} %copy-done.2, f32[8]{0:T(128)S(1)} %copy-done.3, bf16[64,96,256]{2,1,0:T(8,128)(2,1)S(1)} %get-tuple-element.28.rows_ref, bf16[1,64,256]{2,1,0:T(8,128)(2,1)S(1)} %collective-permute-done.3.inner_ref, ...), custom_call_target="tpu_custom_call" | custom-call | tf_op jit(solution)/shard_map/pattern_spectra/pallas_call | solution.py:197
  18.7 0.0 collective-permute-done.6.refs_1_
  18.7 0.0 copy-done
  18.7 0.0 copy-done.1
  18.7 2.8 %match.2 = (f32[32,96]{1,0:T(8,128)S(1)}, f32[16,128]{1,0:T(8,128)S(1)}) custom-call(s32[32]{0:T(128)S(1)} %bitcast.3, bf16[128,128,128]{2,1,0:T(8,128)(2,1)S(1)} %pattern_spectra.1.pat_ref, bf16[256,256]{1,0:T(8,128)(2,1)S(1)} %get-tuple-element.31.table_ref, bf16[256,256]{1,0:T(8,128)(2,1)S(1)} %copy-done, ...), custom_call_target="tpu_custom_call" | custom-call | tf_op jit(solution)/shard_map/match/pallas_call | solution.py:217
  21.5 0.8 %collective-permute-done.5.refs_0_ = bf16[8,64,256]{2,1,0:T(8,128)(2,1)S(1)} collective-permute-done((bf16[8,64,256]{2,1,0:T(8,128)(2,1)S(1)}, bf16[8,64,256]{2,1,0:T(8,128)(2,1)S(1)}, u32[]{:S(2)}, u32[]{:S(2)}) %collective-permute-start.5) | collective-permute-done | bytes 262176 | tf_op jit(solution)/shard_map/ppermute | solution.py:239
  22.3 0.0 collective-permute-start.7
  22.3 1.5 %collective-permute-done.7.refs_1_ = bf16[8,64,256]{2,1,0:T(8,128)(2,1)S(1)} collective-permute-done((bf16[8,64,256]{2,1,0:T(8,128)(2,1)S(1)}, bf16[8,64,256]{2,1,0:T(8,128)(2,1)S(1)}, u32[]{:S(2)}, u32[]{:S(2)}) %collective-permute-start.7) | collective-permute-done | bytes 262176 | tf_op jit(solution)/shard_map/ppermute | solution.py:239
  23.8 3.5 %match.3 = (f32[32,96]{1,0:T(8,128)}, f32[16,96]{1,0:T(8,128)}) custom-call(s32[32]{0:T(128)S(1)} %bitcast.4, bf16[128,128,128]{2,1,0:T(8,128)(2,1)S(1)} %pattern_spectra.1.pat_ref, bf16[256,256]{1,0:T(8,128)(2,1)S(1)} %get-tuple-element.31.table_ref, bf16[256,256]{1,0:T(8,128)(2,1)S(1)} %copy-done, bf16[8,64,256]{2,1,0:T(8,128)(2,1)S(1)} %collective-permute-done.5.refs_0_, ...), custom_call_target="tpu_custom_call" | custom-call | tf_op jit(solution)/shard_map/match/pallas_call | solution.py:217
  (1 shorter events, 0.0 us)
Async XLA Ops:
  0.6 15.1 %copy-start.3 = (f32[8]{0:T(128)S(1)}, f32[8]{0:T(128)}, u32[]{:S(2)}) copy-start(f32[8]{0:T(128)} %gain_ref.1) | copy-start | bytes 100
  0.6 15.1 %copy-start.2 = (s32[64]{0:T(128)S(1)}, s32[64]{0:T(128)}, u32[]{:S(2)}) copy-start(s32[64]{0:T(128)} %bin_ref.1) | copy-start | bytes 772
  0.6 10.3 %collective-permute-start = (bf16[2,64,256]{2,1,0:T(8,128)(2,1)}, bf16[2,64,256]{2,1,0:T(8,128)(2,1)S(1)}, u32[]{:S(2)}, u32[]{:S(2)}) collective-permute-start(bf16[2,64,256]{2,1,0:T(8,128)(2,1)} %tmpl_hbm.1), channel_id=1, source_target_pairs={{0,8},{1,9},{2,10},{3,11},{4,12},{5,13},{6,14},{7,15},{8,0},{9,1},... | collective-permute-start | bytes 196616 | tf_op jit(solution)/shard_map/ppermute | solution.py:239
  4.8 6.4 %collective-permute-start.1 = (bf16[2,64,256]{2,1,0:T(8,128)(2,1)}, bf16[2,64,256]{2,1,0:T(8,128)(2,1)S(1)}, u32[]{:S(2)}, u32[]{:S(2)}) collective-permute-start(bf16[2,64,256]{2,1,0:T(8,128)(2,1)} %tmpl_hbm.1), channel_id=1, source_target_pairs={{0,12},{1,13},{2,14},{3,15},{4,8},{5,9},{6,10},{7,11},{8,4},{9,5},... | collective-permute-start | bytes 196616 | tf_op jit(solution)/shard_map/ppermute | solution.py:239
  6.1 5.2 %collective-permute-start.2 = (bf16[2,64,256]{2,1,0:T(8,128)(2,1)}, bf16[2,64,256]{2,1,0:T(8,128)(2,1)S(1)}, u32[]{:S(2)}, u32[]{:S(2)}) collective-permute-start(bf16[2,64,256]{2,1,0:T(8,128)(2,1)} %tmpl_hbm.1), channel_id=1, source_target_pairs={{0,4},{1,5},{2,6},{3,7},{4,0},{5,1},{6,2},{7,3},{8,12},{9,13},{10,... | collective-permute-start | bytes 196616 | tf_op jit(solution)/shard_map/ppermute | solution.py:239
  7.1 3.8 %collective-permute-start.3 = (bf16[1,64,256]{2,1,0:T(8,128)(2,1)S(1)}, bf16[1,64,256]{2,1,0:T(8,128)(2,1)S(1)}, u32[]{:S(2)}, u32[]{:S(2)}) collective-permute-start(bf16[1,64,256]{2,1,0:T(8,128)(2,1)S(1)} %get-tuple-element.41), channel_id=1, source_target_pairs={{0,1},{1,0},{2,3},{3,2},{4,5},{5,4},{6,7},{7,6},{8,9},{9,8},{10,11... | collective-permute-start | bytes 98312 | tf_op jit(solution)/shard_map/ppermute | solution.py:239
  7.2 3.8 %collective-permute-start.4 = (bf16[1,64,256]{2,1,0:T(8,128)(2,1)S(1)}, bf16[1,64,256]{2,1,0:T(8,128)(2,1)S(1)}, u32[]{:S(2)}, u32[]{:S(2)}) collective-permute-start(bf16[1,64,256]{2,1,0:T(8,128)(2,1)S(1)} %get-tuple-element.40), channel_id=1, source_target_pairs={{1,2},{3,4},{5,6},{7,8},{9,10},{11,12},{13,14},{2,1},{4,3},{6,5},{... | collective-permute-start | bytes 98312 | tf_op jit(solution)/shard_map/ppermute | solution.py:248
  11.3 7.4 %copy-start = (bf16[256,256]{1,0:T(8,128)(2,1)S(1)}, bf16[256,256]{1,0:T(8,128)(2,1)}, u32[]{:S(2)}) copy-start(bf16[256,256]{1,0:T(8,128)(2,1)} %constant.23.clone.inv_ref) | copy-start | bytes 393220
  11.3 7.4 %copy-start.1 = (s32[32,1]{0,1:T(1,128)S(1)}, s32[32,1]{0,1:T(1,128)}, u32[]{:S(2)}) copy-start(s32[32,1]{0,1:T(1,128)} %param.11) | copy-start | bytes 388
  11.3 7.4 %collective-permute-start.6 = (bf16[8,64,256]{2,1,0:T(8,128)(2,1)S(1)}, bf16[8,64,256]{2,1,0:T(8,128)(2,1)S(1)}, u32[]{:S(2)}, u32[]{:S(2)}) collective-permute-start(bf16[8,64,256]{2,1,0:T(8,128)(2,1)S(1)} %pad_maximum_fusion.refs_0_), channel_id=1, source_target_pairs={{0,1},{1,0},{2,3},{3,2},{4,5},{5,4},{6,7},{7,6},{8,9},{9,8},{10,11... | collective-permute-start | bytes 786440 | tf_op jit(solution)/shard_map/ppermute | solution.py:239
  14.0 8.3 %collective-permute-start.5 = (bf16[8,64,256]{2,1,0:T(8,128)(2,1)S(1)}, bf16[8,64,256]{2,1,0:T(8,128)(2,1)S(1)}, u32[]{:S(2)}, u32[]{:S(2)}) collective-permute-start(bf16[8,64,256]{2,1,0:T(8,128)(2,1)S(1)} %pad_maximum_fusion.refs_0_), channel_id=1, source_target_pairs={{0,2},{1,3},{2,0},{3,1},{4,6},{5,7},{6,4},{7,5},{8,10},{9,11},{10,... | collective-permute-start | bytes 786440 | tf_op jit(solution)/shard_map/ppermute | solution.py:239
  22.3 1.5 %collective-permute-start.7 = (bf16[8,64,256]{2,1,0:T(8,128)(2,1)S(1)}, bf16[8,64,256]{2,1,0:T(8,128)(2,1)S(1)}, u32[]{:S(2)}, u32[]{:S(2)}) collective-permute-start(bf16[8,64,256]{2,1,0:T(8,128)(2,1)S(1)} %collective-permute-done.5.refs_0_), channel_id=1, source_target_pairs={{0,1},{1,0},{2,3},{3,2},{4,5},{5,4},{6,7},{7,6},{8,9},{9,8},{10,11... | collective-permute-start | bytes 786440 | tf_op jit(solution)/shard_map/ppermute | solution.py:239

commit v5 on v4

--- a/solution.py
+++ b/solution.py
@@ -100,16 +100,13 @@
         out_ref[k] = spec_ref[pl.ds(k * PITCH, LANES), :].astype(BF16)
 
 
-def match_kernel(orient_ref, pat_ref, table_ref, inv_ref, *refs, held, more):
+def match_kernel(pat_ref, table_ref, inv_ref, *refs, held, final):
     parts, refs = refs[: len(held)], refs[len(held) :]
-    if more:
-        corr_ref, best_ref, side_ref, cross_ref = refs
-        best_ref[...] = jnp.full(best_ref.shape, -jnp.inf, F32)
+    if final:
+        orient_ref, rows_in, corr_ref, smooth_ref, side_ref, cross_ref, rows_ref = refs
+        rows_ref[...] = rows_in[...]
     else:
-        corr_in, best_in, corr_ref, smooth_ref, side_ref, cross_ref, best_ref = refs
-        corr_ref[...] = corr_in[...]
-        best_ref[...] = best_in[...]
-    count = corr_ref.shape[1]
+        rows_ref, side_ref, cross_ref = refs
     index = lax.axis_index("scan")
     blocks = [(part, i, mask) for part, masks in zip(parts, held) for i, mask in enumerate(masks)]
     low = lax.broadcasted_iota(jnp.int32, (HALF, LANES), 1) < RADII
@@ -130,15 +127,17 @@
                 side_ref[pl.ds(t + 1, HALF, stride=SIDE), :] = jnp.where(low, turned_cos, sin)
                 side_ref[pl.ds(BLOCK + t, HALF, stride=SIDE), :] = jnp.where(low, sin, -turned_cos)
                 side_ref[pl.ds(BLOCK + t + 1, HALF, stride=SIDE), :] = jnp.where(low, turned_sin, -cos)
-        for k in range(HALF):
-            if k:
-                left = side_ref[pl.ds(k * SIDE, 2 * BLOCK), :]
-            else:
-                edge = side_ref[pl.ds(0, BLOCK), :]
-                left = jnp.concatenate([jnp.where(low_edge, edge, 0.0), jnp.where(low_edge, 0.0, edge)], axis=0)
-            cross_ref[pl.ds(k * SIDE, 2 * BLOCK), :] = jnp.dot(
-                left.astype(BF16), pat_ref[k], preferred_element_type=F32
-            )
+        none = jnp.zeros((2 * BLOCK, LANES), BF16)
+        for k in range(0, HALF, 2):
+            left = [side_ref[pl.ds(u * SIDE, 2 * BLOCK), :] for u in (k, k + 1)]
+            if k == 0:
+                edge = left[0][:BLOCK]
+                left[0] = jnp.concatenate([jnp.where(low_edge, edge, 0.0), jnp.where(low_edge, 0.0, edge)], axis=0)
+            left = [jnp.concatenate([left[0].astype(BF16), none], axis=1), jnp.concatenate([none, left[1].astype(BF16)], axis=1)]
+            right = pat_ref[pl.ds(k, 2)].reshape(2 * LANES, LANES)
+            both = jnp.dot(jnp.concatenate(left, axis=0), right, preferred_element_type=F32)
+            cross_ref[pl.ds(k * SIDE, 2 * BLOCK), :] = both[: 2 * BLOCK]
+            cross_ref[pl.ds((k + 1) * SIDE, 2 * BLOCK), :] = both[2 * BLOCK :]
         rows = []
         for t in range(0, len(chunk) * PER_DEVICE, 2):
             cross = [
@@ -152,16 +151,23 @@
             rows += [top[:, :LANES], top[:, LANES:]]
         for number, (_, _, mask) in enumerate(chunk):
             for e in range(PER_DEVICE):
-                row = rows[number * PER_DEVICE + e]
                 where = (index ^ mask) * PER_DEVICE + e
-                corr_ref[pl.ds(where, 1), :] = row[:, :count]
-                group = orient_ref[where]
-                best_ref[pl.ds(group, 1), :] = jnp.maximum(best_ref[pl.ds(group, 1), :], row)
-    if more:
+                rows_ref[pl.ds(where, 1), :] = rows[number * PER_DEVICE + e]
+    if not final:
         return
-    best = best_ref[...]
+    corr = rows_ref[...]
+    corr_ref[...] = corr[:, : corr_ref.shape[1]]
+    total = corr.shape[0]
+    groups = orient_ref[...].astype(F32)
+    if total % LANES:
+        groups = jnp.concatenate([groups, jnp.zeros((1, LANES - total % LANES), F32)], axis=1)
+    groups = jnp.broadcast_to(groups, (LANES, groups.shape[1])).T[:total]
+    best = [
+        jnp.max(jnp.where(groups == float(g), corr, -jnp.inf), axis=0, keepdims=True) for g in range(smooth_ref.shape[0])
+    ]
+    best = jnp.concatenate(best, axis=0)
     smooth = 0.25 * (pltpu.roll(best, 1, 1) + 2.0 * best + pltpu.roll(best, LANES - 1, 1))
-    smooth_ref[...] = smooth[:, :count]
+    smooth_ref[...] = smooth[:, : smooth_ref.shape[1]]
 
 
 VMEM = pl.BlockSpec(memory_space=pltpu.VMEM)
@@ -209,20 +215,21 @@
     )(bins, gains, rows, inner, outer, table)
 
 
-def match(orientation, pat_spec, table, inverse, parts, held, carry, count, groups):
-    corr = jax.ShapeDtypeStruct((orientation.shape[0], count), F32)
-    best = pltpu.VMEM((groups, LANES), F32)
+def match(pat_spec, table, inverse, parts, held, orientation, carry, count, groups):
+    total = orientation.shape[1]
+    rows = jax.ShapeDtypeStruct((total, LANES), F32)
+    outs = [jax.ShapeDtypeStruct((total, count), F32), jax.ShapeDtypeStruct((groups, count), F32)] if carry else [rows]
     scratch = [pltpu.VMEM((HALF * SIDE, LANES), F32), pltpu.VMEM((HALF * SIDE, LANES), F32)]
-    second = jax.ShapeDtypeStruct((groups, count if carry else LANES), F32)
+    more = [orientation, *carry] if carry else []
     return pl.pallas_call(
-        functools.partial(match_kernel, held=held, more=not carry),
-        out_shape=(corr, second),
-        in_specs=[SMEM] + [VMEM] * (3 + len(parts) + len(carry)),
-        out_specs=(VMEM, VMEM),
-        scratch_shapes=scratch + [best] * bool(carry),
+        functools.partial(match_kernel, held=held, final=bool(carry)),
+        out_shape=outs,
+        in_specs=[VMEM] * (3 + len(parts) + len(more)),
+        out_specs=[VMEM] * len(outs),
+        scratch_shapes=scratch + [pltpu.VMEM(rows.shape, F32)] * bool(carry),
         compiler_params=pltpu.CompilerParams(vmem_limit_bytes=16 << 20),
         name="match",
-    )(orientation, pat_spec, table, inverse, *parts, *carry)
+    )(pat_spec, table, inverse, *parts, *more)
 
 
 def on_device(patterns, templates, radius_bin, radial_gain, orientation):
@@ -231,7 +238,7 @@
     count = patterns.shape[0]
     size = lax.axis_size("scan")
     groups = templates.shape[0] * size // TMPL_PER_GROUP
-    orientation = orientation.reshape(-1)
+    orientation = orientation.reshape(1, -1)
     bits = [1 << b for b in reversed(range(size.bit_length() - 1))]
     far, near, middle, core = bits[0], bits[1], bits[2:-1], bits[-1]
 
@@ -257,10 +264,10 @@
     pat_spec = pattern_spectra(radius_bin, radial_gain, rows, inner, outer, table)
     crossed = [[m ^ core for m in masks] for masks in held]
     early = [parts[0], send(parts[0], core)]
-    carry = match(orientation, pat_spec, table, inverse, early, [held[0], crossed[0]], [], count, groups)
+    carry = match(pat_spec, table, inverse, early, [held[0], crossed[0]], orientation, [], count, groups)
     last, pat_spec, carry = lax.optimization_barrier((parts[1], pat_spec, carry))
     late = [last, send(last, core)]
-    corr, smooth = match(orientation, pat_spec, table, inverse, late, [held[1], crossed[1]], carry, count, groups)
+    corr, smooth = match(pat_spec, table, inverse, late, [held[1], crossed[1]], orientation, carry, count, groups)
     return corr.T, smooth.T
 
 

time: 27.5 us -> 26.5 us (0.964)
  Pallas kernels: 12.3 us -> 10.4 us
  waiting for transfers between devices: 2.62 us -> 3.56 us
    pallas_call x2, Pallas kernels: 6.27 us -> 4.37 us  [match(): pl.pallas_call(functools.partial(match_kernel, held=held, final=bool(carr...]
    ppermute x7, waiting for transfers between devices: 2.61 us -> 3.56 us  [send(): return lax.ppermute(part, 'scan', [(i, i ^ mask) for i in range(size)])]
  transfers between devices with their start and end apart: 8 -> 8, of which waited for: 4 -> 4; matrix products, arithmetic and copies ran while one was open for 3% -> 3% of each run, Pallas kernels for 32% -> 30%
where the time goes in v5:
time: 26.5 us; the launch traced here: 26.4 us
  starting transfers between devices  10.8 us (41%)
  Pallas kernels  10.4 us (39%)
  waiting for transfers between devices  3.56 us (13%)
  other arithmetic  0.82 us (3%)
  between operations  0.75 us (3%)
    ppermute x7, starting transfers between devices, send(): return lax.ppermute(part, 'scan', [(i, i ^ mask) for i in range(size)])  10.2 us
    pallas_call x2, Pallas kernels, match(): pl.pallas_call(functools.partial(match_kernel, held=held, final=bool(carr...  4.37 us
    ppermute x7, waiting for transfers between devices, send(): return lax.ppermute(part, 'scan', [(i, i ^ mask) for i in range(size)])  3.56 us
    pallas_call x1, Pallas kernels, arrange(): pl.pallas_call(arrange_kernel, out_shape=(jax.ShapeDtypeStruct((RADII, co...  3.08 us
    pallas_call x1, Pallas kernels, pattern_spectra(): pl.pallas_call(pattern_kernel, out_shape=jax.ShapeDtypeStruct((HALF, LANE...  2.92 us
    select_n x1, other arithmetic, on_device(): jnp.where(even, leading, last)  0.78 us
    ppermute x1, starting transfers between devices, on_device(): outer = lax.ppermute(outer, 'scan', pairs + [(j, i) for i, j in pairs])  0.66 us
  transfers between devices with their start and end apart: 8, of which 4 were waited for; matrix products, arithmetic and copies ran while one was open for 3% of the time, Pallas kernels for 30%

profile of v5, /device:TPU:0, one launch (start us, length us, event | category | flops | bytes accessed | tf_op | source)
XLA Modules:
  0.0 26.4 jit_solution(13303571780412749330)
XLA Ops:
  0.6 0.0 copy-start.2
  0.6 0.0 copy-start.1
  0.6 4.1 %collective-permute-start = (bf16[2,64,256]{2,1,0:T(8,128)(2,1)}, bf16[2,64,256]{2,1,0:T(8,128)(2,1)S(1)}, u32[]{:S(2)}, u32[]{:S(2)}) collective-permute-start(bf16[2,64,256]{2,1,0:T(8,128)(2,1)} %tmpl_hbm.1), channel_id=1, source_target_pairs={{0,8},{1,9},{2,10},{3,11},{4,12},{5,13},{6,14},{7,15},{8,0},{9,1},... | collective-permute-start | bytes 196616 | tf_op jit(solution)/shard_map/ppermute | solution.py:246
  4.8 1.3 %collective-permute-start.1 = (bf16[2,64,256]{2,1,0:T(8,128)(2,1)}, bf16[2,64,256]{2,1,0:T(8,128)(2,1)S(1)}, u32[]{:S(2)}, u32[]{:S(2)}) collective-permute-start(bf16[2,64,256]{2,1,0:T(8,128)(2,1)} %tmpl_hbm.1), channel_id=1, source_target_pairs={{0,12},{1,13},{2,14},{3,15},{4,8},{5,9},{6,10},{7,11},{8,4},{9,5},... | collective-permute-start | bytes 196616 | tf_op jit(solution)/shard_map/ppermute | solution.py:246
  6.1 0.2 collective-permute-start.2
  6.3 0.8 %broadcast_select_fusion = (bf16[1,64,256]{2,1,0:T(8,128)(2,1)S(1)}, bf16[1,64,256]{2,1,0:T(8,128)(2,1)S(1)}) fusion(pred[]{:T(512)S(6)} %eq.5, bf16[96,64,256]{2,1,0:T(8,128)(2,1)} %pat_hbm.1), kind=kLoop, calls=%fused_computation.1 | loop fusion | flops 32768 | bytes 131073 | tf_op jit(solution)/shard_map/jit(_where)/select_n | solution.py:252
  7.1 0.1 collective-permute-start.3
  7.2 0.7 %collective-permute-start.4 = (bf16[1,64,256]{2,1,0:T(8,128)(2,1)S(1)}, bf16[1,64,256]{2,1,0:T(8,128)(2,1)S(1)}, u32[]{:S(2)}, u32[]{:S(2)}) collective-permute-start(bf16[1,64,256]{2,1,0:T(8,128)(2,1)S(1)} %get-tuple-element.34), channel_id=1, source_target_pairs={{1,2},{3,4},{5,6},{7,8},{9,10},{11,12},{13,14},{2,1},{4,3},{6,5},{... | collective-permute-start | bytes 98312 | tf_op jit(solution)/shard_map/ppermute | solution.py:255
  7.9 3.1 %arrange.1 = (bf16[64,96,256]{2,1,0:T(8,128)(2,1)S(1)}, bf16[2,64,256]{2,1,0:T(8,128)(2,1)S(1)}, bf16[256,256]{1,0:T(8,128)(2,1)S(1)}) custom-call(bf16[96,64,256]{2,1,0:T(8,128)(2,1)} %pat_hbm.1, bf16[2,64,256]{2,1,0:T(8,128)(2,1)} %tmpl_hbm.1, bf16[256,256]{1,0:T(8,128)(2,1)} %constant.22.clone.table_hbm), custom_call_target="tpu_custom_call" | custom-call | tf_op jit(solution)/shard_map/arrange/pallas_call | solution.py:181
  10.9 0.0 collective-permute-done.3.inner_ref
  11.0 0.0 collective-permute-done.4.outer_ref
  11.0 0.0 collective-permute-done
  11.0 0.2 collective-permute-done.1
  11.2 0.1 collective-permute-done.2
  11.3 0.0 copy-start
  11.3 2.7 %collective-permute-start.6 = (bf16[8,64,256]{2,1,0:T(8,128)(2,1)S(1)}, bf16[8,64,256]{2,1,0:T(8,128)(2,1)S(1)}, u32[]{:S(2)}, u32[]{:S(2)}) collective-permute-start(bf16[8,64,256]{2,1,0:T(8,128)(2,1)S(1)} %pad_maximum_fusion.refs_0_), channel_id=1, source_target_pairs={{0,1},{1,0},{2,3},{3,2},{4,5},{5,4},{6,7},{7,6},{8,9},{9,8},{10,11... | collective-permute-start | bytes 786440 | tf_op jit(solution)/shard_map/ppermute | solution.py:246
  14.0 1.7 %collective-permute-start.5 = (bf16[8,64,256]{2,1,0:T(8,128)(2,1)S(1)}, bf16[8,64,256]{2,1,0:T(8,128)(2,1)S(1)}, u32[]{:S(2)}, u32[]{:S(2)}) collective-permute-start(bf16[8,64,256]{2,1,0:T(8,128)(2,1)S(1)} %pad_maximum_fusion.refs_0_), channel_id=1, source_target_pairs={{0,2},{1,3},{2,0},{3,1},{4,6},{5,7},{6,4},{7,5},{8,10},{9,11},{10,... | collective-permute-start | bytes 786440 | tf_op jit(solution)/shard_map/ppermute | solution.py:246
  15.7 0.0 copy-done.2
  15.7 0.0 copy-done.1
  15.7 2.9 %pattern_spectra.1.pat_ref = bf16[128,128,128]{2,1,0:T(8,128)(2,1)S(1)} custom-call(s32[64]{0:T(128)S(1)} %copy-done.1, f32[8]{0:T(128)S(1)} %copy-done.2, bf16[64,96,256]{2,1,0:T(8,128)(2,1)S(1)} %get-tuple-element.25.rows_ref, bf16[1,64,256]{2,1,0:T(8,128)(2,1)S(1)} %collective-permute-done.3.inner_ref, ...), custom_call_target="tpu_custom_call" | custom-call | tf_op jit(solution)/shard_map/pattern_spectra/pallas_call | solution.py:203
  18.7 0.0 copy-start.3
  18.7 0.0 collective-permute-done.6.refs_1_
  18.7 0.0 copy-done
  18.7 1.9 %match.2.refs_3_ = f32[32,128]{1,0:T(8,128)S(1)} custom-call(bf16[128,128,128]{2,1,0:T(8,128)(2,1)S(1)} %pattern_spectra.1.pat_ref, bf16[256,256]{1,0:T(8,128)(2,1)S(1)} %get-tuple-element.28.table_ref, bf16[256,256]{1,0:T(8,128)(2,1)S(1)} %copy-done, bf16[8,64,256]{2,1,0:T(8,128)(2,1)S(1)} %pad_maximum_fusion.refs_0_, ...), custom_call_target="tpu_custom_call" | custom-call | tf_op jit(solution)/shard_map/match/pallas_call | solution.py:224
  20.6 1.7 %collective-permute-done.5.refs_0_ = bf16[8,64,256]{2,1,0:T(8,128)(2,1)S(1)} collective-permute-done((bf16[8,64,256]{2,1,0:T(8,128)(2,1)S(1)}, bf16[8,64,256]{2,1,0:T(8,128)(2,1)S(1)}, u32[]{:S(2)}, u32[]{:S(2)}) %collective-permute-start.5) | collective-permute-done | bytes 262176 | tf_op jit(solution)/shard_map/ppermute | solution.py:246
  22.3 0.0 collective-permute-start.7
  22.3 1.5 %collective-permute-done.7.refs_1_ = bf16[8,64,256]{2,1,0:T(8,128)(2,1)S(1)} collective-permute-done((bf16[8,64,256]{2,1,0:T(8,128)(2,1)S(1)}, bf16[8,64,256]{2,1,0:T(8,128)(2,1)S(1)}, u32[]{:S(2)}, u32[]{:S(2)}) %collective-permute-start.7) | collective-permute-done | bytes 262176 | tf_op jit(solution)/shard_map/ppermute | solution.py:246
  23.8 0.0 copy-done.3
  23.8 2.5 %match.3 = (f32[32,96]{1,0:T(8,128)}, f32[16,96]{1,0:T(8,128)}) custom-call(bf16[128,128,128]{2,1,0:T(8,128)(2,1)S(1)} %pattern_spectra.1.pat_ref, bf16[256,256]{1,0:T(8,128)(2,1)S(1)} %get-tuple-element.28.table_ref, bf16[256,256]{1,0:T(8,128)(2,1)S(1)} %copy-done, bf16[8,64,256]{2,1,0:T(8,128)(2,1)S(1)} %collective-permute-done.5.refs_0_, ...), custom_call_target="tpu_custom_call" | custom-call | tf_op jit(solution)/shard_map/match/pallas_call | solution.py:224
  (1 shorter events, 0.0 us)
Async XLA Ops:
  0.6 15.1 %copy-start.2 = (f32[8]{0:T(128)S(1)}, f32[8]{0:T(128)}, u32[]{:S(2)}) copy-start(f32[8]{0:T(128)} %gain_ref.1) | copy-start | bytes 100
  0.6 15.1 %copy-start.1 = (s32[64]{0:T(128)S(1)}, s32[64]{0:T(128)}, u32[]{:S(2)}) copy-start(s32[64]{0:T(128)} %bin_ref.1) | copy-start | bytes 772
  0.6 10.3 %collective-permute-start = (bf16[2,64,256]{2,1,0:T(8,128)(2,1)}, bf16[2,64,256]{2,1,0:T(8,128)(2,1)S(1)}, u32[]{:S(2)}, u32[]{:S(2)}) collective-permute-start(bf16[2,64,256]{2,1,0:T(8,128)(2,1)} %tmpl_hbm.1), channel_id=1, source_target_pairs={{0,8},{1,9},{2,10},{3,11},{4,12},{5,13},{6,14},{7,15},{8,0},{9,1},... | collective-permute-start | bytes 196616 | tf_op jit(solution)/shard_map/ppermute | solution.py:246
  4.8 6.4 %collective-permute-start.1 = (bf16[2,64,256]{2,1,0:T(8,128)(2,1)}, bf16[2,64,256]{2,1,0:T(8,128)(2,1)S(1)}, u32[]{:S(2)}, u32[]{:S(2)}) collective-permute-start(bf16[2,64,256]{2,1,0:T(8,128)(2,1)} %tmpl_hbm.1), channel_id=1, source_target_pairs={{0,12},{1,13},{2,14},{3,15},{4,8},{5,9},{6,10},{7,11},{8,4},{9,5},... | collective-permute-start | bytes 196616 | tf_op jit(solution)/shard_map/ppermute | solution.py:246
  6.1 5.2 %collective-permute-start.2 = (bf16[2,64,256]{2,1,0:T(8,128)(2,1)}, bf16[2,64,256]{2,1,0:T(8,128)(2,1)S(1)}, u32[]{:S(2)}, u32[]{:S(2)}) collective-permute-start(bf16[2,64,256]{2,1,0:T(8,128)(2,1)} %tmpl_hbm.1), channel_id=1, source_target_pairs={{0,4},{1,5},{2,6},{3,7},{4,0},{5,1},{6,2},{7,3},{8,12},{9,13},{10,... | collective-permute-start | bytes 196616 | tf_op jit(solution)/shard_map/ppermute | solution.py:246
  7.1 3.8 %collective-permute-start.3 = (bf16[1,64,256]{2,1,0:T(8,128)(2,1)S(1)}, bf16[1,64,256]{2,1,0:T(8,128)(2,1)S(1)}, u32[]{:S(2)}, u32[]{:S(2)}) collective-permute-start(bf16[1,64,256]{2,1,0:T(8,128)(2,1)S(1)} %get-tuple-element.35), channel_id=1, source_target_pairs={{0,1},{1,0},{2,3},{3,2},{4,5},{5,4},{6,7},{7,6},{8,9},{9,8},{10,11... | collective-permute-start | bytes 98312 | tf_op jit(solution)/shard_map/ppermute | solution.py:246
  7.2 3.8 %collective-permute-start.4 = (bf16[1,64,256]{2,1,0:T(8,128)(2,1)S(1)}, bf16[1,64,256]{2,1,0:T(8,128)(2,1)S(1)}, u32[]{:S(2)}, u32[]{:S(2)}) collective-permute-start(bf16[1,64,256]{2,1,0:T(8,128)(2,1)S(1)} %get-tuple-element.34), channel_id=1, source_target_pairs={{1,2},{3,4},{5,6},{7,8},{9,10},{11,12},{13,14},{2,1},{4,3},{6,5},{... | collective-permute-start | bytes 98312 | tf_op jit(solution)/shard_map/ppermute | solution.py:255
  11.3 7.4 %copy-start = (bf16[256,256]{1,0:T(8,128)(2,1)S(1)}, bf16[256,256]{1,0:T(8,128)(2,1)}, u32[]{:S(2)}) copy-start(bf16[256,256]{1,0:T(8,128)(2,1)} %constant.23.clone.inv_ref) | copy-start | bytes 393220
  11.3 7.4 %collective-permute-start.6 = (bf16[8,64,256]{2,1,0:T(8,128)(2,1)S(1)}, bf16[8,64,256]{2,1,0:T(8,128)(2,1)S(1)}, u32[]{:S(2)}, u32[]{:S(2)}) collective-permute-start(bf16[8,64,256]{2,1,0:T(8,128)(2,1)S(1)} %pad_maximum_fusion.refs_0_), channel_id=1, source_target_pairs={{0,1},{1,0},{2,3},{3,2},{4,5},{5,4},{6,7},{7,6},{8,9},{9,8},{10,11... | collective-permute-start | bytes 786440 | tf_op jit(solution)/shard_map/ppermute | solution.py:246
  14.0 8.3 %collective-permute-start.5 = (bf16[8,64,256]{2,1,0:T(8,128)(2,1)S(1)}, bf16[8,64,256]{2,1,0:T(8,128)(2,1)S(1)}, u32[]{:S(2)}, u32[]{:S(2)}) collective-permute-start(bf16[8,64,256]{2,1,0:T(8,128)(2,1)S(1)} %pad_maximum_fusion.refs_0_), channel_id=1, source_target_pairs={{0,2},{1,3},{2,0},{3,1},{4,6},{5,7},{6,4},{7,5},{8,10},{9,11},{10,... | collective-permute-start | bytes 786440 | tf_op jit(solution)/shard_map/ppermute | solution.py:246
  18.7 5.2 %copy-start.3 = (s32[32,1]{0,1:T(1,128)S(1)}, s32[32,1]{0,1:T(1,128)}, u32[]{:S(2)}) copy-start(s32[32,1]{0,1:T(1,128)} %param.11) | copy-start | bytes 388
  22.3 1.5 %collective-permute-start.7 = (bf16[8,64,256]{2,1,0:T(8,128)(2,1)S(1)}, bf16[8,64,256]{2,1,0:T(8,128)(2,1)S(1)}, u32[]{:S(2)}, u32[]{:S(2)}) collective-permute-start(bf16[8,64,256]{2,1,0:T(8,128)(2,1)S(1)} %collective-permute-done.5.refs_0_), channel_id=1, source_target_pairs={{0,1},{1,0},{2,3},{3,2},{4,5},{5,4},{6,7},{7,6},{8,9},{9,8},{10,11... | collective-permute-start | bytes 786440 | tf_op jit(solution)/shard_map/ppermute | solution.py:246

commit v6 on v5

--- a/solution.py
+++ b/solution.py
@@ -39,7 +39,6 @@
 
 
 PITCH = LANES + 8
-SIDE = 2 * BLOCK + 8
 
 
 def arrange_kernel(pat_hbm, tmpl_hbm, table_hbm, out_ref, own_ref, table_ref, pat_ref, raw_ref, sem, side_sem):
@@ -100,19 +99,23 @@
         out_ref[k] = spec_ref[pl.ds(k * PITCH, LANES), :].astype(BF16)
 
 
-def match_kernel(pat_ref, table_ref, inv_ref, *refs, held, final):
+def match_kernel(pat_ref, table_ref, inv_ref, *refs, held, block, first, final):
+    side = 2 * block + 8
     parts, refs = refs[: len(held)], refs[len(held) :]
     if final:
         orient_ref, rows_in, corr_ref, smooth_ref, side_ref, cross_ref, rows_ref = refs
+    elif first:
+        rows_ref, side_ref, cross_ref = refs
+    else:
+        rows_in, rows_ref, side_ref, cross_ref = refs
+    if not first:
         rows_ref[...] = rows_in[...]
-    else:
-        rows_ref, side_ref, cross_ref = refs
     index = lax.axis_index("scan")
     blocks = [(part, i, mask) for part, masks in zip(parts, held) for i, mask in enumerate(masks)]
     low = lax.broadcasted_iota(jnp.int32, (HALF, LANES), 1) < RADII
-    low_edge = lax.broadcasted_iota(jnp.int32, (BLOCK, LANES), 1) < RADII
-    for begin in range(0, len(blocks), BLOCK // PER_DEVICE):
-        chunk = blocks[begin : begin + BLOCK // PER_DEVICE]
+    low_edge = lax.broadcasted_iota(jnp.int32, (block, LANES), 1) < RADII
+    for begin in range(0, len(blocks), block // PER_DEVICE):
+        chunk = blocks[begin : begin + block // PER_DEVICE]
         for number in range(0, len(chunk), 2):
             (part, i, _), (other, j, _) = chunk[number : number + 2]
             raw = jnp.concatenate([part[pl.ds(i * PER_DEVICE, PER_DEVICE)], other[pl.ds(j * PER_DEVICE, PER_DEVICE)]])
@@ -123,26 +126,26 @@
                 spec = both[:, u * LANES : (u + 1) * LANES]
                 cos, sin = spec[:HALF], spec[HALF:]
                 turned_cos, turned_sin = pltpu.roll(cos, RADII, 1), pltpu.roll(sin, RADII, 1)
-                side_ref[pl.ds(t, HALF, stride=SIDE), :] = jnp.where(low, cos, turned_sin)
-                side_ref[pl.ds(t + 1, HALF, stride=SIDE), :] = jnp.where(low, turned_cos, sin)
-                side_ref[pl.ds(BLOCK + t, HALF, stride=SIDE), :] = jnp.where(low, sin, -turned_cos)
-                side_ref[pl.ds(BLOCK + t + 1, HALF, stride=SIDE), :] = jnp.where(low, turned_sin, -cos)
-        none = jnp.zeros((2 * BLOCK, LANES), BF16)
+                side_ref[pl.ds(t, HALF, stride=side), :] = jnp.where(low, cos, turned_sin)
+                side_ref[pl.ds(t + 1, HALF, stride=side), :] = jnp.where(low, turned_cos, sin)
+                side_ref[pl.ds(block + t, HALF, stride=side), :] = jnp.where(low, sin, -turned_cos)
+                side_ref[pl.ds(block + t + 1, HALF, stride=side), :] = jnp.where(low, turned_sin, -cos)
+        none = jnp.zeros((2 * block, LANES), BF16)
         for k in range(0, HALF, 2):
-            left = [side_ref[pl.ds(u * SIDE, 2 * BLOCK), :] for u in (k, k + 1)]
+            left = [side_ref[pl.ds(u * side, 2 * block), :] for u in (k, k + 1)]
             if k == 0:
-                edge = left[0][:BLOCK]
+                edge = left[0][:block]
                 left[0] = jnp.concatenate([jnp.where(low_edge, edge, 0.0), jnp.where(low_edge, 0.0, edge)], axis=0)
             left = [jnp.concatenate([left[0].astype(BF16), none], axis=1), jnp.concatenate([none, left[1].astype(BF16)], axis=1)]
             right = pat_ref[pl.ds(k, 2)].reshape(2 * LANES, LANES)
             both = jnp.dot(jnp.concatenate(left, axis=0), right, preferred_element_type=F32)
-            cross_ref[pl.ds(k * SIDE, 2 * BLOCK), :] = both[: 2 * BLOCK]
-            cross_ref[pl.ds((k + 1) * SIDE, 2 * BLOCK), :] = both[2 * BLOCK :]
+            cross_ref[pl.ds(k * side, 2 * block), :] = both[: 2 * block]
+            cross_ref[pl.ds((k + 1) * side, 2 * block), :] = both[2 * block :]
         rows = []
         for t in range(0, len(chunk) * PER_DEVICE, 2):
             cross = [
                 jnp.concatenate(
-                    [cross_ref[pl.ds(u, HALF, stride=SIDE), :], cross_ref[pl.ds(BLOCK + u, HALF, stride=SIDE), :]], axis=0
+                    [cross_ref[pl.ds(u, HALF, stride=side), :], cross_ref[pl.ds(block + u, HALF, stride=side), :]], axis=0
                 ).astype(BF16)
                 for u in (t, t + 1)
             ]
@@ -215,21 +218,23 @@
     )(bins, gains, rows, inner, outer, table)
 
 
-def match(pat_spec, table, inverse, parts, held, orientation, carry, count, groups):
-    total = orientation.shape[1]
+def match(pat_spec, table, inverse, parts, held, carry, total, final=None):
+    block = min(BLOCK, sum(part.shape[0] for part in parts))
     rows = jax.ShapeDtypeStruct((total, LANES), F32)
-    outs = [jax.ShapeDtypeStruct((total, count), F32), jax.ShapeDtypeStruct((groups, count), F32)] if carry else [rows]
-    scratch = [pltpu.VMEM((HALF * SIDE, LANES), F32), pltpu.VMEM((HALF * SIDE, LANES), F32)]
-    more = [orientation, *carry] if carry else []
+    outs = [rows]
+    if final:
+        orientation, *outs = final
+        carry = [orientation, *carry]
+    scratch = [pltpu.VMEM((HALF * (2 * block + 8), LANES), F32)] * 2
     return pl.pallas_call(
-        functools.partial(match_kernel, held=held, final=bool(carry)),
+        functools.partial(match_kernel, held=held, block=block, first=not carry, final=bool(final)),
         out_shape=outs,
-        in_specs=[VMEM] * (3 + len(parts) + len(more)),
+        in_specs=[VMEM] * (3 + len(parts) + len(carry)),
         out_specs=[VMEM] * len(outs),
-        scratch_shapes=scratch + [pltpu.VMEM(rows.shape, F32)] * bool(carry),
+        scratch_shapes=scratch + [pltpu.VMEM(rows.shape, F32)] * bool(final),
         compiler_params=pltpu.CompilerParams(vmem_limit_bytes=16 << 20),
         name="match",
-    )(pat_spec, table, inverse, *parts, *more)
+    )(pat_spec, table, inverse, *parts, *carry)
 
 
 def on_device(patterns, templates, radius_bin, radial_gain, orientation):
@@ -264,10 +269,14 @@
     pat_spec = pattern_spectra(radius_bin, radial_gain, rows, inner, outer, table)
     crossed = [[m ^ core for m in masks] for masks in held]
     early = [parts[0], send(parts[0], core)]
-    carry = match(pat_spec, table, inverse, early, [held[0], crossed[0]], orientation, [], count, groups)
+    total = orientation.shape[1]
+    outs = jax.ShapeDtypeStruct((total, count), F32), jax.ShapeDtypeStruct((groups, count), F32)
+    carry = match(pat_spec, table, inverse, early, [held[0], crossed[0]], [], total)
     last, pat_spec, carry = lax.optimization_barrier((parts[1], pat_spec, carry))
-    late = [last, send(last, core)]
-    corr, smooth = match(pat_spec, table, inverse, late, [held[1], crossed[1]], orientation, carry, count, groups)
+    over = send(last, core)
+    carry = match(pat_spec, table, inverse, [last], [held[1]], carry, total)
+    over, carry = lax.optimization_barrier((over, carry))
+    corr, smooth = match(pat_spec, table, inverse, [over], [crossed[1]], carry, total, (orientation, *outs))
     return corr.T, smooth.T
 
 

time: 26.5 us -> 26.2 us (0.989)
  waiting for transfers between devices: 3.56 us -> 2.26 us
  Pallas kernels: 10.4 us -> 11.3 us
    ppermute x7, waiting for transfers between devices: 3.56 us -> 2.26 us  [send(): return lax.ppermute(part, 'scan', [(i, i ^ mask) for i in range(size)])]
    pallas_call x2 -> x3, Pallas kernels: 4.37 us -> 5.29 us  [match(): pl.pallas_call(functools.partial(match_kernel, held=held, block=block, fi...]
  transfers between devices with their start and end apart: 8 -> 8, of which waited for: 4 -> 4; matrix products, arithmetic and copies ran while one was open for 3% -> 3% of each run, Pallas kernels for 30% -> 35%
where the time goes in v6:
time: 26.2 us; the launch traced here: 26 us
  Pallas kernels  11.3 us (43%)
  starting transfers between devices  10.8 us (41%)
  waiting for transfers between devices  2.26 us (9%)
  other arithmetic  0.82 us (3%)
  between operations  0.76 us (3%)
    ppermute x7, starting transfers between devices, send(): return lax.ppermute(part, 'scan', [(i, i ^ mask) for i in range(size)])  10.2 us
    pallas_call x3, Pallas kernels, match(): pl.pallas_call(functools.partial(match_kernel, held=held, block=block, fi...  5.29 us
    pallas_call x1, Pallas kernels, arrange(): pl.pallas_call(arrange_kernel, out_shape=(jax.ShapeDtypeStruct((RADII, co...  3.08 us
    pallas_call x1, Pallas kernels, pattern_spectra(): pl.pallas_call(pattern_kernel, out_shape=jax.ShapeDtypeStruct((HALF, LANE...  2.93 us
    ppermute x7, waiting for transfers between devices, send(): return lax.ppermute(part, 'scan', [(i, i ^ mask) for i in range(size)])  2.26 us
    select_n x1, other arithmetic, on_device(): jnp.where(even, leading, last)  0.78 us
    ppermute x1, starting transfers between devices, on_device(): outer = lax.ppermute(outer, 'scan', pairs + [(j, i) for i, j in pairs])  0.66 us
  transfers between devices with their start and end apart: 8, of which 4 were waited for; matrix products, arithmetic and copies ran while one was open for 3% of the time, Pallas kernels for 35%

profile of v6, /device:TPU:0, one launch (start us, length us, event | category | flops | bytes accessed | tf_op | source)
XLA Modules:
  0.0 26.0 jit_solution(1065946005316188451)
XLA Ops:
  0.6 0.0 copy-start.2
  0.6 0.0 copy-start.1
  0.6 4.1 %collective-permute-start = (bf16[2,64,256]{2,1,0:T(8,128)(2,1)}, bf16[2,64,256]{2,1,0:T(8,128)(2,1)S(1)}, u32[]{:S(2)}, u32[]{:S(2)}) collective-permute-start(bf16[2,64,256]{2,1,0:T(8,128)(2,1)} %tmpl_hbm.1), channel_id=1, source_target_pairs={{0,8},{1,9},{2,10},{3,11},{4,12},{5,13},{6,14},{7,15},{8,0},{9,1},... | collective-permute-start | bytes 196616 | tf_op jit(solution)/shard_map/ppermute | solution.py:251
  4.8 1.3 %collective-permute-start.1 = (bf16[2,64,256]{2,1,0:T(8,128)(2,1)}, bf16[2,64,256]{2,1,0:T(8,128)(2,1)S(1)}, u32[]{:S(2)}, u32[]{:S(2)}) collective-permute-start(bf16[2,64,256]{2,1,0:T(8,128)(2,1)} %tmpl_hbm.1), channel_id=1, source_target_pairs={{0,12},{1,13},{2,14},{3,15},{4,8},{5,9},{6,10},{7,11},{8,4},{9,5},... | collective-permute-start | bytes 196616 | tf_op jit(solution)/shard_map/ppermute | solution.py:251
  6.1 0.2 collective-permute-start.2
  6.3 0.8 %broadcast_select_fusion = (bf16[1,64,256]{2,1,0:T(8,128)(2,1)S(1)}, bf16[1,64,256]{2,1,0:T(8,128)(2,1)S(1)}) fusion(pred[]{:T(512)S(6)} %eq.5, bf16[96,64,256]{2,1,0:T(8,128)(2,1)} %pat_hbm.1), kind=kLoop, calls=%fused_computation.1 | loop fusion | flops 32768 | bytes 131073 | tf_op jit(solution)/shard_map/jit(_where)/select_n | solution.py:257
  7.1 0.1 collective-permute-start.3
  7.2 0.7 %collective-permute-start.4 = (bf16[1,64,256]{2,1,0:T(8,128)(2,1)S(1)}, bf16[1,64,256]{2,1,0:T(8,128)(2,1)S(1)}, u32[]{:S(2)}, u32[]{:S(2)}) collective-permute-start(bf16[1,64,256]{2,1,0:T(8,128)(2,1)S(1)} %get-tuple-element.38), channel_id=1, source_target_pairs={{1,2},{3,4},{5,6},{7,8},{9,10},{11,12},{13,14},{2,1},{4,3},{6,5},{... | collective-permute-start | bytes 98312 | tf_op jit(solution)/shard_map/ppermute | solution.py:260
  7.9 3.1 %arrange.1 = (bf16[64,96,256]{2,1,0:T(8,128)(2,1)S(1)}, bf16[2,64,256]{2,1,0:T(8,128)(2,1)S(1)}, bf16[256,256]{1,0:T(8,128)(2,1)S(1)}) custom-call(bf16[96,64,256]{2,1,0:T(8,128)(2,1)} %pat_hbm.1, bf16[2,64,256]{2,1,0:T(8,128)(2,1)} %tmpl_hbm.1, bf16[256,256]{1,0:T(8,128)(2,1)} %constant.22.clone.table_hbm), custom_call_target="tpu_custom_call" | custom-call | tf_op jit(solution)/shard_map/arrange/pallas_call | solution.py:184
  10.9 0.0 collective-permute-done.3.inner_ref
  11.0 0.0 collective-permute-done.4.outer_ref
  11.0 0.0 collective-permute-done
  11.0 0.2 collective-permute-done.1
  11.2 0.1 collective-permute-done.2
  11.3 0.0 copy-start
  11.3 2.7 %collective-permute-start.6 = (bf16[8,64,256]{2,1,0:T(8,128)(2,1)S(1)}, bf16[8,64,256]{2,1,0:T(8,128)(2,1)S(1)}, u32[]{:S(2)}, u32[]{:S(2)}) collective-permute-start(bf16[8,64,256]{2,1,0:T(8,128)(2,1)S(1)} %pad_maximum_fusion.refs_0_), channel_id=1, source_target_pairs={{0,1},{1,0},{2,3},{3,2},{4,5},{5,4},{6,7},{7,6},{8,9},{9,8},{10,11... | collective-permute-start | bytes 786440 | tf_op jit(solution)/shard_map/ppermute | solution.py:251
  14.0 1.7 %collective-permute-start.5 = (bf16[8,64,256]{2,1,0:T(8,128)(2,1)S(1)}, bf16[8,64,256]{2,1,0:T(8,128)(2,1)S(1)}, u32[]{:S(2)}, u32[]{:S(2)}) collective-permute-start(bf16[8,64,256]{2,1,0:T(8,128)(2,1)S(1)} %pad_maximum_fusion.refs_0_), channel_id=1, source_target_pairs={{0,2},{1,3},{2,0},{3,1},{4,6},{5,7},{6,4},{7,5},{8,10},{9,11},{10,... | collective-permute-start | bytes 786440 | tf_op jit(solution)/shard_map/ppermute | solution.py:251
  15.7 0.0 copy-done.2
  15.7 0.0 copy-done.1
  15.7 2.9 %pattern_spectra.1.pat_ref = bf16[128,128,128]{2,1,0:T(8,128)(2,1)S(1)} custom-call(s32[64]{0:T(128)S(1)} %copy-done.1, f32[8]{0:T(128)S(1)} %copy-done.2, bf16[64,96,256]{2,1,0:T(8,128)(2,1)S(1)} %get-tuple-element.27.rows_ref, bf16[1,64,256]{2,1,0:T(8,128)(2,1)S(1)} %collective-permute-done.3.inner_ref, ...), custom_call_target="tpu_custom_call" | custom-call | tf_op jit(solution)/shard_map/pattern_spectra/pallas_call | solution.py:206
  18.7 0.0 collective-permute-done.6.refs_1_
  18.7 0.0 copy-done
  18.7 1.7 %match.3.refs_1_ = f32[32,128]{1,0:T(8,128)S(1)} custom-call(bf16[128,128,128]{2,1,0:T(8,128)(2,1)S(1)} %pattern_spectra.1.pat_ref, bf16[256,256]{1,0:T(8,128)(2,1)S(1)} %get-tuple-element.30.table_ref, bf16[256,256]{1,0:T(8,128)(2,1)S(1)} %copy-done, bf16[8,64,256]{2,1,0:T(8,128)(2,1)S(1)} %pad_maximum_fusion.refs_0_, ...), custom_call_target="tpu_custom_call" | custom-call | tf_op jit(solution)/shard_map/match/pallas_call | solution.py:229
  20.4 0.0 copy-start.3
  20.4 1.9 %collective-permute-done.5.refs_0_ = bf16[8,64,256]{2,1,0:T(8,128)(2,1)S(1)} collective-permute-done((bf16[8,64,256]{2,1,0:T(8,128)(2,1)S(1)}, bf16[8,64,256]{2,1,0:T(8,128)(2,1)S(1)}, u32[]{:S(2)}, u32[]{:S(2)}) %collective-permute-start.5) | collective-permute-done | bytes 262176 | tf_op jit(solution)/shard_map/ppermute | solution.py:251
  22.3 0.0 collective-permute-start.7
  22.3 1.4 %match.4.refs_2_ = f32[32,128]{1,0:T(8,128)S(1)} custom-call(bf16[128,128,128]{2,1,0:T(8,128)(2,1)S(1)} %pattern_spectra.1.pat_ref, bf16[256,256]{1,0:T(8,128)(2,1)S(1)} %get-tuple-element.30.table_ref, bf16[256,256]{1,0:T(8,128)(2,1)S(1)} %copy-done, bf16[8,64,256]{2,1,0:T(8,128)(2,1)S(1)} %collective-permute-done.5.refs_0_, f32[32,128]{1,0:T(8,128)S(1)} %match.3.refs_1_), custom_call_target="tpu_custom_call" | custom-call | tf_op jit(solution)/shard_map/match/pallas_call | solution.py:229
  23.7 0.1 collective-permute-done.7.refs_0_
  23.8 0.0 copy-done.3
  23.8 2.1 %match.5 = (f32[32,96]{1,0:T(8,128)}, f32[16,96]{1,0:T(8,128)}) custom-call(bf16[128,128,128]{2,1,0:T(8,128)(2,1)S(1)} %pattern_spectra.1.pat_ref, bf16[256,256]{1,0:T(8,128)(2,1)S(1)} %get-tuple-element.30.table_ref, bf16[256,256]{1,0:T(8,128)(2,1)S(1)} %copy-done, bf16[8,64,256]{2,1,0:T(8,128)(2,1)S(1)} %collective-permute-done.7.refs_0_, ...), custom_call_target="tpu_custom_call" | custom-call | tf_op jit(solution)/shard_map/match/pallas_call | solution.py:229
  (1 shorter events, 0.0 us)
Async XLA Ops:
  0.6 15.1 %copy-start.2 = (f32[8]{0:T(128)S(1)}, f32[8]{0:T(128)}, u32[]{:S(2)}) copy-start(f32[8]{0:T(128)} %gain_ref.1) | copy-start | bytes 100
  0.6 15.1 %copy-start.1 = (s32[64]{0:T(128)S(1)}, s32[64]{0:T(128)}, u32[]{:S(2)}) copy-start(s32[64]{0:T(128)} %bin_ref.1) | copy-start | bytes 772
  0.6 10.3 %collective-permute-start = (bf16[2,64,256]{2,1,0:T(8,128)(2,1)}, bf16[2,64,256]{2,1,0:T(8,128)(2,1)S(1)}, u32[]{:S(2)}, u32[]{:S(2)}) collective-permute-start(bf16[2,64,256]{2,1,0:T(8,128)(2,1)} %tmpl_hbm.1), channel_id=1, source_target_pairs={{0,8},{1,9},{2,10},{3,11},{4,12},{5,13},{6,14},{7,15},{8,0},{9,1},... | collective-permute-start | bytes 196616 | tf_op jit(solution)/shard_map/ppermute | solution.py:251
  4.8 6.4 %collective-permute-start.1 = (bf16[2,64,256]{2,1,0:T(8,128)(2,1)}, bf16[2,64,256]{2,1,0:T(8,128)(2,1)S(1)}, u32[]{:S(2)}, u32[]{:S(2)}) collective-permute-start(bf16[2,64,256]{2,1,0:T(8,128)(2,1)} %tmpl_hbm.1), channel_id=1, source_target_pairs={{0,12},{1,13},{2,14},{3,15},{4,8},{5,9},{6,10},{7,11},{8,4},{9,5},... | collective-permute-start | bytes 196616 | tf_op jit(solution)/shard_map/ppermute | solution.py:251
  6.1 5.2 %collective-permute-start.2 = (bf16[2,64,256]{2,1,0:T(8,128)(2,1)}, bf16[2,64,256]{2,1,0:T(8,128)(2,1)S(1)}, u32[]{:S(2)}, u32[]{:S(2)}) collective-permute-start(bf16[2,64,256]{2,1,0:T(8,128)(2,1)} %tmpl_hbm.1), channel_id=1, source_target_pairs={{0,4},{1,5},{2,6},{3,7},{4,0},{5,1},{6,2},{7,3},{8,12},{9,13},{10,... | collective-permute-start | bytes 196616 | tf_op jit(solution)/shard_map/ppermute | solution.py:251
  7.1 3.8 %collective-permute-start.3 = (bf16[1,64,256]{2,1,0:T(8,128)(2,1)S(1)}, bf16[1,64,256]{2,1,0:T(8,128)(2,1)S(1)}, u32[]{:S(2)}, u32[]{:S(2)}) collective-permute-start(bf16[1,64,256]{2,1,0:T(8,128)(2,1)S(1)} %get-tuple-element.39), channel_id=1, source_target_pairs={{0,1},{1,0},{2,3},{3,2},{4,5},{5,4},{6,7},{7,6},{8,9},{9,8},{10,11... | collective-permute-start | bytes 98312 | tf_op jit(solution)/shard_map/ppermute | solution.py:251
  7.2 3.8 %collective-permute-start.4 = (bf16[1,64,256]{2,1,0:T(8,128)(2,1)S(1)}, bf16[1,64,256]{2,1,0:T(8,128)(2,1)S(1)}, u32[]{:S(2)}, u32[]{:S(2)}) collective-permute-start(bf16[1,64,256]{2,1,0:T(8,128)(2,1)S(1)} %get-tuple-element.38), channel_id=1, source_target_pairs={{1,2},{3,4},{5,6},{7,8},{9,10},{11,12},{13,14},{2,1},{4,3},{6,5},{... | collective-permute-start | bytes 98312 | tf_op jit(solution)/shard_map/ppermute | solution.py:260
  11.3 7.4 %copy-start = (bf16[256,256]{1,0:T(8,128)(2,1)S(1)}, bf16[256,256]{1,0:T(8,128)(2,1)}, u32[]{:S(2)}) copy-start(bf16[256,256]{1,0:T(8,128)(2,1)} %constant.23.clone.inv_ref) | copy-start | bytes 393220
  11.3 7.4 %collective-permute-start.6 = (bf16[8,64,256]{2,1,0:T(8,128)(2,1)S(1)}, bf16[8,64,256]{2,1,0:T(8,128)(2,1)S(1)}, u32[]{:S(2)}, u32[]{:S(2)}) collective-permute-start(bf16[8,64,256]{2,1,0:T(8,128)(2,1)S(1)} %pad_maximum_fusion.refs_0_), channel_id=1, source_target_pairs={{0,1},{1,0},{2,3},{3,2},{4,5},{5,4},{6,7},{7,6},{8,9},{9,8},{10,11... | collective-permute-start | bytes 786440 | tf_op jit(solution)/shard_map/ppermute | solution.py:251
  14.0 8.3 %collective-permute-start.5 = (bf16[8,64,256]{2,1,0:T(8,128)(2,1)S(1)}, bf16[8,64,256]{2,1,0:T(8,128)(2,1)S(1)}, u32[]{:S(2)}, u32[]{:S(2)}) collective-permute-start(bf16[8,64,256]{2,1,0:T(8,128)(2,1)S(1)} %pad_maximum_fusion.refs_0_), channel_id=1, source_target_pairs={{0,2},{1,3},{2,0},{3,1},{4,6},{5,7},{6,4},{7,5},{8,10},{9,11},{10,... | collective-permute-start | bytes 786440 | tf_op jit(solution)/shard_map/ppermute | solution.py:251
  20.4 3.4 %copy-start.3 = (s32[32,1]{0,1:T(1,128)S(1)}, s32[32,1]{0,1:T(1,128)}, u32[]{:S(2)}) copy-start(s32[32,1]{0,1:T(1,128)} %param.11) | copy-start | bytes 388
  22.3 1.5 %collective-permute-start.7 = (bf16[8,64,256]{2,1,0:T(8,128)(2,1)S(1)}, bf16[8,64,256]{2,1,0:T(8,128)(2,1)S(1)}, u32[]{:S(2)}, u32[]{:S(2)}) collective-permute-start(bf16[8,64,256]{2,1,0:T(8,128)(2,1)S(1)} %collective-permute-done.5.refs_0_), channel_id=1, source_target_pairs={{0,1},{1,0},{2,3},{3,2},{4,5},{5,4},{6,7},{7,6},{8,9},{9,8},{10,11... | collective-permute-start | bytes 786440 | tf_op jit(solution)/shard_map/ppermute | solution.py:251

commit v7 on v6

--- a/solution.py
+++ b/solution.py
@@ -41,7 +41,7 @@
 PITCH = LANES + 8
 
 
-def arrange_kernel(pat_hbm, tmpl_hbm, table_hbm, out_ref, own_ref, table_ref, pat_ref, raw_ref, sem, side_sem):
+def arrange_kernel(pat_hbm, tmpl_hbm, table_hbm, out_ref, own_ref, table_ref, tail_ref, pat_ref, raw_ref, sem, side_sem):
     chunks = pat_ref.shape[0] // ROWS
 
     def fetch(c):
@@ -51,6 +51,7 @@
     sides = [
         pltpu.make_async_copy(tmpl_hbm, own_ref, side_sem.at[0]),
         pltpu.make_async_copy(table_hbm, table_ref, side_sem.at[1]),
+        pltpu.make_async_copy(pat_hbm.at[pl.ds(pat_ref.shape[0], tail_ref.shape[0])], tail_ref, side_sem.at[2]),
     ]
     for c in range(chunks):
         fetch(c).start()
@@ -71,16 +72,25 @@
         copy.wait()
 
 
-def pattern_kernel(bin_ref, gain_ref, rows_ref, inner_ref, outer_ref, table_ref, out_ref, edge_ref, weight_ref, spec_ref):
-    count = rows_ref.shape[1]
-    spare = LANES - count
+def pattern_kernel(bin_ref, gain_ref, rows_ref, tail_ref, inner_ref, outer_ref, table_ref, out_ref, edge_ref, weight_ref, spec_ref):
+    spare = LANES - rows_ref.shape[1]
+    tail = tail_ref.shape[0]
     pitch = spare + 8
     even = lax.axis_index("scan") % 2 == 0
-    edge_ref[...] = jnp.zeros(edge_ref.shape, F32)
-    inner, outer = inner_ref[0].astype(F32), outer_ref[0].astype(F32)
-    for at, wide in ((0, jnp.where(even, inner, outer)), (spare - 1, jnp.where(even, outer, inner))):
+    zero = jnp.zeros((spare - tail, LANES), F32)
+    for r in range(RADII):
+        edge_ref[0, pl.ds(r * pitch + tail, spare - tail), :] = zero
+        edge_ref[1, pl.ds(r * pitch + tail, spare - tail), :] = zero
+
+    def put(at, wide):
         edge_ref[0, pl.ds(at, RADII, stride=pitch), :] = wide[:, :LANES]
         edge_ref[1, pl.ds(at, RADII, stride=pitch), :] = wide[:, LANES:]
+
+    for p in range(tail):
+        put(p, tail_ref[p].astype(F32))
+    inner, outer = inner_ref[0].astype(F32), outer_ref[0].astype(F32)
+    put(tail, jnp.where(even, inner, outer))
+    put(spare - 1, jnp.where(even, outer, inner))
     for r in range(RADII):
         weight_ref[pl.ds(r, 1), :] = jnp.full((1, LANES), gain_ref[bin_ref[r]], F32)
     for r in range(0, RADII, 2):
@@ -180,33 +190,35 @@
 
 def arrange(patterns, templates, table):
     count = patterns.shape[0]
+    head = count - count // (3 * ROWS) * ROWS
     args = (patterns, templates, table)
     return pl.pallas_call(
         arrange_kernel,
         out_shape=(
-            jax.ShapeDtypeStruct((RADII, count, ANGLES), BF16),
+            jax.ShapeDtypeStruct((RADII, head, ANGLES), BF16),
             jax.ShapeDtypeStruct(templates.shape, BF16),
             jax.ShapeDtypeStruct(table.shape, BF16),
+            jax.ShapeDtypeStruct((count - head,) + patterns.shape[1:], BF16),
         ),
         in_specs=[HBM] * 3,
-        out_specs=(VMEM,) * 3,
+        out_specs=(VMEM,) * 4,
         scratch_shapes=[
-            pltpu.VMEM(patterns.shape, BF16),
+            pltpu.VMEM((head,) + patterns.shape[1:], BF16),
             pltpu.VMEM((2, 2, RADII * (ROWS + 8), LANES), F32),
-            pltpu.SemaphoreType.DMA((count // ROWS,)),
-            pltpu.SemaphoreType.DMA((2,)),
+            pltpu.SemaphoreType.DMA((head // ROWS,)),
+            pltpu.SemaphoreType.DMA((3,)),
         ],
         compiler_params=pltpu.CompilerParams(vmem_limit_bytes=16 << 20),
         name="arrange",
     )(*(pltpu.with_memory_space_constraint(x, pltpu.HBM) for x in args))
 
 
-def pattern_spectra(bins, gains, rows, inner, outer, table):
+def pattern_spectra(bins, gains, rows, tail, inner, outer, table):
     spare = LANES - rows.shape[1]
     return pl.pallas_call(
         pattern_kernel,
         out_shape=jax.ShapeDtypeStruct((HALF, LANES, LANES), BF16),
-        in_specs=[SMEM] * 2 + [VMEM] * 4,
+        in_specs=[SMEM] * 2 + [VMEM] * 5,
         out_specs=VMEM,
         scratch_shapes=[
             pltpu.VMEM((2, RADII * (spare + 8), LANES), F32),
@@ -215,7 +227,7 @@
         ],
         compiler_params=pltpu.CompilerParams(vmem_limit_bytes=16 << 20),
         name="pattern_spectra",
-    )(bins, gains, rows, inner, outer, table)
+    )(bins, gains, rows, tail, inner, outer, table)
 
 
 def match(pat_spec, table, inverse, parts, held, carry, total, final=None):
@@ -258,15 +270,17 @@
     pairs = [(i, i + 1) for i in range(1, size - 1, 2)]
     inner = send(inner, 1)
     outer = lax.ppermute(outer, "scan", pairs + [(j, i) for i, j in pairs])
-    rows, own, table = arrange(patterns, templates, table)
-    came, rows, own, table, inner, outer = lax.optimization_barrier((came, rows, own, table, inner, outer))
+    rows, own, table, tail = arrange(patterns, templates, table)
+    came, rows, own, table, tail, inner, outer = lax.optimization_barrier(
+        (came, rows, own, table, tail, inner, outer)
+    )
     part = lax.optimization_barrier(jnp.concatenate([own] + came, axis=0))
     parts, held = [part], [masks]
     for mask in middle:
         if mask != middle[0]:
             parts, held = [jnp.concatenate(parts, axis=0)], [held[0] + held[1]]
         parts, held = parts + [send(parts[0], mask)], held + [[m ^ mask for m in held[0]]]
-    pat_spec = pattern_spectra(radius_bin, radial_gain, rows, inner, outer, table)
+    pat_spec = pattern_spectra(radius_bin, radial_gain, rows, tail, inner, outer, table)
     crossed = [[m ^ core for m in masks] for masks in held]
     early = [parts[0], send(parts[0], core)]
     total = orientation.shape[1]

time: 26.2 us -> 25.9 us (0.989)
  starting transfers between devices: 10.8 us -> 10.5 us
    pallas_call x1, Pallas kernels: 3.08 us -> 2.42 us  [arrange(): pl.pallas_call(arrange_kernel, out_shape=(jax.ShapeDtypeStruct((RADII, he...]
    pallas_call x1, Pallas kernels: 2.93 us -> 3.38 us  [pattern_spectra(): pl.pallas_call(pattern_kernel, out_shape=jax.ShapeDtypeStruct((HALF, LANE...]
    ppermute x7, starting transfers between devices: 10.2 us -> 9.87 us  [send(): return lax.ppermute(part, 'scan', [(i, i ^ mask) for i in range(size)])]
where the time goes in v7:
time: 25.9 us; the launch traced here: 25.7 us
  Pallas kernels  11.1 us (43%)
  starting transfers between devices  10.5 us (41%)
  waiting for transfers between devices  2.47 us (10%)
  other arithmetic  0.82 us (3%)
  between operations  0.76 us (3%)
    ppermute x7, starting transfers between devices, send(): return lax.ppermute(part, 'scan', [(i, i ^ mask) for i in range(size)])  9.87 us
    pallas_call x3, Pallas kernels, match(): pl.pallas_call(functools.partial(match_kernel, held=held, block=block, fi...  5.28 us
    pallas_call x1, Pallas kernels, pattern_spectra(): pl.pallas_call(pattern_kernel, out_shape=jax.ShapeDtypeStruct((HALF, LANE...  3.38 us
    ppermute x7, waiting for transfers between devices, send(): return lax.ppermute(part, 'scan', [(i, i ^ mask) for i in range(size)])  2.47 us
    pallas_call x1, Pallas kernels, arrange(): pl.pallas_call(arrange_kernel, out_shape=(jax.ShapeDtypeStruct((RADII, he...  2.42 us
    select_n x1, other arithmetic, on_device(): jnp.where(even, leading, last)  0.78 us
    ppermute x1, starting transfers between devices, on_device(): outer = lax.ppermute(outer, 'scan', pairs + [(j, i) for i, j in pairs])  0.66 us
  transfers between devices with their start and end apart: 8, of which 4 were waited for; matrix products, arithmetic and copies ran while one was open for 3% of the time, Pallas kernels for 35%

profile of v7, /device:TPU:0, one launch (start us, length us, event | category | flops | bytes accessed | tf_op | source)
XLA Modules:
  0.0 25.7 jit_solution(14529144628032094701)
XLA Ops:
  0.6 0.0 copy-start.2
  0.6 0.0 copy-start.1
  0.6 4.1 %collective-permute-start = (bf16[2,64,256]{2,1,0:T(8,128)(2,1)}, bf16[2,64,256]{2,1,0:T(8,128)(2,1)S(1)}, u32[]{:S(2)}, u32[]{:S(2)}) collective-permute-start(bf16[2,64,256]{2,1,0:T(8,128)(2,1)} %tmpl_hbm.1), channel_id=1, source_target_pairs={{0,8},{1,9},{2,10},{3,11},{4,12},{5,13},{6,14},{7,15},{8,0},{9,1},... | collective-permute-start | bytes 196616 | tf_op jit(solution)/shard_map/ppermute | solution.py:263
  4.8 1.3 %collective-permute-start.1 = (bf16[2,64,256]{2,1,0:T(8,128)(2,1)}, bf16[2,64,256]{2,1,0:T(8,128)(2,1)S(1)}, u32[]{:S(2)}, u32[]{:S(2)}) collective-permute-start(bf16[2,64,256]{2,1,0:T(8,128)(2,1)} %tmpl_hbm.1), channel_id=1, source_target_pairs={{0,12},{1,13},{2,14},{3,15},{4,8},{5,9},{6,10},{7,11},{8,4},{9,5},... | collective-permute-start | bytes 196616 | tf_op jit(solution)/shard_map/ppermute | solution.py:263
  6.1 0.2 collective-permute-start.2
  6.3 0.8 %broadcast_select_fusion = (bf16[1,64,256]{2,1,0:T(8,128)(2,1)S(1)}, bf16[1,64,256]{2,1,0:T(8,128)(2,1)S(1)}) fusion(pred[]{:T(512)S(6)} %eq.5, bf16[96,64,256]{2,1,0:T(8,128)(2,1)} %pat_hbm.1), kind=kLoop, calls=%fused_computation.1 | loop fusion | flops 32768 | bytes 131073 | tf_op jit(solution)/shard_map/jit(_where)/select_n | solution.py:269
  7.1 0.1 collective-permute-start.3
  7.2 0.7 %collective-permute-start.4 = (bf16[1,64,256]{2,1,0:T(8,128)(2,1)S(1)}, bf16[1,64,256]{2,1,0:T(8,128)(2,1)S(1)}, u32[]{:S(2)}, u32[]{:S(2)}) collective-permute-start(bf16[1,64,256]{2,1,0:T(8,128)(2,1)S(1)} %get-tuple-element.42), channel_id=1, source_target_pairs={{1,2},{3,4},{5,6},{7,8},{9,10},{11,12},{13,14},{2,1},{4,3},{6,5},{... | collective-permute-start | bytes 98312 | tf_op jit(solution)/shard_map/ppermute | solution.py:272
  7.9 2.4 %arrange.1 = (bf16[64,64,256]{2,1,0:T(8,128)(2,1)S(1)}, bf16[2,64,256]{2,1,0:T(8,128)(2,1)S(1)}, bf16[256,256]{1,0:T(8,128)(2,1)S(1)}, bf16[32,64,256]{2,1,0:T(8,128)(2,1)S(1)}) custom-call(bf16[96,64,256]{2,1,0:T(8,128)(2,1)} %pat_hbm.1, bf16[2,64,256]{2,1,0:T(8,128)(2,1)} %tmpl_hbm.1, bf16[256,256]{1,0:T(8,128)(2,1)} %constant.22.clone.table_hbm), custom_call_target="tpu_custom_call" | custom-call | tf_op jit(solution)/shard_map/arrange/pallas_call | solution.py:195
  10.3 0.0 collective-permute-done.3.inner_ref
  10.3 0.0 collective-permute-done.4.outer_ref
  10.3 0.0 collective-permute-done
  10.3 0.9 %collective-permute-done.1 = bf16[2,64,256]{2,1,0:T(8,128)(2,1)S(1)} collective-permute-done((bf16[2,64,256]{2,1,0:T(8,128)(2,1)}, bf16[2,64,256]{2,1,0:T(8,128)(2,1)S(1)}, u32[]{:S(2)}, u32[]{:S(2)}) %collective-permute-start.1) | collective-permute-done | bytes 65568 | tf_op jit(solution)/shard_map/ppermute | solution.py:263
  11.2 0.1 collective-permute-done.2
  11.3 0.0 copy-start
  11.3 2.0 %collective-permute-start.6 = (bf16[8,64,256]{2,1,0:T(8,128)(2,1)S(1)}, bf16[8,64,256]{2,1,0:T(8,128)(2,1)S(1)}, u32[]{:S(2)}, u32[]{:S(2)}) collective-permute-start(bf16[8,64,256]{2,1,0:T(8,128)(2,1)S(1)} %pad_maximum_fusion.refs_0_), channel_id=1, source_target_pairs={{0,1},{1,0},{2,3},{3,2},{4,5},{5,4},{6,7},{7,6},{8,9},{9,8},{10,11... | collective-permute-start | bytes 786440 | tf_op jit(solution)/shard_map/ppermute | solution.py:263
  13.3 2.1 %collective-permute-start.5 = (bf16[8,64,256]{2,1,0:T(8,128)(2,1)S(1)}, bf16[8,64,256]{2,1,0:T(8,128)(2,1)S(1)}, u32[]{:S(2)}, u32[]{:S(2)}) collective-permute-start(bf16[8,64,256]{2,1,0:T(8,128)(2,1)S(1)} %pad_maximum_fusion.refs_0_), channel_id=1, source_target_pairs={{0,2},{1,3},{2,0},{3,1},{4,6},{5,7},{6,4},{7,5},{8,10},{9,11},{10,... | collective-permute-start | bytes 786440 | tf_op jit(solution)/shard_map/ppermute | solution.py:263
  15.5 0.0 copy-done.2
  15.5 0.0 copy-done.1
  15.5 3.4 %pattern_spectra.1.pat_ref = bf16[128,128,128]{2,1,0:T(8,128)(2,1)S(1)} custom-call(s32[64]{0:T(128)S(1)} %copy-done.1, f32[8]{0:T(128)S(1)} %copy-done.2, bf16[64,64,256]{2,1,0:T(8,128)(2,1)S(1)} %get-tuple-element.30.rows_ref, bf16[32,64,256]{2,1,0:T(8,128)(2,1)S(1)} %get-tuple-element.31.tail_ref, ...), custom_call_target="tpu_custom_call" | custom-call | tf_op jit(solution)/shard_map/pattern_spectra/pallas_call | solution.py:218
  18.9 0.0 collective-permute-done.6.refs_1_
  18.9 0.0 copy-done
  18.9 1.7 %match.3.refs_1_ = f32[32,128]{1,0:T(8,128)S(1)} custom-call(bf16[128,128,128]{2,1,0:T(8,128)(2,1)S(1)} %pattern_spectra.1.pat_ref, bf16[256,256]{1,0:T(8,128)(2,1)S(1)} %get-tuple-element.34.table_ref, bf16[256,256]{1,0:T(8,128)(2,1)S(1)} %copy-done, bf16[8,64,256]{2,1,0:T(8,128)(2,1)S(1)} %pad_maximum_fusion.refs_0_, ...), custom_call_target="tpu_custom_call" | custom-call | tf_op jit(solution)/shard_map/match/pallas_call | solution.py:241
  20.6 0.0 copy-start.3
  20.6 1.4 %collective-permute-done.5.refs_0_ = bf16[8,64,256]{2,1,0:T(8,128)(2,1)S(1)} collective-permute-done((bf16[8,64,256]{2,1,0:T(8,128)(2,1)S(1)}, bf16[8,64,256]{2,1,0:T(8,128)(2,1)S(1)}, u32[]{:S(2)}, u32[]{:S(2)}) %collective-permute-start.5) | collective-permute-done | bytes 262176 | tf_op jit(solution)/shard_map/ppermute | solution.py:263
  22.0 0.0 collective-permute-start.7
  22.0 1.4 %match.4.refs_2_ = f32[32,128]{1,0:T(8,128)S(1)} custom-call(bf16[128,128,128]{2,1,0:T(8,128)(2,1)S(1)} %pattern_spectra.1.pat_ref, bf16[256,256]{1,0:T(8,128)(2,1)S(1)} %get-tuple-element.34.table_ref, bf16[256,256]{1,0:T(8,128)(2,1)S(1)} %copy-done, bf16[8,64,256]{2,1,0:T(8,128)(2,1)S(1)} %collective-permute-done.5.refs_0_, f32[32,128]{1,0:T(8,128)S(1)} %match.3.refs_1_), custom_call_target="tpu_custom_call" | custom-call | tf_op jit(solution)/shard_map/match/pallas_call | solution.py:241
  23.4 0.1 collective-permute-done.7.refs_0_
  23.5 0.0 copy-done.3
  23.5 2.1 %match.5 = (f32[32,96]{1,0:T(8,128)}, f32[16,96]{1,0:T(8,128)}) custom-call(bf16[128,128,128]{2,1,0:T(8,128)(2,1)S(1)} %pattern_spectra.1.pat_ref, bf16[256,256]{1,0:T(8,128)(2,1)S(1)} %get-tuple-element.34.table_ref, bf16[256,256]{1,0:T(8,128)(2,1)S(1)} %copy-done, bf16[8,64,256]{2,1,0:T(8,128)(2,1)S(1)} %collective-permute-done.7.refs_0_, ...), custom_call_target="tpu_custom_call" | custom-call | tf_op jit(solution)/shard_map/match/pallas_call | solution.py:241
  (1 shorter events, 0.0 us)
Async XLA Ops:
  0.6 14.8 %copy-start.2 = (f32[8]{0:T(128)S(1)}, f32[8]{0:T(128)}, u32[]{:S(2)}) copy-start(f32[8]{0:T(128)} %gain_ref.1) | copy-start | bytes 100
  0.6 14.8 %copy-start.1 = (s32[64]{0:T(128)S(1)}, s32[64]{0:T(128)}, u32[]{:S(2)}) copy-start(s32[64]{0:T(128)} %bin_ref.1) | copy-start | bytes 772
  0.6 9.7 %collective-permute-start = (bf16[2,64,256]{2,1,0:T(8,128)(2,1)}, bf16[2,64,256]{2,1,0:T(8,128)(2,1)S(1)}, u32[]{:S(2)}, u32[]{:S(2)}) collective-permute-start(bf16[2,64,256]{2,1,0:T(8,128)(2,1)} %tmpl_hbm.1), channel_id=1, source_target_pairs={{0,8},{1,9},{2,10},{3,11},{4,12},{5,13},{6,14},{7,15},{8,0},{9,1},... | collective-permute-start | bytes 196616 | tf_op jit(solution)/shard_map/ppermute | solution.py:263
  4.8 6.4 %collective-permute-start.1 = (bf16[2,64,256]{2,1,0:T(8,128)(2,1)}, bf16[2,64,256]{2,1,0:T(8,128)(2,1)S(1)}, u32[]{:S(2)}, u32[]{:S(2)}) collective-permute-start(bf16[2,64,256]{2,1,0:T(8,128)(2,1)} %tmpl_hbm.1), channel_id=1, source_target_pairs={{0,12},{1,13},{2,14},{3,15},{4,8},{5,9},{6,10},{7,11},{8,4},{9,5},... | collective-permute-start | bytes 196616 | tf_op jit(solution)/shard_map/ppermute | solution.py:263
  6.1 5.2 %collective-permute-start.2 = (bf16[2,64,256]{2,1,0:T(8,128)(2,1)}, bf16[2,64,256]{2,1,0:T(8,128)(2,1)S(1)}, u32[]{:S(2)}, u32[]{:S(2)}) collective-permute-start(bf16[2,64,256]{2,1,0:T(8,128)(2,1)} %tmpl_hbm.1), channel_id=1, source_target_pairs={{0,4},{1,5},{2,6},{3,7},{4,0},{5,1},{6,2},{7,3},{8,12},{9,13},{10,... | collective-permute-start | bytes 196616 | tf_op jit(solution)/shard_map/ppermute | solution.py:263
  7.1 3.2 %collective-permute-start.3 = (bf16[1,64,256]{2,1,0:T(8,128)(2,1)S(1)}, bf16[1,64,256]{2,1,0:T(8,128)(2,1)S(1)}, u32[]{:S(2)}, u32[]{:S(2)}) collective-permute-start(bf16[1,64,256]{2,1,0:T(8,128)(2,1)S(1)} %get-tuple-element.43), channel_id=1, source_target_pairs={{0,1},{1,0},{2,3},{3,2},{4,5},{5,4},{6,7},{7,6},{8,9},{9,8},{10,11... | collective-permute-start | bytes 98312 | tf_op jit(solution)/shard_map/ppermute | solution.py:263
  7.2 3.1 %collective-permute-start.4 = (bf16[1,64,256]{2,1,0:T(8,128)(2,1)S(1)}, bf16[1,64,256]{2,1,0:T(8,128)(2,1)S(1)}, u32[]{:S(2)}, u32[]{:S(2)}) collective-permute-start(bf16[1,64,256]{2,1,0:T(8,128)(2,1)S(1)} %get-tuple-element.42), channel_id=1, source_target_pairs={{1,2},{3,4},{5,6},{7,8},{9,10},{11,12},{13,14},{2,1},{4,3},{6,5},{... | collective-permute-start | bytes 98312 | tf_op jit(solution)/shard_map/ppermute | solution.py:272
  11.3 7.5 %copy-start = (bf16[256,256]{1,0:T(8,128)(2,1)S(1)}, bf16[256,256]{1,0:T(8,128)(2,1)}, u32[]{:S(2)}) copy-start(bf16[256,256]{1,0:T(8,128)(2,1)} %constant.23.clone.inv_ref) | copy-start | bytes 393220
  11.3 7.5 %collective-permute-start.6 = (bf16[8,64,256]{2,1,0:T(8,128)(2,1)S(1)}, bf16[8,64,256]{2,1,0:T(8,128)(2,1)S(1)}, u32[]{:S(2)}, u32[]{:S(2)}) collective-permute-start(bf16[8,64,256]{2,1,0:T(8,128)(2,1)S(1)} %pad_maximum_fusion.refs_0_), channel_id=1, source_target_pairs={{0,1},{1,0},{2,3},{3,2},{4,5},{5,4},{6,7},{7,6},{8,9},{9,8},{10,11... | collective-permute-start | bytes 786440 | tf_op jit(solution)/shard_map/ppermute | solution.py:263
  13.3 8.7 %collective-permute-start.5 = (bf16[8,64,256]{2,1,0:T(8,128)(2,1)S(1)}, bf16[8,64,256]{2,1,0:T(8,128)(2,1)S(1)}, u32[]{:S(2)}, u32[]{:S(2)}) collective-permute-start(bf16[8,64,256]{2,1,0:T(8,128)(2,1)S(1)} %pad_maximum_fusion.refs_0_), channel_id=1, source_target_pairs={{0,2},{1,3},{2,0},{3,1},{4,6},{5,7},{6,4},{7,5},{8,10},{9,11},{10,... | collective-permute-start | bytes 786440 | tf_op jit(solution)/shard_map/ppermute | solution.py:263
  20.6 3.0 %copy-start.3 = (s32[32,1]{0,1:T(1,128)S(1)}, s32[32,1]{0,1:T(1,128)}, u32[]{:S(2)}) copy-start(s32[32,1]{0,1:T(1,128)} %param.11) | copy-start | bytes 388
  22.0 1.5 %collective-permute-start.7 = (bf16[8,64,256]{2,1,0:T(8,128)(2,1)S(1)}, bf16[8,64,256]{2,1,0:T(8,128)(2,1)S(1)}, u32[]{:S(2)}, u32[]{:S(2)}) collective-permute-start(bf16[8,64,256]{2,1,0:T(8,128)(2,1)S(1)} %collective-permute-done.5.refs_0_), channel_id=1, source_target_pairs={{0,1},{1,0},{2,3},{3,2},{4,5},{5,4},{6,7},{7,6},{8,9},{9,8},{10,11... | collective-permute-start | bytes 786440 | tf_op jit(solution)/shard_map/ppermute | solution.py:263
